TPU v7x, 768 devices: a whole 4x8x12 slice. The times are simulated.
768 devices in a mesh: dp: 128 (over x, z_hi, y, core), tensor: 6 (over z_lo).
Axes of the slice: x: 4, y: 8, z: 12 (z_hi: 2, z_lo: 6; z = z_hi * 6 + z_lo), core: 2. Of those that a mesh axis runs over, the one named last changes fastest.
Arguments:
- resid: bfloat16 [512, 32, 8192], P('dp'), may hold values from -24 to 24
- norm_gain: float32 [8192], replicated, may hold values from 0.1 to 1.9
- w_value: bfloat16 [8192, 768], P('dp', 'tensor'), may hold values from -0.0625 to 0.0625
- d_value: bfloat16 [512, 32, 768], P('dp', None, 'tensor'), may hold values from -6 to 6
- rewards: bfloat16 [512], P('dp'), may hold values from 0 to 1
- lengths: int32 [128, 4], P('dp'), may hold values from 1 to 32, 96 in all within a row
Outputs:
- value: bfloat16 [512, 32, 768], P('dp', None, 'tensor')
- w_grad: bfloat16 [8192, 768], P('dp', 'tensor')
Inputs may be any that keep to these rules, and one draw needn't show every extreme that they name: The 4 responses of each index of dp have lengths that sum to exactly 96.
All inputs are finite; a program needn't handle non-finite values.
Results may differ from a plain program's by a relative error of at most 0.0058.
Values may be sent and summed in bfloat16 or wider, within the bound.
No kernel may reach another device: no remote copies, remote signals or barrier semaphores. Data moves between devices by JAX's collectives and lax.ppermute only.
A program may use at most 32 MiB of HBM per device.

v0:
```python
import jax
import jax.numpy as jnp
from jax import lax
from jax.experimental import pallas as pl
from jax.experimental.pallas import tpu as pltpu
from jax.sharding import Mesh
from jax.sharding import PartitionSpec as P

DP = ("x", "zh", "y", "c")
SWAP = ((0, 1), (1, 0))
Y_PAIR = tuple((j, j ^ 1) for j in range(8))
LANES = 128
BLOCK = 64
bf16, f32 = jnp.bfloat16, jnp.float32


def norm_kernel(core_ref, x_ref, gain_ref, dval_ref, rew_ref, near_ref, len_ref, own_ref, pack_ref):
    rows, width = x_ref.shape
    total = jnp.zeros((rows, LANES), f32)
    for k in range(width // LANES):
        v = x_ref[:, k * LANES : (k + 1) * LANES].astype(f32)
        total = total + v * v
    scale = lax.rsqrt(jnp.sum(total, axis=1, keepdims=True) * (1.0 / width) + 1e-5)
    first = core_ref[0] == 0
    low = lax.broadcasted_iota(jnp.int32, (rows, LANES), 1) < BLOCK
    for k in range(width // LANES // 2):
        at = 2 * k * LANES
        a = x_ref[:, at : at + LANES].astype(f32) * scale * gain_ref[:, at : at + LANES]
        b = x_ref[:, at + LANES : at + 2 * LANES].astype(f32) * scale * gain_ref[:, at + LANES : at + 2 * LANES]
        even = jnp.where(low, a, pltpu.roll(b, BLOCK, 1))
        odd = jnp.where(low, pltpu.roll(a, BLOCK, 1), b)
        own_ref[:, k * LANES : (k + 1) * LANES] = jnp.where(first, even, odd).astype(bf16)
        pack_ref[:, k * LANES : (k + 1) * LANES] = jnp.where(first, odd, even).astype(bf16)
    half = width // 2
    pack_ref[:, half : half + LANES] = dval_ref[...]
    lane = lax.broadcasted_iota(jnp.int32, (rows, LANES), 1)
    tail = jnp.zeros((rows, LANES), f32)
    n = rew_ref.shape[1]
    for s, ref in enumerate((rew_ref, near_ref, len_ref)):
        vals = ref[...].astype(f32)
        for j in range(n):
            tail = jnp.where(lane == s * n + j, vals[:, j : j + 1], tail)
    pack_ref[:, half + LANES :] = tail.astype(bf16)


def grad_kernel(own_ref, got_ref, gotd_ref, tail_ref, dval_ref, rew_ref, near_ref, len_ref, out_ref, ds_own, ds_other):
    rows, _ = dval_ref.shape
    n = rew_ref.shape[1]
    slots = rows // n

    @pl.when(pl.program_id(0) == 0)
    def _():
        rew = rew_ref[...].astype(f32)
        near = near_ref[...].astype(f32)
        tail = tail_ref[...].astype(f32)[0:1, :]
        in_group = lax.broadcasted_iota(jnp.int32, (1, LANES), 1) < 2 * n
        count = 1.0 / (4 * n)
        total = jnp.sum(rew, axis=1, keepdims=True) + jnp.sum(near, axis=1, keepdims=True)
        total = total + jnp.sum(jnp.where(in_group, tail, 0.0), axis=1, keepdims=True)
        mean = total * count
        sq = jnp.sum((rew - mean) ** 2, axis=1, keepdims=True) + jnp.sum((near - mean) ** 2, axis=1, keepdims=True)
        sq = sq + jnp.sum(jnp.where(in_group, (tail - mean) ** 2, 0.0), axis=1, keepdims=True)
        spread = jnp.maximum(jnp.sqrt(sq * count), 0.25)
        row = lax.broadcasted_iota(jnp.int32, (rows, 1), 0)
        place = (row % slots).astype(f32)

        def factor(rewards_at, length_at):
            r = jnp.zeros((rows, 1), f32)
            length = jnp.ones((rows, 1), f32)
            for j in range(n):
                mine = row // slots == j
                r = jnp.where(mine, rewards_at(j), r)
                length = jnp.where(mine, length_at(j), length)
            coef = -((r - mean) / spread) / length
            return jnp.where(place < length, coef, 0.0)

        lens = len_ref[...].astype(f32)
        own = factor(lambda j: rew[:, j : j + 1], lambda j: lens[:, j : j + 1])
        other = factor(lambda j: tail[:, j : j + 1], lambda j: tail[:, 2 * n + j : 2 * n + j + 1])
        ds_own[...] = (dval_ref[...].astype(f32) * own).astype(bf16)
        ds_other[...] = (gotd_ref[...].astype(f32) * other).astype(bf16)

    over_rows = (((0,), (0,)), ((), ()))
    acc = lax.dot_general(ds_own[...], own_ref[...], over_rows, preferred_element_type=f32)
    acc = acc + lax.dot_general(ds_other[...], got_ref[...], over_rows, preferred_element_type=f32)
    out_ref[0] = acc.astype(bf16)


def turn_kernel(got_ref, out_ref):
    total = got_ref[0].astype(f32)
    for s in range(1, got_ref.shape[0]):
        total = total + got_ref[s].astype(f32)
    for k in range(total.shape[1] // LANES):
        piece = total[:, k * LANES : (k + 1) * LANES].T.astype(bf16)
        out_ref[2 * k] = piece[:BLOCK]
        out_ref[2 * k + 1] = piece[BLOCK:]


def per_device(resid, norm_gain, w_value, d_value, rewards, lengths):
    rolls, slots, width = resid.shape
    rows = rolls * slots
    cols = w_value.shape[1]
    nx, nz, ny, nc = [lax.axis_size(a) for a in DP]
    nzy = nz * ny
    half = width // nc
    chunk = half // nx
    whole = lambda *shape: pl.BlockSpec(shape, lambda *_: (0,) * len(shape))

    near = lax.ppermute(rewards, "y", Y_PAIR)
    w_zy = lax.all_to_all(jnp.broadcast_to(w_value[None], (nzy, BLOCK, cols)), ("zh", "y"), 0, 0, tiled=True)
    w_all = lax.all_to_all(jnp.broadcast_to(w_zy[None], (nx, nzy, BLOCK, cols)), "x", 0, 0, tiled=True)
    w_full = w_all.reshape(half, cols)

    core = lax.axis_index("c").astype(jnp.int32).reshape(1)
    dval = d_value.reshape(rows, cols)
    rew, near = rewards.reshape(1, rolls), near.reshape(1, rolls)
    step = 32
    own, packed = pl.pallas_call(
        norm_kernel,
        grid=(rows // step,),
        in_specs=[
            pl.BlockSpec(memory_space=pltpu.SMEM),
            pl.BlockSpec((step, width), lambda i: (i, 0)),
            whole(1, width),
            pl.BlockSpec((step, cols), lambda i: (i, 0)),
            whole(1, rolls),
            whole(1, rolls),
            whole(1, rolls),
        ],
        out_specs=[
            pl.BlockSpec((step, half), lambda i: (i, 0)),
            pl.BlockSpec((step, half + 2 * LANES), lambda i: (i, 0)),
        ],
        out_shape=[
            jax.ShapeDtypeStruct((rows, half), bf16),
            jax.ShapeDtypeStruct((rows, half + 2 * LANES), bf16),
        ],
        name="norm_split",
    )(core, resid.reshape(rows, width), norm_gain.reshape(1, width), dval, rew, near, lengths)
    got = lax.ppermute(packed, "c", SWAP)
    send = pl.pallas_call(
        grad_kernel,
        grid=(nx,),
        in_specs=[
            pl.BlockSpec((rows, chunk), lambda k: (0, k)),
            pl.BlockSpec((rows, chunk), lambda k: (0, k)),
            pl.BlockSpec((rows, cols), lambda k: (0, half // LANES)),
            pl.BlockSpec((16, LANES), lambda k: (0, half // LANES + 1)),
            whole(rows, cols),
            whole(1, rolls),
            whole(1, rolls),
            whole(1, rolls),
        ],
        out_specs=pl.BlockSpec((1, cols, chunk), lambda k: (k, 0, 0)),
        out_shape=jax.ShapeDtypeStruct((nx, cols, chunk), bf16),
        scratch_shapes=[pltpu.VMEM((rows, cols), bf16), pltpu.VMEM((rows, cols), bf16)],
        name="grad_partial",
    )(own, got, got, got, dval, rew, near, lengths)
    g_x = lax.all_to_all(send, "x", 0, 0, tiled=True)
    split = 2
    g_send = pl.pallas_call(
        turn_kernel,
        grid=(split,),
        in_specs=[pl.BlockSpec((nx, cols, chunk // split), lambda k: (0, 0, k))],
        out_specs=pl.BlockSpec((nzy // split, BLOCK, cols), lambda k: (k, 0, 0)),
        out_shape=jax.ShapeDtypeStruct((nzy, BLOCK, cols), bf16),
        name="sum_turn",
    )(g_x)
    g_zy = lax.all_to_all(g_send, ("zh", "y"), 0, 0, tiled=True)
    w_grad = jnp.sum(g_zy.astype(f32), axis=0).astype(bf16)

    v_other = jnp.dot(got[:, :half], w_full, preferred_element_type=f32)
    v_got = lax.ppermute(v_other, "c", SWAP)
    v_own = jnp.dot(own, w_full, preferred_element_type=f32)
    live = jnp.arange(slots, dtype=jnp.int32)[None, :] < lengths.reshape(rolls, 1)
    value = (v_own + v_got).reshape(rolls, slots, cols) * live.astype(f32)[:, :, None]
    return value.astype(bf16), w_grad


def solution(mesh):
    finer = Mesh(mesh.devices.reshape(4, 2, 8, 2, mesh.shape["tensor"]), DP + ("tensor",))
    placed = (P(DP, None, None), P(), P(DP, "tensor"), P(DP, None, "tensor"), P(DP), P(DP, None))
    return jax.shard_map(
        per_device,
        mesh=finer,
        in_specs=placed,
        out_specs=(P(DP, None, "tensor"), P(DP, "tensor")),
        check_vma=False,
    )
```

profile of v0, /device:TPU:64, one launch (start us, length us, event | category | flops | bytes accessed | tf_op | source)
XLA Modules:
  0.0 112.5 jit_solution(18407798668968545514)
XLA Ops:
  0.6 0.0 copy-start.3
  0.6 3.5 %collective-permute-start = (bf16[4]{0:T(256)(128)(2,1)}, bf16[4]{0:T(256)(128)(2,1)S(1)}, u32[]{:S(2)}, u32[]{:S(2)}) collective-permute-start(bf16[4]{0:T(256)(128)(2,1)} %param.10), channel_id=1, source_target_pairs={{0,12},{12,0},{24,36},{36,24},{48,60},{60,48},{72,84},{84,72},{1,1... | collective-permute-start | bytes 32 | tf_op jit(solution)/shard_map/ppermute | solution.py:109
  4.1 2.1 %collective-permute-done = bf16[4]{0:T(256)(128)(2,1)S(1)} collective-permute-done((bf16[4]{0:T(256)(128)(2,1)}, bf16[4]{0:T(256)(128)(2,1)S(1)}, u32[]{:S(2)}, u32[]{:S(2)}) %collective-permute-start) | collective-permute-done | bytes 40 | tf_op jit(solution)/shard_map/ppermute | solution.py:109
  6.2 0.0 copy-start.5
  6.2 0.5 copy-done.5
  6.8 4.7 %norm_split.1 = (bf16[128,4096]{1,0:T(8,128)(2,1)}, bf16[128,4352]{1,0:T(8,128)(2,1)}) custom-call(s32[1]{0:T(128)} %bitcast.core_ref, bf16[128,8192]{1,0:T(8,128)(2,1)} %bitcast.14, f32[1,8192]{1,0:T(1,128)} %bitcast.18, bf16[128,128]{1,0:T(8,128)(2,1)} %bitcast.16, bf16[1,4]{1,0:T(2,128)(2,1)} %bitcast.20, bf16[1,4]{1,0:T(2,128)(2,1)} %bitcast.22, ...), custom_call_target="tpu_custom_call" | custom-call | tf_op jit(solution)/shard_map/norm_split/pallas_call | solution.py:118
  11.4 1.9 %collective-permute-start.1 = (bf16[128,4352]{1,0:T(8,128)(2,1)}, bf16[128,4352]{1,0:T(8,128)(2,1)S(1)}, u32[]{:S(2)}, u32[]{:S(2)}) collective-permute-start(bf16[128,4352]{1,0:T(8,128)(2,1)} %get-tuple-element.5), channel_id=1, source_target_pairs={{0,6},{6,0},{1,7},{7,1},{2,8},{8,2},{3,9},{9,3},{4,10},{10,4},{5,1... | collective-permute-start | bytes 3342344 | tf_op jit(solution)/shard_map/ppermute | solution.py:140
  13.3 0.0 copy-done.3
  13.3 0.8 broadcast_in_dim.4
  14.1 19.0 %all-to-all-start = ((bf16[16,64,128]{2,1,0:T(8,128)(2,1)}), bf16[16,64,128]{2,1,0:T(8,128)(2,1)S(1)}, u32[]{:S(2)}, u32[]{:S(2)}) async-start(bf16[16,64,128]{2,1,0:T(8,128)(2,1)} %broadcast_in_dim.4), calls=%async_computation | async-start | bytes 524288 | tf_op jit(solution)/shard_map/all_to_all | solution.py:110
  33.1 0.0 collective-permute-done.1.got_ref.gotd_ref.tail_ref
  33.1 0.0 copy-start
  33.1 1.0 copy-done
  34.1 4.7 %grad_partial.1 = bf16[4,128,1024]{2,1,0:T(8,128)(2,1)} custom-call(bf16[128,4096]{1,0:T(8,128)(2,1)} %get-tuple-element.4.own_ref, bf16[128,4352]{1,0:T(8,128)(2,1)} %copy-done, bf16[128,4352]{1,0:T(8,128)(2,1)} %copy-done, bf16[128,4352]{1,0:T(8,128)(2,1)} %copy-done, bf16[128,128]{1,0:T(8,128)(2,1)} %bitcast.17, bf16[1,4]{1,0:T(2,128)(2,1)} %bitcast.21, ...), custom_call_target="tpu_custom_call" | custom-call | tf_op jit(solution)/shard_map/grad_partial/pallas_call | solution.py:141
  38.8 15.4 %all-to-all-done = bf16[16,64,128]{2,1,0:T(8,128)(2,1)S(1)} async-done(((bf16[16,64,128]{2,1,0:T(8,128)(2,1)}), bf16[16,64,128]{2,1,0:T(8,128)(2,1)S(1)}, u32[]{:S(2)}, u32[]{:S(2)}) %all-to-all-start) | async-done | bytes 262176 | tf_op jit(solution)/shard_map/all_to_all | solution.py:110
  54.1 18.7 %all_to_all.20.got_ref = bf16[4,128,1024]{2,1,0:T(8,128)(2,1)} all-to-all(bf16[4,128,1024]{2,1,0:T(8,128)(2,1)} %grad_partial.1), channel_id=1, replica_groups=mesh['x'=4,'zh'=2,'y'=8,'c'=2,'tensor'=6] {'x'}, dimensions={0} | all-to-all | bytes 2097152 | tf_op jit(solution)/shard_map/all_to_all | solution.py:159
  72.8 1.3 %broadcast_in_dim.5 = bf16[4,16,64,128]{3,2,1,0:T(8,128)(2,1)} broadcast(bf16[16,64,128]{2,1,0:T(8,128)(2,1)S(1)} %all-to-all-done), dimensions={1,2,3} | broadcast | bytes 1310720 | tf_op jit(solution)/shard_map/broadcast_in_dim | solution.py:111
  74.1 3.5 %all-to-all-start.1 = ((bf16[4,16,64,128]{3,2,1,0:T(8,128)(2,1)}), bf16[4,16,64,128]{3,2,1,0:T(8,128)(2,1)S(1)}, u32[]{:S(2)}, u32[]{:S(2)}) async-start(bf16[4,16,64,128]{3,2,1,0:T(8,128)(2,1)} %broadcast_in_dim.5), calls=%async_computation.1 | async-start | bytes 2097152 | tf_op jit(solution)/shard_map/all_to_all | solution.py:111
  77.6 0.0 copy-start.1
  77.6 2.1 %sum_turn.1 = bf16[16,64,128]{2,1,0:T(8,128)(2,1)} custom-call(bf16[4,128,1024]{2,1,0:T(8,128)(2,1)} %all_to_all.20.got_ref), custom_call_target="tpu_custom_call" | custom-call | tf_op jit(solution)/shard_map/sum_turn/pallas_call | solution.py:161
  79.7 11.3 %all-to-all-done.1 = bf16[4,16,64,128]{3,2,1,0:T(8,128)(2,1)S(1)} async-done(((bf16[4,16,64,128]{3,2,1,0:T(8,128)(2,1)}), bf16[4,16,64,128]{3,2,1,0:T(8,128)(2,1)S(1)}, u32[]{:S(2)}, u32[]{:S(2)}) %all-to-all-start.1) | async-done | bytes 1048608 | tf_op jit(solution)/shard_map/all_to_all | solution.py:111
  91.0 4.0 %all-to-all-start.3 = ((bf16[16,64,128]{2,1,0:T(8,128)(2,1)}), bf16[16,64,128]{2,1,0:T(8,128)(2,1)S(1)}, u32[]{:S(2)}, u32[]{:S(2)}) async-start(bf16[16,64,128]{2,1,0:T(8,128)(2,1)} %sum_turn.1), calls=%async_computation.3 | async-start | bytes 524288 | tf_op jit(solution)/shard_map/all_to_all | solution.py:169
  95.0 0.0 copy-start.4
  95.0 0.0 copy-start.2
  95.0 0.0 copy-done.1
  95.0 0.4 fusion
  95.4 1.9 %collective-permute-start.2 = (f32[128,128]{1,0:T(8,128)S(1)}, f32[128,128]{1,0:T(8,128)S(1)}, u32[]{:S(2)}, u32[]{:S(2)}) collective-permute-start(f32[128,128]{1,0:T(8,128)S(1)} %fusion), channel_id=1, source_target_pairs={{0,6},{6,0},{1,7},{7,1},{2,8},{8,2},{3,9},{9,3},{4,10},{10,4},{5,1... | collective-permute-start | bytes 196616 | tf_op jit(solution)/shard_map/ppermute | solution.py:173
  97.3 0.0 copy-done.4
  97.4 0.1 fusion.2
  97.4 1.1 %collective-permute-done.2 = f32[128,128]{1,0:T(8,128)S(1)} collective-permute-done((f32[128,128]{1,0:T(8,128)S(1)}, f32[128,128]{1,0:T(8,128)S(1)}, u32[]{:S(2)}, u32[]{:S(2)}) %collective-permute-start.2) | collective-permute-done | bytes 65568 | tf_op jit(solution)/shard_map/ppermute | solution.py:173
  98.6 0.0 copy-done.2
  98.6 0.4 convolution_add_fusion
  99.0 0.7 multiply_convert_fusion
  99.7 12.1 %all-to-all-done.3 = bf16[16,64,128]{2,1,0:T(8,128)(2,1)S(1)} async-done(((bf16[16,64,128]{2,1,0:T(8,128)(2,1)}), bf16[16,64,128]{2,1,0:T(8,128)(2,1)S(1)}, u32[]{:S(2)}, u32[]{:S(2)}) %all-to-all-start.3) | async-done | bytes 262176 | tf_op jit(solution)/shard_map/all_to_all | solution.py:169
  111.8 0.6 reduce_sum.12
Async XLA Ops:
  0.6 12.7 %copy-start.3 = (bf16[64,128]{1,0:T(8,128)(2,1)S(1)}, bf16[64,128]{1,0:T(8,128)(2,1)}, u32[]{:S(2)}) copy-start(bf16[64,128]{1,0:T(8,128)(2,1)} %param.8) | copy-start | bytes 49156
  0.6 5.6 %collective-permute-start = (bf16[4]{0:T(256)(128)(2,1)}, bf16[4]{0:T(256)(128)(2,1)S(1)}, u32[]{:S(2)}, u32[]{:S(2)}) collective-permute-start(bf16[4]{0:T(256)(128)(2,1)} %param.10), channel_id=1, source_target_pairs={{0,12},{12,0},{24,36},{36,24},{48,60},{60,48},{72,84},{84,72},{1,1... | collective-permute-start | bytes 32 | tf_op jit(solution)/shard_map/ppermute | solution.py:109
  6.2 0.5 copy-start.5
  11.4 21.7 %collective-permute-start.1 = (bf16[128,4352]{1,0:T(8,128)(2,1)}, bf16[128,4352]{1,0:T(8,128)(2,1)S(1)}, u32[]{:S(2)}, u32[]{:S(2)}) collective-permute-start(bf16[128,4352]{1,0:T(8,128)(2,1)} %get-tuple-element.5), channel_id=1, source_target_pairs={{0,6},{6,0},{1,7},{7,1},{2,8},{8,2},{3,9},{9,3},{4,10},{10,4},{5,1... | collective-permute-start | bytes 3342344 | tf_op jit(solution)/shard_map/ppermute | solution.py:140
  14.1 40.0 %all-to-all-start = ((bf16[16,64,128]{2,1,0:T(8,128)(2,1)}), bf16[16,64,128]{2,1,0:T(8,128)(2,1)S(1)}, u32[]{:S(2)}, u32[]{:S(2)}) async-start(bf16[16,64,128]{2,1,0:T(8,128)(2,1)} %broadcast_in_dim.4), calls=%async_computation | async-start | bytes 524288 | tf_op jit(solution)/shard_map/all_to_all | solution.py:110
  33.1 1.0 copy-start
  74.1 16.9 %all-to-all-start.1 = ((bf16[4,16,64,128]{3,2,1,0:T(8,128)(2,1)}), bf16[4,16,64,128]{3,2,1,0:T(8,128)(2,1)S(1)}, u32[]{:S(2)}, u32[]{:S(2)}) async-start(bf16[4,16,64,128]{3,2,1,0:T(8,128)(2,1)} %broadcast_in_dim.5), calls=%async_computation.1 | async-start | bytes 2097152 | tf_op jit(solution)/shard_map/all_to_all | solution.py:111
  77.6 17.4 %copy-start.1 = (bf16[128,4352]{1,0:T(8,128)(2,1)S(1)}, bf16[128,4352]{1,0:T(8,128)(2,1)}, u32[]{:S(2)}) copy-start(bf16[128,4352]{1,0:T(8,128)(2,1)} %copy-done) | copy-start | bytes 3342340
  91.0 20.8 %all-to-all-start.3 = ((bf16[16,64,128]{2,1,0:T(8,128)(2,1)}), bf16[16,64,128]{2,1,0:T(8,128)(2,1)S(1)}, u32[]{:S(2)}, u32[]{:S(2)}) async-start(bf16[16,64,128]{2,1,0:T(8,128)(2,1)} %sum_turn.1), calls=%async_computation.3 | async-start | bytes 524288 | tf_op jit(solution)/shard_map/all_to_all | solution.py:169
  95.0 2.4 %copy-start.4 = (s32[1,4]{1,0:T(1,128)S(1)}, s32[1,4]{1,0:T(1,128)}, u32[]{:S(2)}) copy-start(s32[1,4]{1,0:T(1,128)} %len_ref.3) | copy-start | bytes 52
  95.0 3.6 %copy-start.2 = (bf16[128,4096]{1,0:T(8,128)(2,1)S(1)}, bf16[128,4096]{1,0:T(8,128)(2,1)}, u32[]{:S(2)}) copy-start(bf16[128,4096]{1,0:T(8,128)(2,1)} %get-tuple-element.4.own_ref) | copy-start | bytes 3145732
  95.4 3.1 %collective-permute-start.2 = (f32[128,128]{1,0:T(8,128)S(1)}, f32[128,128]{1,0:T(8,128)S(1)}, u32[]{:S(2)}, u32[]{:S(2)}) collective-permute-start(f32[128,128]{1,0:T(8,128)S(1)} %fusion), channel_id=1, source_target_pairs={{0,6},{6,0},{1,7},{7,1},{2,8},{8,2},{3,9},{9,3},{4,10},{10,4},{5,1... | collective-permute-start | bytes 196616 | tf_op jit(solution)/shard_map/ppermute | solution.py:173
where the time goes:
time: 113 us; the launch traced here: 112 us
  waiting for transfers between devices  42 us (37%)
  starting transfers between devices  33.8 us (30%)
  blocking collectives  18.7 us (17%)
  Pallas kernels  11.4 us (10%)
  local copies, waits for them, and re-layouts  3.56 us (3%)
  other arithmetic  1.42 us (1%)
    all_to_all x1, starting transfers between devices, per_device(): lax.all_to_all(jnp.broadcast_to(w_value[None], (nzy, BLOCK, cols)), ('zh'...  19 us
    all_to_all x1, blocking collectives, per_device(): g_x = lax.all_to_all(send, 'x', 0, 0, tiled=True)  18.7 us
    all_to_all x1, waiting for transfers between devices, per_device(): lax.all_to_all(jnp.broadcast_to(w_value[None], (nzy, BLOCK, cols)), ('zh'...  15.4 us
    all_to_all x1, waiting for transfers between devices, per_device(): g_zy = lax.all_to_all(g_send, ('zh', 'y'), 0, 0, tiled=True)  12.1 us
    all_to_all x1, waiting for transfers between devices, per_device(): lax.all_to_all(jnp.broadcast_to(w_zy[None], (nx, nzy, BLOCK, cols)), 'x',...  11.3 us
    pallas_call x1, Pallas kernels, per_device(): pl.pallas_call(norm_kernel, grid=(rows // step,), in_specs=[pl.BlockSpec(...  4.67 us
    pallas_call x1, Pallas kernels, per_device(): pl.pallas_call(grad_kernel, grid=(nx,), in_specs=[pl.BlockSpec((rows, chu...  4.66 us
    all_to_all x1, starting transfers between devices, per_device(): g_zy = lax.all_to_all(g_send, ('zh', 'y'), 0, 0, tiled=True)  3.96 us
  transfers between devices with their start and end apart: 6, of which 5 were waited for; matrix products, arithmetic and copies ran while one was open for 2% of the time, Pallas kernels for 6%

commit v1 on v0

--- a/solution.py
+++ b/solution.py
@@ -11,22 +11,28 @@
 Y_PAIR = tuple((j, j ^ 1) for j in range(8))
 LANES = 128
 BLOCK = 64
+NX = 4
+X_SHIFTS = tuple(tuple((j, (j + s) % NX) for j in range(NX)) for s in range(NX))
+SWAP_Z = ((0, 1), (1, 0))
 bf16, f32 = jnp.bfloat16, jnp.float32
 
 
-def norm_kernel(core_ref, x_ref, gain_ref, dval_ref, rew_ref, near_ref, len_ref, own_ref, pack_ref):
+def norm_kernel(place_ref, x_ref, gain_ref, dval_ref, rew_ref, near_ref, len_ref, own_ref, pack_ref):
     rows, width = x_ref.shape
     total = jnp.zeros((rows, LANES), f32)
     for k in range(width // LANES):
         v = x_ref[:, k * LANES : (k + 1) * LANES].astype(f32)
         total = total + v * v
     scale = lax.rsqrt(jnp.sum(total, axis=1, keepdims=True) * (1.0 / width) + 1e-5)
-    first = core_ref[0] == 0
+    first = place_ref[0] == 0
     low = lax.broadcasted_iota(jnp.int32, (rows, LANES), 1) < BLOCK
-    for k in range(width // LANES // 2):
-        at = 2 * k * LANES
-        a = x_ref[:, at : at + LANES].astype(f32) * scale * gain_ref[:, at : at + LANES]
-        b = x_ref[:, at + LANES : at + 2 * LANES].astype(f32) * scale * gain_ref[:, at + LANES : at + 2 * LANES]
+    tiles = width // LANES // 2
+    for k in range(tiles):
+        shift, inside = divmod(k, tiles // NX)
+        at = (place_ref[1] + NX - shift) % NX * (width // NX) + inside * 2 * LANES
+        at_a, at_b = pl.ds(pl.multiple_of(at, LANES), LANES), pl.ds(pl.multiple_of(at + LANES, LANES), LANES)
+        a = x_ref[:, at_a].astype(f32) * scale * gain_ref[:, at_a]
+        b = x_ref[:, at_b].astype(f32) * scale * gain_ref[:, at_b]
         even = jnp.where(low, a, pltpu.roll(b, BLOCK, 1))
         odd = jnp.where(low, pltpu.roll(a, BLOCK, 1), b)
         own_ref[:, k * LANES : (k + 1) * LANES] = jnp.where(first, even, odd).astype(bf16)
@@ -43,7 +49,7 @@
     pack_ref[:, half + LANES :] = tail.astype(bf16)
 
 
-def grad_kernel(own_ref, got_ref, gotd_ref, tail_ref, dval_ref, rew_ref, near_ref, len_ref, out_ref, ds_own, ds_other):
+def grad_kernel(place_ref, own_ref, got_ref, gotd_ref, tail_ref, dval_ref, rew_ref, near_ref, len_ref, out_ref, ds_own, ds_other):
     rows, _ = dval_ref.shape
     n = rew_ref.shape[1]
     slots = rows // n
@@ -92,8 +98,8 @@
         total = total + got_ref[s].astype(f32)
     for k in range(total.shape[1] // LANES):
         piece = total[:, k * LANES : (k + 1) * LANES].T.astype(bf16)
-        out_ref[2 * k] = piece[:BLOCK]
-        out_ref[2 * k + 1] = piece[BLOCK:]
+        out_ref[2 * k, 0] = piece[:BLOCK]
+        out_ref[2 * k + 1, 0] = piece[BLOCK:]
 
 
 def per_device(resid, norm_gain, w_value, d_value, rewards, lengths):
@@ -108,10 +114,13 @@
 
     near = lax.ppermute(rewards, "y", Y_PAIR)
     w_zy = lax.all_to_all(jnp.broadcast_to(w_value[None], (nzy, BLOCK, cols)), ("zh", "y"), 0, 0, tiled=True)
-    w_all = lax.all_to_all(jnp.broadcast_to(w_zy[None], (nx, nzy, BLOCK, cols)), "x", 0, 0, tiled=True)
-    w_full = w_all.reshape(half, cols)
-
-    core = lax.axis_index("c").astype(jnp.int32).reshape(1)
+    w_parts = [w_zy]
+    for s in range(1, nx):
+        w_parts.append(lax.ppermute(w_zy, "x", X_SHIFTS[s]))
+    w_full = jnp.concatenate(w_parts).reshape(half, cols)
+
+    zpart = lax.axis_index("zh")
+    place = jnp.stack([lax.axis_index("c"), lax.axis_index("x")]).astype(jnp.int32)
     dval = d_value.reshape(rows, cols)
     rew, near = rewards.reshape(1, rolls), near.reshape(1, rolls)
     step = 32
@@ -136,38 +145,42 @@
             jax.ShapeDtypeStruct((rows, half + 2 * LANES), bf16),
         ],
         name="norm_split",
-    )(core, resid.reshape(rows, width), norm_gain.reshape(1, width), dval, rew, near, lengths)
+    )(place, resid.reshape(rows, width), norm_gain.reshape(1, width), dval, rew, near, lengths)
     got = lax.ppermute(packed, "c", SWAP)
     send = pl.pallas_call(
         grad_kernel,
-        grid=(nx,),
-        in_specs=[
-            pl.BlockSpec((rows, chunk), lambda k: (0, k)),
-            pl.BlockSpec((rows, chunk), lambda k: (0, k)),
-            pl.BlockSpec((rows, cols), lambda k: (0, half // LANES)),
-            pl.BlockSpec((16, LANES), lambda k: (0, half // LANES + 1)),
-            whole(rows, cols),
-            whole(1, rolls),
-            whole(1, rolls),
-            whole(1, rolls),
-        ],
-        out_specs=pl.BlockSpec((1, cols, chunk), lambda k: (k, 0, 0)),
+        grid_spec=pltpu.PrefetchScalarGridSpec(
+            num_scalar_prefetch=1,
+            grid=(nx,),
+            in_specs=[
+                pl.BlockSpec((rows, chunk), lambda k, p: (0, k)),
+                pl.BlockSpec((rows, chunk), lambda k, p: (0, k)),
+                pl.BlockSpec((rows, cols), lambda k, p: (0, half // LANES)),
+                pl.BlockSpec((16, LANES), lambda k, p: (0, half // LANES + 1)),
+                whole(rows, cols),
+                whole(1, rolls),
+                whole(1, rolls),
+                whole(1, rolls),
+            ],
+            out_specs=pl.BlockSpec((1, cols, chunk), lambda k, p: ((p[1] + NX - k) % NX, 0, 0)),
+            scratch_shapes=[pltpu.VMEM((rows, cols), bf16), pltpu.VMEM((rows, cols), bf16)],
+        ),
         out_shape=jax.ShapeDtypeStruct((nx, cols, chunk), bf16),
-        scratch_shapes=[pltpu.VMEM((rows, cols), bf16), pltpu.VMEM((rows, cols), bf16)],
         name="grad_partial",
-    )(own, got, got, got, dval, rew, near, lengths)
+    )(place, own, got, got, got, dval, rew, near, lengths)
     g_x = lax.all_to_all(send, "x", 0, 0, tiled=True)
-    split = 2
     g_send = pl.pallas_call(
         turn_kernel,
-        grid=(split,),
-        in_specs=[pl.BlockSpec((nx, cols, chunk // split), lambda k: (0, 0, k))],
-        out_specs=pl.BlockSpec((nzy // split, BLOCK, cols), lambda k: (k, 0, 0)),
-        out_shape=jax.ShapeDtypeStruct((nzy, BLOCK, cols), bf16),
+        grid=(nz,),
+        in_specs=[pl.BlockSpec((nx, cols, chunk // nz), lambda k: (0, 0, k))],
+        out_specs=pl.BlockSpec((ny, 1, BLOCK, cols), lambda k: (0, k, 0, 0)),
+        out_shape=jax.ShapeDtypeStruct((ny, nz, BLOCK, cols), bf16),
         name="sum_turn",
     )(g_x)
-    g_zy = lax.all_to_all(g_send, ("zh", "y"), 0, 0, tiled=True)
-    w_grad = jnp.sum(g_zy.astype(f32), axis=0).astype(bf16)
+    g_y = lax.all_to_all(g_send, "y", 0, 0, tiled=True)
+    g_sum = jnp.sum(g_y.astype(f32), axis=0)
+    g_z = lax.ppermute(jnp.where(zpart == 0, g_sum[1], g_sum[0]), "zh", SWAP_Z)
+    w_grad = (jnp.where(zpart == 0, g_sum[0], g_sum[1]) + g_z).astype(bf16)
 
     v_other = jnp.dot(got[:, :half], w_full, preferred_element_type=f32)
     v_got = lax.ppermute(v_other, "c", SWAP)

time: 113 us -> 119 us (1.053)
  blocking collectives: 18.7 us -> 0 us
  starting transfers between devices: 33.8 us -> 48.9 us
  waiting for transfers between devices: 42 us -> 50.5 us
    ppermute x0 -> x4, waiting for transfers between devices: none -> 22.4 us  [the longest x3 13.3 us: per_device(): w_parts.append(lax.ppermute(w_zy, 'x', X_SHIFTS[s]))]
    all_to_all x1 -> x0, blocking collectives: 18.7 us -> none  [per_device(): g_x = lax.all_to_all(send, 'x', 0, 0, tiled=True)]
    ppermute x0 -> x4, starting transfers between devices: none -> 14.3 us  [the longest x3 12 us: per_device(): w_parts.append(lax.ppermute(w_zy, 'x', X_SHIFTS[s]))]
    all_to_all x2, waiting for transfers between devices: 23.4 us -> 12 us  [the longest x1 12 us: per_device(): g_y = lax.all_to_all(g_send, 'y', 0, 0, tiled=True)]
    broadcast_in_dim x1 -> x0, local copies, waits for them, and re-layouts: 1.27 us -> none  [per_device(): jnp.broadcast_to(w_zy[None], (nx, nzy, BLOCK, cols))]
    unnamed x12 -> x14, local copies, waits for them, and re-layouts: 1.53 us -> 2.52 us
  transfers between devices with their start and end apart: 6 -> 10, of which waited for: 5 -> 6; matrix products, arithmetic and copies ran while one was open for 2% -> 3% of each run, Pallas kernels for 6% -> 6%
where the time goes in v1:
time: 119 us
  waiting for transfers between devices  50.5 us (42%)
  starting transfers between devices  48.9 us (41%)
  Pallas kernels  12.2 us (10%)
  local copies, waits for them, and re-layouts  3.26 us (3%)
  other arithmetic  2.15 us (2%)
    all_to_all x1, starting transfers between devices, per_device(): lax.all_to_all(jnp.broadcast_to(w_value[None], (nzy, BLOCK, cols)), ('zh'...  19 us
    all_to_all x1, waiting for transfers between devices, per_device(): lax.all_to_all(jnp.broadcast_to(w_value[None], (nzy, BLOCK, cols)), ('zh'...  14.6 us
    ppermute x3, waiting for transfers between devices, per_device(): w_parts.append(lax.ppermute(w_zy, 'x', X_SHIFTS[s]))  13.3 us
    all_to_all x1, waiting for transfers between devices, per_device(): g_y = lax.all_to_all(g_send, 'y', 0, 0, tiled=True)  12 us
    ppermute x3, starting transfers between devices, per_device(): w_parts.append(lax.ppermute(w_zy, 'x', X_SHIFTS[s]))  12 us
    ppermute x1, waiting for transfers between devices, per_device(): g_z = lax.ppermute(jnp.where(zpart == 0, g_sum[1], g_sum[0]), 'zh', SWAP_Z)  9.06 us
    pallas_call x1, Pallas kernels, per_device(): pl.pallas_call(grad_kernel, grid_spec=pltpu.PrefetchScalarGridSpec(num_sc...  5.36 us
    pallas_call x1, Pallas kernels, per_device(): pl.pallas_call(norm_kernel, grid=(rows // step,), in_specs=[pl.BlockSpec(...  4.8 us
  transfers between devices with their start and end apart: 10, of which 6 were waited for; matrix products, arithmetic and copies ran while one was open for 3% of the time, Pallas kernels for 6%

profile of v1, /device:TPU:64, one launch (start us, length us, event | category | flops | bytes accessed | tf_op | source)
XLA Modules:
  0.0 118.7 jit_solution(2104805064907933885)
XLA Ops:
  0.6 0.0 copy-start.4
  0.6 3.5 %collective-permute-start = (bf16[4]{0:T(256)(128)(2,1)}, bf16[4]{0:T(256)(128)(2,1)S(1)}, u32[]{:S(2)}, u32[]{:S(2)}) collective-permute-start(bf16[4]{0:T(256)(128)(2,1)} %param.10), channel_id=1, source_target_pairs={{0,12},{12,0},{24,36},{36,24},{48,60},{60,48},{72,84},{84,72},{1,1... | collective-permute-start | bytes 32 | tf_op jit(solution)/shard_map/ppermute | solution.py:115
  4.1 0.6 pad_add_fusion.place_ref
  4.7 1.5 %collective-permute-done = bf16[4]{0:T(256)(128)(2,1)S(1)} collective-permute-done((bf16[4]{0:T(256)(128)(2,1)}, bf16[4]{0:T(256)(128)(2,1)S(1)}, u32[]{:S(2)}, u32[]{:S(2)}) %collective-permute-start) | collective-permute-done | bytes 40 | tf_op jit(solution)/shard_map/ppermute | solution.py:115
  6.2 0.0 copy-start.6
  6.2 0.5 copy-done.6
  6.7 4.8 %norm_split.1 = (bf16[128,4096]{1,0:T(8,128)(2,1)}, bf16[128,4352]{1,0:T(8,128)(2,1)}) custom-call(s32[2]{0:T(128)} %pad_add_fusion.place_ref, bf16[128,8192]{1,0:T(8,128)(2,1)} %bitcast.21, f32[1,8192]{1,0:T(1,128)} %bitcast.25, bf16[128,128]{1,0:T(8,128)(2,1)} %bitcast.23, bf16[1,4]{1,0:T(2,128)(2,1)} %bitcast.27, bf16[1,4]{1,0:T(2,128)(2,1)} %bitcast.29, ...), custom_call_target="tpu_custom_call" | custom-call | tf_op jit(solution)/shard_map/norm_split/pallas_call | solution.py:127
  11.5 1.9 %collective-permute-start.4 = (bf16[128,4352]{1,0:T(8,128)(2,1)}, bf16[128,4352]{1,0:T(8,128)(2,1)S(1)}, u32[]{:S(2)}, u32[]{:S(2)}) collective-permute-start(bf16[128,4352]{1,0:T(8,128)(2,1)} %get-tuple-element.5), channel_id=1, source_target_pairs={{0,6},{6,0},{1,7},{7,1},{2,8},{8,2},{3,9},{9,3},{4,10},{10,4},{5,1... | collective-permute-start | bytes 3342344 | tf_op jit(solution)/shard_map/ppermute | solution.py:149
  13.5 0.0 copy-done.4
  13.5 0.7 broadcast_in_dim.2
  14.2 19.0 %all-to-all-start = ((bf16[16,64,128]{2,1,0:T(8,128)(2,1)}), bf16[16,64,128]{2,1,0:T(8,128)(2,1)S(1)}, u32[]{:S(2)}, u32[]{:S(2)}) async-start(bf16[16,64,128]{2,1,0:T(8,128)(2,1)} %broadcast_in_dim.2), calls=%async_computation | async-start | bytes 524288 | tf_op jit(solution)/shard_map/all_to_all | solution.py:116
  33.2 0.0 collective-permute-done.4.got_ref.gotd_ref.tail_ref
  33.2 0.0 copy-start
  33.2 1.0 copy-done
  34.2 5.4 %grad_partial.1 = bf16[4,128,1024]{2,1,0:T(8,128)(2,1)} custom-call(s32[2]{0:T(128)} %pad_add_fusion.place_ref, bf16[128,4096]{1,0:T(8,128)(2,1)} %get-tuple-element.4.own_ref, bf16[128,4352]{1,0:T(8,128)(2,1)} %copy-done, bf16[128,4352]{1,0:T(8,128)(2,1)} %copy-done, bf16[128,4352]{1,0:T(8,128)(2,1)} %copy-done, bf16[128,128]{1,0:T(8,128)(2,1)} %bitcast.24, ...), custom_call_target="tpu_custom_call" | custom-call | tf_op jit(solution)/shard_map/grad_partial/pallas_call | solution.py:150
  39.6 14.6 %all-to-all-done = bf16[16,64,128]{2,1,0:T(8,128)(2,1)S(1)} async-done(((bf16[16,64,128]{2,1,0:T(8,128)(2,1)}), bf16[16,64,128]{2,1,0:T(8,128)(2,1)S(1)}, u32[]{:S(2)}, u32[]{:S(2)}) %all-to-all-start) | async-done | bytes 262176 | tf_op jit(solution)/shard_map/all_to_all | solution.py:116
  54.2 4.3 %all-to-all-start.1 = ((bf16[4,128,1024]{2,1,0:T(8,128)(2,1)}), bf16[4,128,1024]{2,1,0:T(8,128)(2,1)S(1)}, u32[]{:S(2)}, u32[]{:S(2)}) async-start(bf16[4,128,1024]{2,1,0:T(8,128)(2,1)} %grad_partial.1), calls=%async_computation.1 | async-start | bytes 2097152 | tf_op jit(solution)/shard_map/all_to_all | solution.py:171
  58.5 0.0 copy-start.1
  58.5 4.1 %collective-permute-start.1 = (bf16[16,64,128]{2,1,0:T(8,128)(2,1)S(1)}, bf16[16,64,128]{2,1,0:T(8,128)(2,1)S(1)}, u32[]{:S(2)}, u32[]{:S(2)}) collective-permute-start(bf16[16,64,128]{2,1,0:T(8,128)(2,1)S(1)} %all-to-all-done), channel_id=1, source_target_pairs={{0,192},{192,384},{384,576},{576,0},{1,193},{193,385},{385,577},{5... | collective-permute-start | bytes 786440 | tf_op jit(solution)/shard_map/ppermute | solution.py:119
  62.6 4.6 %collective-permute-start.2 = (bf16[16,64,128]{2,1,0:T(8,128)(2,1)S(1)}, bf16[16,64,128]{2,1,0:T(8,128)(2,1)S(1)}, u32[]{:S(2)}, u32[]{:S(2)}) collective-permute-start(bf16[16,64,128]{2,1,0:T(8,128)(2,1)S(1)} %all-to-all-done), channel_id=1, source_target_pairs={{0,384},{192,576},{384,0},{576,192},{1,385},{193,577},{385,1},{577... | collective-permute-start | bytes 786440 | tf_op jit(solution)/shard_map/ppermute | solution.py:119
  67.2 3.4 %collective-permute-start.3 = (bf16[16,64,128]{2,1,0:T(8,128)(2,1)S(1)}, bf16[16,64,128]{2,1,0:T(8,128)(2,1)S(1)}, u32[]{:S(2)}, u32[]{:S(2)}) collective-permute-start(bf16[16,64,128]{2,1,0:T(8,128)(2,1)S(1)} %all-to-all-done), channel_id=1, source_target_pairs={{0,576},{192,0},{384,192},{576,384},{1,577},{193,1},{385,193},{577... | collective-permute-start | bytes 786440 | tf_op jit(solution)/shard_map/ppermute | solution.py:119
  70.6 9.5 %collective-permute-done.1 = bf16[16,64,128]{2,1,0:T(8,128)(2,1)S(1)} collective-permute-done((bf16[16,64,128]{2,1,0:T(8,128)(2,1)S(1)}, bf16[16,64,128]{2,1,0:T(8,128)(2,1)S(1)}, u32[]{:S(2)}, u32[]{:S(2)}) %collective-permute-start.1) | collective-permute-done | bytes 262176 | tf_op jit(solution)/shard_map/ppermute | solution.py:119
  80.1 3.8 %collective-permute-done.2 = bf16[16,64,128]{2,1,0:T(8,128)(2,1)S(1)} collective-permute-done((bf16[16,64,128]{2,1,0:T(8,128)(2,1)S(1)}, bf16[16,64,128]{2,1,0:T(8,128)(2,1)S(1)}, u32[]{:S(2)}, u32[]{:S(2)}) %collective-permute-start.2) | collective-permute-done | bytes 262176 | tf_op jit(solution)/shard_map/ppermute | solution.py:119
  83.9 0.0 collective-permute-done.3
  83.9 0.1 pad_maximum_fusion
  84.0 0.0 copy-done.1
  84.0 0.4 fusion
  84.4 0.0 copy-start.5
  84.5 0.0 copy-start.2
  84.5 2.1 %collective-permute-start.5 = (f32[128,128]{1,0:T(8,128)S(1)}, f32[128,128]{1,0:T(8,128)S(1)}, u32[]{:S(2)}, u32[]{:S(2)}) collective-permute-start(f32[128,128]{1,0:T(8,128)S(1)} %fusion), channel_id=1, source_target_pairs={{0,6},{6,0},{1,7},{7,1},{2,8},{8,2},{3,9},{9,3},{4,10},{10,4},{5,1... | collective-permute-start | bytes 196616 | tf_op jit(solution)/shard_map/ppermute | solution.py:186
  86.5 0.0 all-to-all-done.1.got_ref
  86.5 0.0 copy-start.3
  86.6 1.0 copy-done.3
  87.5 2.0 %sum_turn.1 = bf16[8,2,64,128]{3,2,1,0:T(8,128)(2,1)} custom-call(bf16[4,128,1024]{2,1,0:T(8,128)(2,1)} %copy-done.3), custom_call_target="tpu_custom_call" | custom-call | tf_op jit(solution)/shard_map/sum_turn/pallas_call | solution.py:172
  89.5 3.8 %all-to-all-start.2 = ((bf16[8,2,64,128]{3,2,1,0:T(8,128)(2,1)}), bf16[8,2,64,128]{3,2,1,0:T(8,128)(2,1)S(1)}, u32[]{:S(2)}, u32[]{:S(2)}) async-start(bf16[8,2,64,128]{3,2,1,0:T(8,128)(2,1)} %sum_turn.1), calls=%async_computation.2 | async-start | bytes 524288 | tf_op jit(solution)/shard_map/all_to_all | solution.py:180
  93.4 0.0 copy-done.5
  93.4 0.1 fusion.3
  93.4 0.0 collective-permute-done.5
  93.4 0.0 copy-done.2
  93.5 0.4 convolution_add_fusion
  93.9 12.0 %all-to-all-done.2 = bf16[8,2,64,128]{3,2,1,0:T(8,128)(2,1)S(1)} async-done(((bf16[8,2,64,128]{3,2,1,0:T(8,128)(2,1)}), bf16[8,2,64,128]{3,2,1,0:T(8,128)(2,1)S(1)}, u32[]{:S(2)}, u32[]{:S(2)}) %all-to-all-start.2) | async-done | bytes 262176 | tf_op jit(solution)/shard_map/all_to_all | solution.py:180
  106.0 2.3 %collective-permute-start.6 = (f32[64,128]{1,0:T(8,128)S(1)}, f32[64,128]{1,0:T(8,128)S(1)}, u32[]{:S(2)}, u32[]{:S(2)}) collective-permute-start(f32[64,128]{1,0:T(8,128)S(1)} %select_bitcast_fusion), channel_id=1, source_target_pairs={{0,96},{96,0},{1,97},{97,1},{2,98},{98,2},{3,99},{99,3},{4,100},{1... | collective-permute-start | bytes 98312 | tf_op jit(solution)/shard_map/ppermute | solution.py:182
  108.3 0.7 multiply_convert_fusion
  109.0 9.1 %collective-permute-done.6 = f32[64,128]{1,0:T(8,128)S(1)} collective-permute-done((f32[64,128]{1,0:T(8,128)S(1)}, f32[64,128]{1,0:T(8,128)S(1)}, u32[]{:S(2)}, u32[]{:S(2)}) %collective-permute-start.6) | collective-permute-done | bytes 32800 | tf_op jit(solution)/shard_map/ppermute | solution.py:182
  118.1 0.6 fusion.2
  (2 shorter events, 0.0 us)
Async XLA Ops:
  0.6 12.8 %copy-start.4 = (bf16[64,128]{1,0:T(8,128)(2,1)S(1)}, bf16[64,128]{1,0:T(8,128)(2,1)}, u32[]{:S(2)}) copy-start(bf16[64,128]{1,0:T(8,128)(2,1)} %param.8) | copy-start | bytes 49156
  0.6 5.6 %collective-permute-start = (bf16[4]{0:T(256)(128)(2,1)}, bf16[4]{0:T(256)(128)(2,1)S(1)}, u32[]{:S(2)}, u32[]{:S(2)}) collective-permute-start(bf16[4]{0:T(256)(128)(2,1)} %param.10), channel_id=1, source_target_pairs={{0,12},{12,0},{24,36},{36,24},{48,60},{60,48},{72,84},{84,72},{1,1... | collective-permute-start | bytes 32 | tf_op jit(solution)/shard_map/ppermute | solution.py:115
  6.2 0.5 copy-start.6
  11.5 21.7 %collective-permute-start.4 = (bf16[128,4352]{1,0:T(8,128)(2,1)}, bf16[128,4352]{1,0:T(8,128)(2,1)S(1)}, u32[]{:S(2)}, u32[]{:S(2)}) collective-permute-start(bf16[128,4352]{1,0:T(8,128)(2,1)} %get-tuple-element.5), channel_id=1, source_target_pairs={{0,6},{6,0},{1,7},{7,1},{2,8},{8,2},{3,9},{9,3},{4,10},{10,4},{5,1... | collective-permute-start | bytes 3342344 | tf_op jit(solution)/shard_map/ppermute | solution.py:149
  14.2 40.0 %all-to-all-start = ((bf16[16,64,128]{2,1,0:T(8,128)(2,1)}), bf16[16,64,128]{2,1,0:T(8,128)(2,1)S(1)}, u32[]{:S(2)}, u32[]{:S(2)}) async-start(bf16[16,64,128]{2,1,0:T(8,128)(2,1)} %broadcast_in_dim.2), calls=%async_computation | async-start | bytes 524288 | tf_op jit(solution)/shard_map/all_to_all | solution.py:116
  33.2 1.0 copy-start
  54.2 32.3 %all-to-all-start.1 = ((bf16[4,128,1024]{2,1,0:T(8,128)(2,1)}), bf16[4,128,1024]{2,1,0:T(8,128)(2,1)S(1)}, u32[]{:S(2)}, u32[]{:S(2)}) async-start(bf16[4,128,1024]{2,1,0:T(8,128)(2,1)} %grad_partial.1), calls=%async_computation.1 | async-start | bytes 2097152 | tf_op jit(solution)/shard_map/all_to_all | solution.py:171
  58.5 25.5 %copy-start.1 = (bf16[128,4352]{1,0:T(8,128)(2,1)S(1)}, bf16[128,4352]{1,0:T(8,128)(2,1)}, u32[]{:S(2)}) copy-start(bf16[128,4352]{1,0:T(8,128)(2,1)} %copy-done) | copy-start | bytes 3342340
  58.5 21.5 %collective-permute-start.1 = (bf16[16,64,128]{2,1,0:T(8,128)(2,1)S(1)}, bf16[16,64,128]{2,1,0:T(8,128)(2,1)S(1)}, u32[]{:S(2)}, u32[]{:S(2)}) collective-permute-start(bf16[16,64,128]{2,1,0:T(8,128)(2,1)S(1)} %all-to-all-done), channel_id=1, source_target_pairs={{0,192},{192,384},{384,576},{576,0},{1,193},{193,385},{385,577},{5... | collective-permute-start | bytes 786440 | tf_op jit(solution)/shard_map/ppermute | solution.py:119
  62.6 21.3 %collective-permute-start.2 = (bf16[16,64,128]{2,1,0:T(8,128)(2,1)S(1)}, bf16[16,64,128]{2,1,0:T(8,128)(2,1)S(1)}, u32[]{:S(2)}, u32[]{:S(2)}) collective-permute-start(bf16[16,64,128]{2,1,0:T(8,128)(2,1)S(1)} %all-to-all-done), channel_id=1, source_target_pairs={{0,384},{192,576},{384,0},{576,192},{1,385},{193,577},{385,1},{577... | collective-permute-start | bytes 786440 | tf_op jit(solution)/shard_map/ppermute | solution.py:119
  67.2 16.7 %collective-permute-start.3 = (bf16[16,64,128]{2,1,0:T(8,128)(2,1)S(1)}, bf16[16,64,128]{2,1,0:T(8,128)(2,1)S(1)}, u32[]{:S(2)}, u32[]{:S(2)}) collective-permute-start(bf16[16,64,128]{2,1,0:T(8,128)(2,1)S(1)} %all-to-all-done), channel_id=1, source_target_pairs={{0,576},{192,0},{384,192},{576,384},{1,577},{193,1},{385,193},{577... | collective-permute-start | bytes 786440 | tf_op jit(solution)/shard_map/ppermute | solution.py:119
  84.4 8.9 %copy-start.5 = (s32[1,4]{1,0:T(1,128)S(1)}, s32[1,4]{1,0:T(1,128)}, u32[]{:S(2)}) copy-start(s32[1,4]{1,0:T(1,128)} %len_ref.3) | copy-start | bytes 52
  84.5 9.0 %copy-start.2 = (bf16[128,4096]{1,0:T(8,128)(2,1)S(1)}, bf16[128,4096]{1,0:T(8,128)(2,1)}, u32[]{:S(2)}) copy-start(bf16[128,4096]{1,0:T(8,128)(2,1)} %get-tuple-element.4.own_ref) | copy-start | bytes 3145732
  84.5 9.0 %collective-permute-start.5 = (f32[128,128]{1,0:T(8,128)S(1)}, f32[128,128]{1,0:T(8,128)S(1)}, u32[]{:S(2)}, u32[]{:S(2)}) collective-permute-start(f32[128,128]{1,0:T(8,128)S(1)} %fusion), channel_id=1, source_target_pairs={{0,6},{6,0},{1,7},{7,1},{2,8},{8,2},{3,9},{9,3},{4,10},{10,4},{5,1... | collective-permute-start | bytes 196616 | tf_op jit(solution)/shard_map/ppermute | solution.py:186
  86.5 1.0 copy-start.3
  89.5 16.4 %all-to-all-start.2 = ((bf16[8,2,64,128]{3,2,1,0:T(8,128)(2,1)}), bf16[8,2,64,128]{3,2,1,0:T(8,128)(2,1)S(1)}, u32[]{:S(2)}, u32[]{:S(2)}) async-start(bf16[8,2,64,128]{3,2,1,0:T(8,128)(2,1)} %sum_turn.1), calls=%async_computation.2 | async-start | bytes 524288 | tf_op jit(solution)/shard_map/all_to_all | solution.py:180
  106.0 12.1 %collective-permute-start.6 = (f32[64,128]{1,0:T(8,128)S(1)}, f32[64,128]{1,0:T(8,128)S(1)}, u32[]{:S(2)}, u32[]{:S(2)}) collective-permute-start(f32[64,128]{1,0:T(8,128)S(1)} %select_bitcast_fusion), channel_id=1, source_target_pairs={{0,96},{96,0},{1,97},{97,1},{2,98},{98,2},{3,99},{99,3},{4,100},{1... | collective-permute-start | bytes 98312 | tf_op jit(solution)/shard_map/ppermute | solution.py:182

commit v2 on v1

--- a/solution.py
+++ b/solution.py
@@ -17,20 +17,21 @@
 bf16, f32 = jnp.bfloat16, jnp.float32
 
 
-def norm_kernel(place_ref, x_ref, gain_ref, dval_ref, rew_ref, near_ref, len_ref, own_ref, pack_ref):
+def norm_kernel(core_ref, xpos_ref, x_ref, gain_ref, dval_ref, rew_ref, near_ref, len_ref, own_ref, pack_ref):
     rows, width = x_ref.shape
     total = jnp.zeros((rows, LANES), f32)
     for k in range(width // LANES):
         v = x_ref[:, k * LANES : (k + 1) * LANES].astype(f32)
         total = total + v * v
     scale = lax.rsqrt(jnp.sum(total, axis=1, keepdims=True) * (1.0 / width) + 1e-5)
-    first = place_ref[0] == 0
+    first = core_ref[0] == 0
     low = lax.broadcasted_iota(jnp.int32, (rows, LANES), 1) < BLOCK
     tiles = width // LANES // 2
     for k in range(tiles):
         shift, inside = divmod(k, tiles // NX)
-        at = (place_ref[1] + NX - shift) % NX * (width // NX) + inside * 2 * LANES
-        at_a, at_b = pl.ds(pl.multiple_of(at, LANES), LANES), pl.ds(pl.multiple_of(at + LANES, LANES), LANES)
+        at = (xpos_ref[0] + NX - shift) % NX * (width // NX) + inside * LANES
+        next_z = at + width // NX // 2
+        at_a, at_b = pl.ds(pl.multiple_of(at, LANES), LANES), pl.ds(pl.multiple_of(next_z, LANES), LANES)
         a = x_ref[:, at_a].astype(f32) * scale * gain_ref[:, at_a]
         b = x_ref[:, at_b].astype(f32) * scale * gain_ref[:, at_b]
         even = jnp.where(low, a, pltpu.roll(b, BLOCK, 1))
@@ -49,7 +50,7 @@
     pack_ref[:, half + LANES :] = tail.astype(bf16)
 
 
-def grad_kernel(place_ref, own_ref, got_ref, gotd_ref, tail_ref, dval_ref, rew_ref, near_ref, len_ref, out_ref, ds_own, ds_other):
+def grad_kernel(xpos_ref, own_ref, got_ref, gotd_ref, tail_ref, dval_ref, rew_ref, near_ref, len_ref, out_ref, ds_own, ds_other):
     rows, _ = dval_ref.shape
     n = rew_ref.shape[1]
     slots = rows // n
@@ -89,17 +90,8 @@
     over_rows = (((0,), (0,)), ((), ()))
     acc = lax.dot_general(ds_own[...], own_ref[...], over_rows, preferred_element_type=f32)
     acc = acc + lax.dot_general(ds_other[...], got_ref[...], over_rows, preferred_element_type=f32)
-    out_ref[0] = acc.astype(bf16)
-
-
-def turn_kernel(got_ref, out_ref):
-    total = got_ref[0].astype(f32)
-    for s in range(1, got_ref.shape[0]):
-        total = total + got_ref[s].astype(f32)
-    for k in range(total.shape[1] // LANES):
-        piece = total[:, k * LANES : (k + 1) * LANES].T.astype(bf16)
-        out_ref[2 * k, 0] = piece[:BLOCK]
-        out_ref[2 * k + 1, 0] = piece[BLOCK:]
+    for j in range(out_ref.shape[0]):
+        out_ref[j] = acc[:, j * LANES : (j + 1) * LANES].astype(bf16)
 
 
 def per_device(resid, norm_gain, w_value, d_value, rewards, lengths):
@@ -107,20 +99,22 @@
     rows = rolls * slots
     cols = w_value.shape[1]
     nx, nz, ny, nc = [lax.axis_size(a) for a in DP]
-    nzy = nz * ny
     half = width // nc
     chunk = half // nx
     whole = lambda *shape: pl.BlockSpec(shape, lambda *_: (0,) * len(shape))
 
     near = lax.ppermute(rewards, "y", Y_PAIR)
-    w_zy = lax.all_to_all(jnp.broadcast_to(w_value[None], (nzy, BLOCK, cols)), ("zh", "y"), 0, 0, tiled=True)
-    w_parts = [w_zy]
+    w_far = lax.ppermute(w_value, "zh", SWAP_Z)
+    zpart = lax.axis_index("zh")
+    w_pair = jnp.where(zpart == 0, jnp.stack([w_value, w_far]), jnp.stack([w_far, w_value]))
+    w_y = lax.all_to_all(jnp.broadcast_to(w_pair[None], (ny, nz, BLOCK, cols)), "y", 0, 0, tiled=True)
+    w_parts = [w_y]
     for s in range(1, nx):
-        w_parts.append(lax.ppermute(w_zy, "x", X_SHIFTS[s]))
+        w_parts.append(lax.ppermute(w_y, "x", X_SHIFTS[s]))
     w_full = jnp.concatenate(w_parts).reshape(half, cols)
 
-    zpart = lax.axis_index("zh")
-    place = jnp.stack([lax.axis_index("c"), lax.axis_index("x")]).astype(jnp.int32)
+    core = lax.axis_index("c").astype(jnp.int32).reshape(1)
+    xpos = lax.axis_index("x").astype(jnp.int32).reshape(1)
     dval = d_value.reshape(rows, cols)
     rew, near = rewards.reshape(1, rolls), near.reshape(1, rolls)
     step = 32
@@ -128,6 +122,7 @@
         norm_kernel,
         grid=(rows // step,),
         in_specs=[
+            pl.BlockSpec(memory_space=pltpu.SMEM),
             pl.BlockSpec(memory_space=pltpu.SMEM),
             pl.BlockSpec((step, width), lambda i: (i, 0)),
             whole(1, width),
@@ -145,7 +140,7 @@
             jax.ShapeDtypeStruct((rows, half + 2 * LANES), bf16),
         ],
         name="norm_split",
-    )(place, resid.reshape(rows, width), norm_gain.reshape(1, width), dval, rew, near, lengths)
+    )(core, xpos, resid.reshape(rows, width), norm_gain.reshape(1, width), dval, rew, near, lengths)
     got = lax.ppermute(packed, "c", SWAP)
     send = pl.pallas_call(
         grad_kernel,
@@ -162,23 +157,14 @@
                 whole(1, rolls),
                 whole(1, rolls),
             ],
-            out_specs=pl.BlockSpec((1, cols, chunk), lambda k, p: ((p[1] + NX - k) % NX, 0, 0)),
+            out_specs=pl.BlockSpec((ny, cols, nz * BLOCK), lambda k, p: ((p[0] + NX - k) % NX, 0, 0)),
             scratch_shapes=[pltpu.VMEM((rows, cols), bf16), pltpu.VMEM((rows, cols), bf16)],
         ),
-        out_shape=jax.ShapeDtypeStruct((nx, cols, chunk), bf16),
+        out_shape=jax.ShapeDtypeStruct((nx * ny, cols, nz * BLOCK), bf16),
         name="grad_partial",
-    )(place, own, got, got, got, dval, rew, near, lengths)
-    g_x = lax.all_to_all(send, "x", 0, 0, tiled=True)
-    g_send = pl.pallas_call(
-        turn_kernel,
-        grid=(nz,),
-        in_specs=[pl.BlockSpec((nx, cols, chunk // nz), lambda k: (0, 0, k))],
-        out_specs=pl.BlockSpec((ny, 1, BLOCK, cols), lambda k: (0, k, 0, 0)),
-        out_shape=jax.ShapeDtypeStruct((ny, nz, BLOCK, cols), bf16),
-        name="sum_turn",
-    )(g_x)
-    g_y = lax.all_to_all(g_send, "y", 0, 0, tiled=True)
-    g_sum = jnp.sum(g_y.astype(f32), axis=0)
+    )(xpos, own, got, got, got, dval, rew, near, lengths)
+    g_xy = lax.all_to_all(send, ("x", "y"), 0, 0, tiled=True)
+    g_sum = jnp.sum(g_xy.astype(f32), axis=0).T.reshape(nz, BLOCK, cols)
     g_z = lax.ppermute(jnp.where(zpart == 0, g_sum[1], g_sum[0]), "zh", SWAP_Z)
     w_grad = (jnp.where(zpart == 0, g_sum[0], g_sum[1]) + g_z).astype(bf16)
 

time: 119 us -> 102 us (0.86)
  the two profiles are of different devices: /device:TPU:64 before, /device:TPU:18 now
where the time goes in v2:
time: 102 us; the launch traced here: 101 us
  starting transfers between devices  57.7 us (57%)
  waiting for transfers between devices  27.9 us (27%)
  Pallas kernels  9.43 us (9%)
  local copies, waits for them, and re-layouts  3.07 us (3%)
  other arithmetic  1.23 us (1%)
    ppermute x3, waiting for transfers between devices, per_device(): w_parts.append(lax.ppermute(w_y, 'x', X_SHIFTS[s]))  16.7 us
    ppermute x1, starting transfers between devices, per_device(): w_far = lax.ppermute(w_value, 'zh', SWAP_Z)  15.1 us
    ppermute x3, starting transfers between devices, per_device(): w_parts.append(lax.ppermute(w_y, 'x', X_SHIFTS[s]))  10.6 us
    ppermute x1, starting transfers between devices, per_device(): g_z = lax.ppermute(jnp.where(zpart == 0, g_sum[1], g_sum[0]), 'zh', SWAP_Z)  9.9 us
    all_to_all x1, starting transfers between devices, per_device(): lax.all_to_all(jnp.broadcast_to(w_pair[None], (ny, nz, BLOCK, cols)), 'y'...  7.43 us
    all_to_all x1, starting transfers between devices, per_device(): g_xy = lax.all_to_all(send, ('x', 'y'), 0, 0, tiled=True)  7.31 us
    pallas_call x1, Pallas kernels, per_device(): pl.pallas_call(norm_kernel, grid=(rows // step,), in_specs=[pl.BlockSpec(...  4.76 us
    pallas_call x1, Pallas kernels, per_device(): pl.pallas_call(grad_kernel, grid_spec=pltpu.PrefetchScalarGridSpec(num_sc...  4.67 us
  transfers between devices with their start and end apart: 10, of which 8 were waited for; matrix products, arithmetic and copies ran while one was open for 3% of the time, Pallas kernels for 5%

profile of v2, /device:TPU:18, one launch (start us, length us, event | category | flops | bytes accessed | tf_op | source)
XLA Modules:
  0.0 101.0 jit_solution(11762208513177306974)
XLA Ops:
  0.6 0.0 copy-start.3
  0.6 3.5 %collective-permute-start = (bf16[4]{0:T(256)(128)(2,1)}, bf16[4]{0:T(256)(128)(2,1)S(1)}, u32[]{:S(2)}, u32[]{:S(2)}) collective-permute-start(bf16[4]{0:T(256)(128)(2,1)} %param.10), channel_id=1, source_target_pairs={{0,12},{12,0},{24,36},{36,24},{48,60},{60,48},{72,84},{84,72},{1,1... | collective-permute-start | bytes 32 | tf_op jit(solution)/shard_map/ppermute | solution.py:106
  4.1 2.1 %collective-permute-done = bf16[4]{0:T(256)(128)(2,1)S(1)} collective-permute-done((bf16[4]{0:T(256)(128)(2,1)}, bf16[4]{0:T(256)(128)(2,1)S(1)}, u32[]{:S(2)}, u32[]{:S(2)}) %collective-permute-start) | collective-permute-done | bytes 40 | tf_op jit(solution)/shard_map/ppermute | solution.py:106
  6.2 0.0 copy-start.5
  6.2 0.6 copy-done.5
  6.8 4.8 %norm_split.1 = (bf16[128,4096]{1,0:T(8,128)(2,1)}, bf16[128,4352]{1,0:T(8,128)(2,1)}) custom-call(s32[1]{0:T(128)} %bitcast.core_ref, s32[1]{0:T(128)} %bitcast.1.xpos_ref, bf16[128,8192]{1,0:T(8,128)(2,1)} %bitcast.18, f32[1,8192]{1,0:T(1,128)} %bitcast.24, bf16[128,128]{1,0:T(8,128)(2,1)} %bitcast.22, bf16[1,4]{1,0:T(2,128)(2,1)} %bitcast.28, ...), custom_call_target="tpu_custom_call" | custom-call | tf_op jit(solution)/shard_map/norm_split/pallas_call | solution.py:121
  11.6 1.9 %collective-permute-start.5 = (bf16[128,4352]{1,0:T(8,128)(2,1)}, bf16[128,4352]{1,0:T(8,128)(2,1)S(1)}, u32[]{:S(2)}, u32[]{:S(2)}) collective-permute-start(bf16[128,4352]{1,0:T(8,128)(2,1)} %get-tuple-element.5), channel_id=1, source_target_pairs={{0,6},{6,0},{1,7},{7,1},{2,8},{8,2},{3,9},{9,3},{4,10},{10,4},{5,1... | collective-permute-start | bytes 3342344 | tf_op jit(solution)/shard_map/ppermute | solution.py:144
  13.5 0.0 copy-done.3
  13.5 15.1 %collective-permute-start.1 = (bf16[64,128]{1,0:T(8,128)(2,1)S(1)}, bf16[64,128]{1,0:T(8,128)(2,1)S(1)}, u32[]{:S(2)}, u32[]{:S(2)}) collective-permute-start(bf16[64,128]{1,0:T(8,128)(2,1)S(1)} %copy-done.3), channel_id=1, source_target_pairs={{0,96},{96,0},{1,97},{97,1},{2,98},{98,2},{3,99},{99,3},{4,100},{1... | collective-permute-start | bytes 49160 | tf_op jit(solution)/shard_map/ppermute | solution.py:107
  28.7 1.7 %collective-permute-done.1 = bf16[64,128]{1,0:T(8,128)(2,1)S(1)} collective-permute-done((bf16[64,128]{1,0:T(8,128)(2,1)S(1)}, bf16[64,128]{1,0:T(8,128)(2,1)S(1)}, u32[]{:S(2)}, u32[]{:S(2)}) %collective-permute-start.1) | collective-permute-done | bytes 16416 | tf_op jit(solution)/shard_map/ppermute | solution.py:107
  30.4 0.8 broadcast_in_dim.2
  31.1 7.4 %all-to-all-start = ((bf16[8,2,64,128]{3,2,1,0:T(8,128)(2,1)}), bf16[8,2,64,128]{3,2,1,0:T(8,128)(2,1)S(1)}, u32[]{:S(2)}, u32[]{:S(2)}) async-start(bf16[8,2,64,128]{3,2,1,0:T(8,128)(2,1)} %broadcast_in_dim.2), calls=%async_computation | async-start | bytes 524288 | tf_op jit(solution)/shard_map/all_to_all | solution.py:110
  38.6 0.0 collective-permute-done.5.got_ref.gotd_ref.tail_ref
  38.6 0.0 copy-start
  38.6 1.0 copy-done
  39.6 4.7 %grad_partial.1 = bf16[32,128,128]{2,1,0:T(8,128)(2,1)} custom-call(s32[1]{0:T(128)} %bitcast.1.xpos_ref, bf16[128,4096]{1,0:T(8,128)(2,1)} %get-tuple-element.4.own_ref, bf16[128,4352]{1,0:T(8,128)(2,1)} %copy-done, bf16[128,4352]{1,0:T(8,128)(2,1)} %copy-done, bf16[128,4352]{1,0:T(8,128)(2,1)} %copy-done, bf16[128,128]{1,0:T(8,128)(2,1)} %bitcast.23, ...), custom_call_target="tpu_custom_call" | custom-call | tf_op jit(solution)/shard_map/grad_partial/pallas_call | solution.py:145
  44.2 3.1 %all-to-all-done = bf16[8,2,64,128]{3,2,1,0:T(8,128)(2,1)S(1)} async-done(((bf16[8,2,64,128]{3,2,1,0:T(8,128)(2,1)}), bf16[8,2,64,128]{3,2,1,0:T(8,128)(2,1)S(1)}, u32[]{:S(2)}, u32[]{:S(2)}) %all-to-all-start) | async-done | bytes 262176 | tf_op jit(solution)/shard_map/all_to_all | solution.py:110
  47.4 7.3 %all-to-all-start.1 = ((bf16[32,128,128]{2,1,0:T(8,128)(2,1)}), bf16[32,128,128]{2,1,0:T(8,128)(2,1)S(1)}, u32[]{:S(2)}, u32[]{:S(2)}) async-start(bf16[32,128,128]{2,1,0:T(8,128)(2,1)} %grad_partial.1), calls=%async_computation.1 | async-start | bytes 2097152 | tf_op jit(solution)/shard_map/all_to_all | solution.py:166
  54.7 0.0 copy-start.1
  54.7 3.5 %collective-permute-start.2 = (bf16[8,2,64,128]{3,2,1,0:T(8,128)(2,1)S(1)}, bf16[8,2,64,128]{3,2,1,0:T(8,128)(2,1)S(1)}, u32[]{:S(2)}, u32[]{:S(2)}) collective-permute-start(bf16[8,2,64,128]{3,2,1,0:T(8,128)(2,1)S(1)} %all-to-all-done), channel_id=1, source_target_pairs={{0,192},{192,384},{384,576},{576,0},{1,193},{193,385},{385,577},{5... | collective-permute-start | bytes 786440 | tf_op jit(solution)/shard_map/ppermute | solution.py:113
  58.2 3.1 %collective-permute-start.3 = (bf16[8,2,64,128]{3,2,1,0:T(8,128)(2,1)S(1)}, bf16[8,2,64,128]{3,2,1,0:T(8,128)(2,1)S(1)}, u32[]{:S(2)}, u32[]{:S(2)}) collective-permute-start(bf16[8,2,64,128]{3,2,1,0:T(8,128)(2,1)S(1)} %all-to-all-done), channel_id=1, source_target_pairs={{0,384},{192,576},{384,0},{576,192},{1,385},{193,577},{385,1},{577... | collective-permute-start | bytes 786440 | tf_op jit(solution)/shard_map/ppermute | solution.py:113
  61.3 4.0 %collective-permute-start.4 = (bf16[8,2,64,128]{3,2,1,0:T(8,128)(2,1)S(1)}, bf16[8,2,64,128]{3,2,1,0:T(8,128)(2,1)S(1)}, u32[]{:S(2)}, u32[]{:S(2)}) collective-permute-start(bf16[8,2,64,128]{3,2,1,0:T(8,128)(2,1)S(1)} %all-to-all-done), channel_id=1, source_target_pairs={{0,576},{192,0},{384,192},{576,384},{1,577},{193,1},{385,193},{577... | collective-permute-start | bytes 786440 | tf_op jit(solution)/shard_map/ppermute | solution.py:113
  65.3 6.3 %collective-permute-done.2 = bf16[8,2,64,128]{3,2,1,0:T(8,128)(2,1)S(1)} collective-permute-done((bf16[8,2,64,128]{3,2,1,0:T(8,128)(2,1)S(1)}, bf16[8,2,64,128]{3,2,1,0:T(8,128)(2,1)S(1)}, u32[]{:S(2)}, u32[]{:S(2)}) %collective-permute-start.2) | collective-permute-done | bytes 262176 | tf_op jit(solution)/shard_map/ppermute | solution.py:113
  71.7 5.5 %collective-permute-done.3 = bf16[8,2,64,128]{3,2,1,0:T(8,128)(2,1)S(1)} collective-permute-done((bf16[8,2,64,128]{3,2,1,0:T(8,128)(2,1)S(1)}, bf16[8,2,64,128]{3,2,1,0:T(8,128)(2,1)S(1)}, u32[]{:S(2)}, u32[]{:S(2)}) %collective-permute-start.3) | collective-permute-done | bytes 262176 | tf_op jit(solution)/shard_map/ppermute | solution.py:113
  77.2 4.8 %collective-permute-done.4 = bf16[8,2,64,128]{3,2,1,0:T(8,128)(2,1)S(1)} collective-permute-done((bf16[8,2,64,128]{3,2,1,0:T(8,128)(2,1)S(1)}, bf16[8,2,64,128]{3,2,1,0:T(8,128)(2,1)S(1)}, u32[]{:S(2)}, u32[]{:S(2)}) %collective-permute-start.4) | collective-permute-done | bytes 262176 | tf_op jit(solution)/shard_map/ppermute | solution.py:113
  82.0 0.1 pad_maximum_fusion
  82.1 0.0 copy-start.4
  82.1 0.0 copy-start.2
  82.1 0.0 copy-done.1
  82.1 0.4 fusion
  82.6 1.9 %collective-permute-start.6 = (f32[128,128]{1,0:T(8,128)S(1)}, f32[128,128]{1,0:T(8,128)S(1)}, u32[]{:S(2)}, u32[]{:S(2)}) collective-permute-start(f32[128,128]{1,0:T(8,128)S(1)} %fusion), channel_id=1, source_target_pairs={{0,6},{6,0},{1,7},{7,1},{2,8},{8,2},{3,9},{9,3},{4,10},{10,4},{5,1... | collective-permute-start | bytes 196616 | tf_op jit(solution)/shard_map/ppermute | solution.py:172
  84.5 0.0 copy-done.4
  84.5 0.1 fusion.2
  84.6 1.1 %collective-permute-done.6 = f32[128,128]{1,0:T(8,128)S(1)} collective-permute-done((f32[128,128]{1,0:T(8,128)S(1)}, f32[128,128]{1,0:T(8,128)S(1)}, u32[]{:S(2)}, u32[]{:S(2)}) %collective-permute-start.6) | collective-permute-done | bytes 65568 | tf_op jit(solution)/shard_map/ppermute | solution.py:172
  85.7 0.0 copy-done.2
  85.7 0.4 convolution_add_fusion
  86.2 0.0 all-to-all-done.1
  86.2 0.2 convert_reduce_fusion
  86.3 0.1 slice_select_fusion
  86.4 9.9 %collective-permute-start.7 = (f32[64,128]{0,1:T(8,128)S(1)}, f32[64,128]{0,1:T(8,128)S(1)}, u32[]{:S(2)}, u32[]{:S(2)}) collective-permute-start(f32[64,128]{0,1:T(8,128)S(1)} %slice_select_fusion), channel_id=1, source_target_pairs={{0,96},{96,0},{1,97},{97,1},{2,98},{98,2},{3,99},{99,3},{4,100},{1... | collective-permute-start | bytes 98312 | tf_op jit(solution)/shard_map/ppermute | solution.py:168
  96.3 0.7 multiply_convert_fusion
  97.0 3.2 %collective-permute-done.7 = f32[64,128]{0,1:T(8,128)S(1)} collective-permute-done((f32[64,128]{0,1:T(8,128)S(1)}, f32[64,128]{0,1:T(8,128)S(1)}, u32[]{:S(2)}, u32[]{:S(2)}) %collective-permute-start.7) | collective-permute-done | bytes 32800 | tf_op jit(solution)/shard_map/ppermute | solution.py:168
  100.2 0.1 add_convert_fusion
  100.3 0.7 copy.8
  (1 shorter events, 0.0 us)
Async XLA Ops:
  0.6 12.9 %copy-start.3 = (bf16[64,128]{1,0:T(8,128)(2,1)S(1)}, bf16[64,128]{1,0:T(8,128)(2,1)}, u32[]{:S(2)}) copy-start(bf16[64,128]{1,0:T(8,128)(2,1)} %param.8) | copy-start | bytes 49156
  0.6 5.6 %collective-permute-start = (bf16[4]{0:T(256)(128)(2,1)}, bf16[4]{0:T(256)(128)(2,1)S(1)}, u32[]{:S(2)}, u32[]{:S(2)}) collective-permute-start(bf16[4]{0:T(256)(128)(2,1)} %param.10), channel_id=1, source_target_pairs={{0,12},{12,0},{24,36},{36,24},{48,60},{60,48},{72,84},{84,72},{1,1... | collective-permute-start | bytes 32 | tf_op jit(solution)/shard_map/ppermute | solution.py:106
  6.2 0.6 copy-start.5
  11.6 27.0 %collective-permute-start.5 = (bf16[128,4352]{1,0:T(8,128)(2,1)}, bf16[128,4352]{1,0:T(8,128)(2,1)S(1)}, u32[]{:S(2)}, u32[]{:S(2)}) collective-permute-start(bf16[128,4352]{1,0:T(8,128)(2,1)} %get-tuple-element.5), channel_id=1, source_target_pairs={{0,6},{6,0},{1,7},{7,1},{2,8},{8,2},{3,9},{9,3},{4,10},{10,4},{5,1... | collective-permute-start | bytes 3342344 | tf_op jit(solution)/shard_map/ppermute | solution.py:144
  13.5 16.9 %collective-permute-start.1 = (bf16[64,128]{1,0:T(8,128)(2,1)S(1)}, bf16[64,128]{1,0:T(8,128)(2,1)S(1)}, u32[]{:S(2)}, u32[]{:S(2)}) collective-permute-start(bf16[64,128]{1,0:T(8,128)(2,1)S(1)} %copy-done.3), channel_id=1, source_target_pairs={{0,96},{96,0},{1,97},{97,1},{2,98},{98,2},{3,99},{99,3},{4,100},{1... | collective-permute-start | bytes 49160 | tf_op jit(solution)/shard_map/ppermute | solution.py:107
  31.1 16.2 %all-to-all-start = ((bf16[8,2,64,128]{3,2,1,0:T(8,128)(2,1)}), bf16[8,2,64,128]{3,2,1,0:T(8,128)(2,1)S(1)}, u32[]{:S(2)}, u32[]{:S(2)}) async-start(bf16[8,2,64,128]{3,2,1,0:T(8,128)(2,1)} %broadcast_in_dim.2), calls=%async_computation | async-start | bytes 524288 | tf_op jit(solution)/shard_map/all_to_all | solution.py:110
  38.6 1.0 %copy-start = (bf16[128,4352]{1,0:T(8,128)(2,1)}, bf16[128,4352]{1,0:T(8,128)(2,1)S(1)}, u32[]{:S(2)}) copy-start(bf16[128,4352]{1,0:T(8,128)(2,1)S(1)} %collective-permute-done.5.got_ref.gotd_ref.tail_ref) | copy-start | bytes 3342340
  47.4 38.8 %all-to-all-start.1 = ((bf16[32,128,128]{2,1,0:T(8,128)(2,1)}), bf16[32,128,128]{2,1,0:T(8,128)(2,1)S(1)}, u32[]{:S(2)}, u32[]{:S(2)}) async-start(bf16[32,128,128]{2,1,0:T(8,128)(2,1)} %grad_partial.1), calls=%async_computation.1 | async-start | bytes 2097152 | tf_op jit(solution)/shard_map/all_to_all | solution.py:166
  54.7 27.5 %copy-start.1 = (bf16[128,4352]{1,0:T(8,128)(2,1)S(1)}, bf16[128,4352]{1,0:T(8,128)(2,1)}, u32[]{:S(2)}) copy-start(bf16[128,4352]{1,0:T(8,128)(2,1)} %copy-done) | copy-start | bytes 3342340
  54.7 17.0 %collective-permute-start.2 = (bf16[8,2,64,128]{3,2,1,0:T(8,128)(2,1)S(1)}, bf16[8,2,64,128]{3,2,1,0:T(8,128)(2,1)S(1)}, u32[]{:S(2)}, u32[]{:S(2)}) collective-permute-start(bf16[8,2,64,128]{3,2,1,0:T(8,128)(2,1)S(1)} %all-to-all-done), channel_id=1, source_target_pairs={{0,192},{192,384},{384,576},{576,0},{1,193},{193,385},{385,577},{5... | collective-permute-start | bytes 786440 | tf_op jit(solution)/shard_map/ppermute | solution.py:113
  58.2 19.0 %collective-permute-start.3 = (bf16[8,2,64,128]{3,2,1,0:T(8,128)(2,1)S(1)}, bf16[8,2,64,128]{3,2,1,0:T(8,128)(2,1)S(1)}, u32[]{:S(2)}, u32[]{:S(2)}) collective-permute-start(bf16[8,2,64,128]{3,2,1,0:T(8,128)(2,1)S(1)} %all-to-all-done), channel_id=1, source_target_pairs={{0,384},{192,576},{384,0},{576,192},{1,385},{193,577},{385,1},{577... | collective-permute-start | bytes 786440 | tf_op jit(solution)/shard_map/ppermute | solution.py:113
  61.3 20.7 %collective-permute-start.4 = (bf16[8,2,64,128]{3,2,1,0:T(8,128)(2,1)S(1)}, bf16[8,2,64,128]{3,2,1,0:T(8,128)(2,1)S(1)}, u32[]{:S(2)}, u32[]{:S(2)}) collective-permute-start(bf16[8,2,64,128]{3,2,1,0:T(8,128)(2,1)S(1)} %all-to-all-done), channel_id=1, source_target_pairs={{0,576},{192,0},{384,192},{576,384},{1,577},{193,1},{385,193},{577... | collective-permute-start | bytes 786440 | tf_op jit(solution)/shard_map/ppermute | solution.py:113
  82.1 2.4 %copy-start.4 = (s32[1,4]{1,0:T(1,128)S(1)}, s32[1,4]{1,0:T(1,128)}, u32[]{:S(2)}) copy-start(s32[1,4]{1,0:T(1,128)} %len_ref.3) | copy-start | bytes 52
  82.1 3.6 %copy-start.2 = (bf16[128,4096]{1,0:T(8,128)(2,1)S(1)}, bf16[128,4096]{1,0:T(8,128)(2,1)}, u32[]{:S(2)}) copy-start(bf16[128,4096]{1,0:T(8,128)(2,1)} %get-tuple-element.4.own_ref) | copy-start | bytes 3145732
  82.6 3.1 %collective-permute-start.6 = (f32[128,128]{1,0:T(8,128)S(1)}, f32[128,128]{1,0:T(8,128)S(1)}, u32[]{:S(2)}, u32[]{:S(2)}) collective-permute-start(f32[128,128]{1,0:T(8,128)S(1)} %fusion), channel_id=1, source_target_pairs={{0,6},{6,0},{1,7},{7,1},{2,8},{8,2},{3,9},{9,3},{4,10},{10,4},{5,1... | collective-permute-start | bytes 196616 | tf_op jit(solution)/shard_map/ppermute | solution.py:172
  86.4 13.8 %collective-permute-start.7 = (f32[64,128]{0,1:T(8,128)S(1)}, f32[64,128]{0,1:T(8,128)S(1)}, u32[]{:S(2)}, u32[]{:S(2)}) collective-permute-start(f32[64,128]{0,1:T(8,128)S(1)} %slice_select_fusion), channel_id=1, source_target_pairs={{0,96},{96,0},{1,97},{97,1},{2,98},{98,2},{3,99},{99,3},{4,100},{1... | collective-permute-start | bytes 98312 | tf_op jit(solution)/shard_map/ppermute | solution.py:168

commit v3 on v2

--- a/solution.py
+++ b/solution.py
@@ -104,13 +104,13 @@
     whole = lambda *shape: pl.BlockSpec(shape, lambda *_: (0,) * len(shape))
 
     near = lax.ppermute(rewards, "y", Y_PAIR)
-    w_far = lax.ppermute(w_value, "zh", SWAP_Z)
+    w_y = lax.all_to_all(jnp.broadcast_to(w_value[None], (ny, BLOCK, cols)), "y", 0, 0, tiled=True)
+    w_far = lax.ppermute(w_y, "zh", SWAP_Z)
     zpart = lax.axis_index("zh")
-    w_pair = jnp.where(zpart == 0, jnp.stack([w_value, w_far]), jnp.stack([w_far, w_value]))
-    w_y = lax.all_to_all(jnp.broadcast_to(w_pair[None], (ny, nz, BLOCK, cols)), "y", 0, 0, tiled=True)
-    w_parts = [w_y]
+    w_pair = jnp.where(zpart == 0, jnp.stack([w_y, w_far], axis=1), jnp.stack([w_far, w_y], axis=1))
+    w_parts = [w_pair]
     for s in range(1, nx):
-        w_parts.append(lax.ppermute(w_y, "x", X_SHIFTS[s]))
+        w_parts.append(lax.ppermute(w_pair, "x", X_SHIFTS[s]))
     w_full = jnp.concatenate(w_parts).reshape(half, cols)
 
     core = lax.axis_index("c").astype(jnp.int32).reshape(1)

time: 102 us -> 97.9 us (0.960)
  the two profiles are of different devices: /device:TPU:18 before, /device:TPU:72 now
where the time goes in v3:
time: 97.9 us; the launch traced here: 97.2 us
  starting transfers between devices  56.6 us (58%)
  waiting for transfers between devices  25.2 us (26%)
  Pallas kernels  9.41 us (10%)
  local copies, waits for them, and re-layouts  2.96 us (3%)
  other arithmetic  1.24 us (1%)
    ppermute x1, starting transfers between devices, per_device(): w_far = lax.ppermute(w_y, 'zh', SWAP_Z)  14.2 us
    ppermute x3, starting transfers between devices, per_device(): w_parts.append(lax.ppermute(w_pair, 'x', X_SHIFTS[s]))  11.5 us
    ppermute x1, starting transfers between devices, per_device(): g_z = lax.ppermute(jnp.where(zpart == 0, g_sum[1], g_sum[0]), 'zh', SWAP_Z)  9.79 us
    ppermute x1, waiting for transfers between devices, per_device(): w_far = lax.ppermute(w_y, 'zh', SWAP_Z)  8.63 us
    all_to_all x1, starting transfers between devices, per_device(): lax.all_to_all(jnp.broadcast_to(w_value[None], (ny, BLOCK, cols)), 'y', 0...  7.55 us
    all_to_all x1, starting transfers between devices, per_device(): g_xy = lax.all_to_all(send, ('x', 'y'), 0, 0, tiled=True)  7.36 us
    ppermute x3, waiting for transfers between devices, per_device(): w_parts.append(lax.ppermute(w_pair, 'x', X_SHIFTS[s]))  4.92 us
    ppermute x1, waiting for transfers between devices, per_device(): g_z = lax.ppermute(jnp.where(zpart == 0, g_sum[1], g_sum[0]), 'zh', SWAP_Z)  4.82 us
  transfers between devices with their start and end apart: 10, of which 7 were waited for; matrix products, arithmetic and copies ran while one was open for 3% of the time, Pallas kernels for 5%

profile of v3, /device:TPU:72, one launch (start us, length us, event | category | flops | bytes accessed | tf_op | source)
XLA Modules:
  0.0 97.2 jit_solution(15577599168430822357)
XLA Ops:
  0.6 0.0 copy-start.3
  0.6 2.4 %collective-permute-start = (bf16[4]{0:T(256)(128)(2,1)}, bf16[4]{0:T(256)(128)(2,1)S(1)}, u32[]{:S(2)}, u32[]{:S(2)}) collective-permute-start(bf16[4]{0:T(256)(128)(2,1)} %param.10), channel_id=1, source_target_pairs={{0,12},{12,0},{24,36},{36,24},{48,60},{60,48},{72,84},{84,72},{1,1... | collective-permute-start | bytes 32 | tf_op jit(solution)/shard_map/ppermute | solution.py:106
  3.0 3.2 %collective-permute-done = bf16[4]{0:T(256)(128)(2,1)S(1)} collective-permute-done((bf16[4]{0:T(256)(128)(2,1)}, bf16[4]{0:T(256)(128)(2,1)S(1)}, u32[]{:S(2)}, u32[]{:S(2)}) %collective-permute-start) | collective-permute-done | bytes 40 | tf_op jit(solution)/shard_map/ppermute | solution.py:106
  6.2 0.0 copy-start.5
  6.2 0.6 copy-done.5
  6.8 4.8 %norm_split.1 = (bf16[128,4096]{1,0:T(8,128)(2,1)}, bf16[128,4352]{1,0:T(8,128)(2,1)}) custom-call(s32[1]{0:T(128)} %bitcast.core_ref, s32[1]{0:T(128)} %bitcast.1.xpos_ref, bf16[128,8192]{1,0:T(8,128)(2,1)} %bitcast.18, f32[1,8192]{1,0:T(1,128)} %bitcast.26, bf16[128,128]{1,0:T(8,128)(2,1)} %bitcast.23, bf16[1,4]{1,0:T(2,128)(2,1)} %bitcast.28, ...), custom_call_target="tpu_custom_call" | custom-call | tf_op jit(solution)/shard_map/norm_split/pallas_call | solution.py:121
  11.6 1.9 %collective-permute-start.5 = (bf16[128,4352]{1,0:T(8,128)(2,1)}, bf16[128,4352]{1,0:T(8,128)(2,1)S(1)}, u32[]{:S(2)}, u32[]{:S(2)}) collective-permute-start(bf16[128,4352]{1,0:T(8,128)(2,1)} %get-tuple-element.5), channel_id=1, source_target_pairs={{0,6},{6,0},{1,7},{7,1},{2,8},{8,2},{3,9},{9,3},{4,10},{10,4},{5,1... | collective-permute-start | bytes 3342344 | tf_op jit(solution)/shard_map/ppermute | solution.py:144
  13.5 0.0 copy-done.3
  13.5 0.7 broadcast_in_dim.2
  14.2 7.5 %all-to-all-start = ((bf16[8,64,128]{2,1,0:T(8,128)(2,1)}), bf16[8,64,128]{2,1,0:T(8,128)(2,1)S(1)}, u32[]{:S(2)}, u32[]{:S(2)}) async-start(bf16[8,64,128]{2,1,0:T(8,128)(2,1)} %broadcast_in_dim.2), calls=%async_computation | async-start | bytes 262144 | tf_op jit(solution)/shard_map/all_to_all | solution.py:107
  21.7 0.0 collective-permute-done.5.got_ref.gotd_ref.tail_ref
  21.7 0.0 copy-start
  21.7 1.0 %copy-done = bf16[128,4352]{1,0:T(8,128)(2,1)} copy-done((bf16[128,4352]{1,0:T(8,128)(2,1)}, bf16[128,4352]{1,0:T(8,128)(2,1)S(1)}, u32[]{:S(2)}) %copy-start) | copy-done | bytes 1114136
  22.7 4.6 %grad_partial.1 = bf16[32,128,128]{2,1,0:T(8,128)(2,1)} custom-call(s32[1]{0:T(128)} %bitcast.1.xpos_ref, bf16[128,4096]{1,0:T(8,128)(2,1)} %get-tuple-element.4.own_ref, bf16[128,4352]{1,0:T(8,128)(2,1)} %copy-done, bf16[128,4352]{1,0:T(8,128)(2,1)} %copy-done, bf16[128,4352]{1,0:T(8,128)(2,1)} %copy-done, bf16[128,128]{1,0:T(8,128)(2,1)} %bitcast.24, ...), custom_call_target="tpu_custom_call" | custom-call | tf_op jit(solution)/shard_map/grad_partial/pallas_call | solution.py:145
  27.4 2.5 %all-to-all-done = bf16[8,64,128]{2,1,0:T(8,128)(2,1)S(1)} async-done(((bf16[8,64,128]{2,1,0:T(8,128)(2,1)}), bf16[8,64,128]{2,1,0:T(8,128)(2,1)S(1)}, u32[]{:S(2)}, u32[]{:S(2)}) %all-to-all-start) | async-done | bytes 131104 | tf_op jit(solution)/shard_map/all_to_all | solution.py:107
  29.9 7.4 %all-to-all-start.1 = ((bf16[32,128,128]{2,1,0:T(8,128)(2,1)}), bf16[32,128,128]{2,1,0:T(8,128)(2,1)S(1)}, u32[]{:S(2)}, u32[]{:S(2)}) async-start(bf16[32,128,128]{2,1,0:T(8,128)(2,1)} %grad_partial.1), calls=%async_computation.1 | async-start | bytes 2097152 | tf_op jit(solution)/shard_map/all_to_all | solution.py:166
  37.3 14.2 %collective-permute-start.1 = (bf16[8,64,128]{2,1,0:T(8,128)(2,1)S(1)}, bf16[8,64,128]{2,1,0:T(8,128)(2,1)S(1)}, u32[]{:S(2)}, u32[]{:S(2)}) collective-permute-start(bf16[8,64,128]{2,1,0:T(8,128)(2,1)S(1)} %all-to-all-done), channel_id=1, source_target_pairs={{0,96},{96,0},{1,97},{97,1},{2,98},{98,2},{3,99},{99,3},{4,100},{1... | collective-permute-start | bytes 393224 | tf_op jit(solution)/shard_map/ppermute | solution.py:108
  51.5 8.6 %collective-permute-done.1 = bf16[8,64,128]{2,1,0:T(8,128)(2,1)S(1)} collective-permute-done((bf16[8,64,128]{2,1,0:T(8,128)(2,1)S(1)}, bf16[8,64,128]{2,1,0:T(8,128)(2,1)S(1)}, u32[]{:S(2)}, u32[]{:S(2)}) %collective-permute-start.1) | collective-permute-done | bytes 131104 | tf_op jit(solution)/shard_map/ppermute | solution.py:108
  60.2 0.0 copy-start.1
  60.2 3.5 %collective-permute-start.2 = (bf16[8,2,64,128]{3,2,1,0:T(8,128)(2,1)S(1)}, bf16[8,2,64,128]{3,2,1,0:T(8,128)(2,1)S(1)}, u32[]{:S(2)}, u32[]{:S(2)}) collective-permute-start(bf16[8,2,64,128]{3,2,1,0:T(8,128)(2,1)S(1)} %maximum_select_fusion), channel_id=1, source_target_pairs={{0,192},{192,384},{384,576},{576,0},{1,193},{193,385},{385,577},{5... | collective-permute-start | bytes 786440 | tf_op jit(solution)/shard_map/ppermute | solution.py:113
  63.7 4.6 %collective-permute-start.3 = (bf16[8,2,64,128]{3,2,1,0:T(8,128)(2,1)S(1)}, bf16[8,2,64,128]{3,2,1,0:T(8,128)(2,1)S(1)}, u32[]{:S(2)}, u32[]{:S(2)}) collective-permute-start(bf16[8,2,64,128]{3,2,1,0:T(8,128)(2,1)S(1)} %maximum_select_fusion), channel_id=1, source_target_pairs={{0,384},{192,576},{384,0},{576,192},{1,385},{193,577},{385,1},{577... | collective-permute-start | bytes 786440 | tf_op jit(solution)/shard_map/ppermute | solution.py:113
  68.3 3.3 %collective-permute-start.4 = (bf16[8,2,64,128]{3,2,1,0:T(8,128)(2,1)S(1)}, bf16[8,2,64,128]{3,2,1,0:T(8,128)(2,1)S(1)}, u32[]{:S(2)}, u32[]{:S(2)}) collective-permute-start(bf16[8,2,64,128]{3,2,1,0:T(8,128)(2,1)S(1)} %maximum_select_fusion), channel_id=1, source_target_pairs={{0,576},{192,0},{384,192},{576,384},{1,577},{193,1},{385,193},{577... | collective-permute-start | bytes 786440 | tf_op jit(solution)/shard_map/ppermute | solution.py:113
  71.7 0.0 collective-permute-done.2
  71.7 1.9 %collective-permute-done.3 = bf16[8,2,64,128]{3,2,1,0:T(8,128)(2,1)S(1)} collective-permute-done((bf16[8,2,64,128]{3,2,1,0:T(8,128)(2,1)S(1)}, bf16[8,2,64,128]{3,2,1,0:T(8,128)(2,1)S(1)}, u32[]{:S(2)}, u32[]{:S(2)}) %collective-permute-start.3) | collective-permute-done | bytes 262176 | tf_op jit(solution)/shard_map/ppermute | solution.py:113
  73.5 3.0 %collective-permute-done.4 = bf16[8,2,64,128]{3,2,1,0:T(8,128)(2,1)S(1)} collective-permute-done((bf16[8,2,64,128]{3,2,1,0:T(8,128)(2,1)S(1)}, bf16[8,2,64,128]{3,2,1,0:T(8,128)(2,1)S(1)}, u32[]{:S(2)}, u32[]{:S(2)}) %collective-permute-start.4) | collective-permute-done | bytes 262176 | tf_op jit(solution)/shard_map/ppermute | solution.py:113
  76.6 0.1 pad_maximum_fusion
  76.7 0.0 copy-start.4
  76.7 0.0 copy-start.2
  76.8 0.0 copy-done.1
  76.8 0.4 fusion
  77.2 1.9 %collective-permute-start.6 = (f32[128,128]{1,0:T(8,128)S(1)}, f32[128,128]{1,0:T(8,128)S(1)}, u32[]{:S(2)}, u32[]{:S(2)}) collective-permute-start(f32[128,128]{1,0:T(8,128)S(1)} %fusion), channel_id=1, source_target_pairs={{0,6},{6,0},{1,7},{7,1},{2,8},{8,2},{3,9},{9,3},{4,10},{10,4},{5,1... | collective-permute-start | bytes 196616 | tf_op jit(solution)/shard_map/ppermute | solution.py:172
  79.1 0.0 copy-done.4
  79.1 0.1 fusion.2
  79.2 1.1 %collective-permute-done.6 = f32[128,128]{1,0:T(8,128)S(1)} collective-permute-done((f32[128,128]{1,0:T(8,128)S(1)}, f32[128,128]{1,0:T(8,128)S(1)}, u32[]{:S(2)}, u32[]{:S(2)}) %collective-permute-start.6) | collective-permute-done | bytes 65568 | tf_op jit(solution)/shard_map/ppermute | solution.py:172
  80.3 0.0 copy-done.2
  80.3 0.4 convolution_add_fusion
  80.8 0.0 all-to-all-done.1
  80.8 0.2 convert_reduce_fusion
  81.0 0.1 slice_select_fusion
  81.0 9.8 %collective-permute-start.7 = (f32[64,128]{0,1:T(8,128)S(1)}, f32[64,128]{0,1:T(8,128)S(1)}, u32[]{:S(2)}, u32[]{:S(2)}) collective-permute-start(f32[64,128]{0,1:T(8,128)S(1)} %slice_select_fusion), channel_id=1, source_target_pairs={{0,96},{96,0},{1,97},{97,1},{2,98},{98,2},{3,99},{99,3},{4,100},{1... | collective-permute-start | bytes 98312 | tf_op jit(solution)/shard_map/ppermute | solution.py:168
  90.8 0.7 multiply_convert_fusion
  91.5 4.8 %collective-permute-done.7 = f32[64,128]{0,1:T(8,128)S(1)} collective-permute-done((f32[64,128]{0,1:T(8,128)S(1)}, f32[64,128]{0,1:T(8,128)S(1)}, u32[]{:S(2)}, u32[]{:S(2)}) %collective-permute-start.7) | collective-permute-done | bytes 32800 | tf_op jit(solution)/shard_map/ppermute | solution.py:168
  96.4 0.1 add_convert_fusion
  96.5 0.7 copy.8
  (1 shorter events, 0.0 us)
Async XLA Ops:
  0.6 12.9 %copy-start.3 = (bf16[64,128]{1,0:T(8,128)(2,1)S(1)}, bf16[64,128]{1,0:T(8,128)(2,1)}, u32[]{:S(2)}) copy-start(bf16[64,128]{1,0:T(8,128)(2,1)} %param.8) | copy-start | bytes 49156
  0.6 5.6 %collective-permute-start = (bf16[4]{0:T(256)(128)(2,1)}, bf16[4]{0:T(256)(128)(2,1)S(1)}, u32[]{:S(2)}, u32[]{:S(2)}) collective-permute-start(bf16[4]{0:T(256)(128)(2,1)} %param.10), channel_id=1, source_target_pairs={{0,12},{12,0},{24,36},{36,24},{48,60},{60,48},{72,84},{84,72},{1,1... | collective-permute-start | bytes 32 | tf_op jit(solution)/shard_map/ppermute | solution.py:106
  6.2 0.6 copy-start.5
  11.6 10.1 %collective-permute-start.5 = (bf16[128,4352]{1,0:T(8,128)(2,1)}, bf16[128,4352]{1,0:T(8,128)(2,1)S(1)}, u32[]{:S(2)}, u32[]{:S(2)}) collective-permute-start(bf16[128,4352]{1,0:T(8,128)(2,1)} %get-tuple-element.5), channel_id=1, source_target_pairs={{0,6},{6,0},{1,7},{7,1},{2,8},{8,2},{3,9},{9,3},{4,10},{10,4},{5,1... | collective-permute-start | bytes 3342344 | tf_op jit(solution)/shard_map/ppermute | solution.py:144
  14.2 15.7 %all-to-all-start = ((bf16[8,64,128]{2,1,0:T(8,128)(2,1)}), bf16[8,64,128]{2,1,0:T(8,128)(2,1)S(1)}, u32[]{:S(2)}, u32[]{:S(2)}) async-start(bf16[8,64,128]{2,1,0:T(8,128)(2,1)} %broadcast_in_dim.2), calls=%async_computation | async-start | bytes 262144 | tf_op jit(solution)/shard_map/all_to_all | solution.py:107
  21.7 1.0 %copy-start = (bf16[128,4352]{1,0:T(8,128)(2,1)}, bf16[128,4352]{1,0:T(8,128)(2,1)S(1)}, u32[]{:S(2)}) copy-start(bf16[128,4352]{1,0:T(8,128)(2,1)S(1)} %collective-permute-done.5.got_ref.gotd_ref.tail_ref) | copy-start | bytes 3342340
  29.9 50.9 %all-to-all-start.1 = ((bf16[32,128,128]{2,1,0:T(8,128)(2,1)}), bf16[32,128,128]{2,1,0:T(8,128)(2,1)S(1)}, u32[]{:S(2)}, u32[]{:S(2)}) async-start(bf16[32,128,128]{2,1,0:T(8,128)(2,1)} %grad_partial.1), calls=%async_computation.1 | async-start | bytes 2097152 | tf_op jit(solution)/shard_map/all_to_all | solution.py:166
  37.3 22.9 %collective-permute-start.1 = (bf16[8,64,128]{2,1,0:T(8,128)(2,1)S(1)}, bf16[8,64,128]{2,1,0:T(8,128)(2,1)S(1)}, u32[]{:S(2)}, u32[]{:S(2)}) collective-permute-start(bf16[8,64,128]{2,1,0:T(8,128)(2,1)S(1)} %all-to-all-done), channel_id=1, source_target_pairs={{0,96},{96,0},{1,97},{97,1},{2,98},{98,2},{3,99},{99,3},{4,100},{1... | collective-permute-start | bytes 393224 | tf_op jit(solution)/shard_map/ppermute | solution.py:108
  60.2 16.6 %copy-start.1 = (bf16[128,4352]{1,0:T(8,128)(2,1)S(1)}, bf16[128,4352]{1,0:T(8,128)(2,1)}, u32[]{:S(2)}) copy-start(bf16[128,4352]{1,0:T(8,128)(2,1)} %copy-done) | copy-start | bytes 3342340
  60.2 11.5 %collective-permute-start.2 = (bf16[8,2,64,128]{3,2,1,0:T(8,128)(2,1)S(1)}, bf16[8,2,64,128]{3,2,1,0:T(8,128)(2,1)S(1)}, u32[]{:S(2)}, u32[]{:S(2)}) collective-permute-start(bf16[8,2,64,128]{3,2,1,0:T(8,128)(2,1)S(1)} %maximum_select_fusion), channel_id=1, source_target_pairs={{0,192},{192,384},{384,576},{576,0},{1,193},{193,385},{385,577},{5... | collective-permute-start | bytes 786440 | tf_op jit(solution)/shard_map/ppermute | solution.py:113
  63.7 9.9 %collective-permute-start.3 = (bf16[8,2,64,128]{3,2,1,0:T(8,128)(2,1)S(1)}, bf16[8,2,64,128]{3,2,1,0:T(8,128)(2,1)S(1)}, u32[]{:S(2)}, u32[]{:S(2)}) collective-permute-start(bf16[8,2,64,128]{3,2,1,0:T(8,128)(2,1)S(1)} %maximum_select_fusion), channel_id=1, source_target_pairs={{0,384},{192,576},{384,0},{576,192},{1,385},{193,577},{385,1},{577... | collective-permute-start | bytes 786440 | tf_op jit(solution)/shard_map/ppermute | solution.py:113
  68.3 8.3 %collective-permute-start.4 = (bf16[8,2,64,128]{3,2,1,0:T(8,128)(2,1)S(1)}, bf16[8,2,64,128]{3,2,1,0:T(8,128)(2,1)S(1)}, u32[]{:S(2)}, u32[]{:S(2)}) collective-permute-start(bf16[8,2,64,128]{3,2,1,0:T(8,128)(2,1)S(1)} %maximum_select_fusion), channel_id=1, source_target_pairs={{0,576},{192,0},{384,192},{576,384},{1,577},{193,1},{385,193},{577... | collective-permute-start | bytes 786440 | tf_op jit(solution)/shard_map/ppermute | solution.py:113
  76.7 2.4 %copy-start.4 = (s32[1,4]{1,0:T(1,128)S(1)}, s32[1,4]{1,0:T(1,128)}, u32[]{:S(2)}) copy-start(s32[1,4]{1,0:T(1,128)} %len_ref.3) | copy-start | bytes 52
  76.7 3.6 %copy-start.2 = (bf16[128,4096]{1,0:T(8,128)(2,1)S(1)}, bf16[128,4096]{1,0:T(8,128)(2,1)}, u32[]{:S(2)}) copy-start(bf16[128,4096]{1,0:T(8,128)(2,1)} %get-tuple-element.4.own_ref) | copy-start | bytes 3145732
  77.2 3.1 %collective-permute-start.6 = (f32[128,128]{1,0:T(8,128)S(1)}, f32[128,128]{1,0:T(8,128)S(1)}, u32[]{:S(2)}, u32[]{:S(2)}) collective-permute-start(f32[128,128]{1,0:T(8,128)S(1)} %fusion), channel_id=1, source_target_pairs={{0,6},{6,0},{1,7},{7,1},{2,8},{8,2},{3,9},{9,3},{4,10},{10,4},{5,1... | collective-permute-start | bytes 196616 | tf_op jit(solution)/shard_map/ppermute | solution.py:172
  81.0 15.3 %collective-permute-start.7 = (f32[64,128]{0,1:T(8,128)S(1)}, f32[64,128]{0,1:T(8,128)S(1)}, u32[]{:S(2)}, u32[]{:S(2)}) collective-permute-start(f32[64,128]{0,1:T(8,128)S(1)} %slice_select_fusion), channel_id=1, source_target_pairs={{0,96},{96,0},{1,97},{97,1},{2,98},{98,2},{3,99},{99,3},{4,100},{1... | collective-permute-start | bytes 98312 | tf_op jit(solution)/shard_map/ppermute | solution.py:168

commit v4 on v3

--- a/solution.py
+++ b/solution.py
@@ -25,6 +25,7 @@
         total = total + v * v
     scale = lax.rsqrt(jnp.sum(total, axis=1, keepdims=True) * (1.0 / width) + 1e-5)
     first = core_ref[0] == 0
+    here = pl.ds(pl.multiple_of(pl.program_id(0) * rows, rows), rows)
     low = lax.broadcasted_iota(jnp.int32, (rows, LANES), 1) < BLOCK
     tiles = width // LANES // 2
     for k in range(tiles):
@@ -34,12 +35,13 @@
         at_a, at_b = pl.ds(pl.multiple_of(at, LANES), LANES), pl.ds(pl.multiple_of(next_z, LANES), LANES)
         a = x_ref[:, at_a].astype(f32) * scale * gain_ref[:, at_a]
         b = x_ref[:, at_b].astype(f32) * scale * gain_ref[:, at_b]
-        even = jnp.where(low, a, pltpu.roll(b, BLOCK, 1))
-        odd = jnp.where(low, pltpu.roll(a, BLOCK, 1), b)
-        own_ref[:, k * LANES : (k + 1) * LANES] = jnp.where(first, even, odd).astype(bf16)
-        pack_ref[:, k * LANES : (k + 1) * LANES] = jnp.where(first, odd, even).astype(bf16)
+        crossed = pltpu.roll(jnp.where(low, b, a), BLOCK, 1)
+        even = jnp.where(low, a, crossed)
+        odd = jnp.where(low, crossed, b)
+        own_ref[here, k * LANES : (k + 1) * LANES] = jnp.where(first, even, odd).astype(bf16)
+        pack_ref[here, k * LANES : (k + 1) * LANES] = jnp.where(first, odd, even).astype(bf16)
     half = width // 2
-    pack_ref[:, half : half + LANES] = dval_ref[...]
+    pack_ref[here, half : half + LANES] = dval_ref[...]
     lane = lax.broadcasted_iota(jnp.int32, (rows, LANES), 1)
     tail = jnp.zeros((rows, LANES), f32)
     n = rew_ref.shape[1]
@@ -47,11 +49,13 @@
         vals = ref[...].astype(f32)
         for j in range(n):
             tail = jnp.where(lane == s * n + j, vals[:, j : j + 1], tail)
-    pack_ref[:, half + LANES :] = tail.astype(bf16)
+    pack_ref[here, half + LANES :] = tail.astype(bf16)
 
 
-def grad_kernel(xpos_ref, own_ref, got_ref, gotd_ref, tail_ref, dval_ref, rew_ref, near_ref, len_ref, out_ref, ds_own, ds_other):
-    rows, _ = dval_ref.shape
+def grad_kernel(xpos_ref, own_ref, got_ref, dval_ref, rew_ref, near_ref, len_ref, out_ref, ds_own, ds_other):
+    rows, cols = dval_ref.shape
+    half = own_ref.shape[1]
+    chunk = half // NX
     n = rew_ref.shape[1]
     slots = rows // n
 
@@ -59,7 +63,7 @@
     def _():
         rew = rew_ref[...].astype(f32)
         near = near_ref[...].astype(f32)
-        tail = tail_ref[...].astype(f32)[0:1, :]
+        tail = got_ref[:16, half + cols :].astype(f32)[0:1, :]
         in_group = lax.broadcasted_iota(jnp.int32, (1, LANES), 1) < 2 * n
         count = 1.0 / (4 * n)
         total = jnp.sum(rew, axis=1, keepdims=True) + jnp.sum(near, axis=1, keepdims=True)
@@ -84,14 +88,18 @@
         lens = len_ref[...].astype(f32)
         own = factor(lambda j: rew[:, j : j + 1], lambda j: lens[:, j : j + 1])
         other = factor(lambda j: tail[:, j : j + 1], lambda j: tail[:, 2 * n + j : 2 * n + j + 1])
-        ds_own[...] = (dval_ref[...].astype(f32) * own).astype(bf16)
-        ds_other[...] = (gotd_ref[...].astype(f32) * other).astype(bf16)
+        ds_own[...] = (dval_ref[...].astype(f32) * own).T.astype(bf16)
+        ds_other[...] = (got_ref[:, half : half + cols].astype(f32) * other).T.astype(bf16)
 
-    over_rows = (((0,), (0,)), ((), ()))
-    acc = lax.dot_general(ds_own[...], own_ref[...], over_rows, preferred_element_type=f32)
-    acc = acc + lax.dot_general(ds_other[...], got_ref[...], over_rows, preferred_element_type=f32)
+    here = pl.ds(pl.multiple_of(pl.program_id(0) * chunk, chunk), chunk)
+    acc = jnp.dot(ds_own[...], own_ref[:, here], preferred_element_type=f32)
+    acc = acc + jnp.dot(ds_other[...], got_ref[:, here], preferred_element_type=f32)
     for j in range(out_ref.shape[0]):
         out_ref[j] = acc[:, j * LANES : (j + 1) * LANES].astype(bf16)
+
+
+def on_chip(array):
+    return pltpu.with_memory_space_constraint(array, pltpu.VMEM)
 
 
 def per_device(resid, norm_gain, w_value, d_value, rewards, lengths):
@@ -100,7 +108,6 @@
     cols = w_value.shape[1]
     nx, nz, ny, nc = [lax.axis_size(a) for a in DP]
     half = width // nc
-    chunk = half // nx
     whole = lambda *shape: pl.BlockSpec(shape, lambda *_: (0,) * len(shape))
 
     near = lax.ppermute(rewards, "y", Y_PAIR)
@@ -116,8 +123,8 @@
     core = lax.axis_index("c").astype(jnp.int32).reshape(1)
     xpos = lax.axis_index("x").astype(jnp.int32).reshape(1)
     dval = d_value.reshape(rows, cols)
-    rew, near = rewards.reshape(1, rolls), near.reshape(1, rolls)
-    step = 32
+    rew, near = rewards.reshape(1, rolls), on_chip(near.reshape(1, rolls))
+    step = 64
     own, packed = pl.pallas_call(
         norm_kernel,
         grid=(rows // step,),
@@ -128,41 +135,34 @@
             whole(1, width),
             pl.BlockSpec((step, cols), lambda i: (i, 0)),
             whole(1, rolls),
-            whole(1, rolls),
+            pl.BlockSpec(memory_space=pltpu.VMEM),
             whole(1, rolls),
         ],
-        out_specs=[
-            pl.BlockSpec((step, half), lambda i: (i, 0)),
-            pl.BlockSpec((step, half + 2 * LANES), lambda i: (i, 0)),
-        ],
-        out_shape=[
-            jax.ShapeDtypeStruct((rows, half), bf16),
-            jax.ShapeDtypeStruct((rows, half + 2 * LANES), bf16),
-        ],
+        out_specs=[pl.BlockSpec(memory_space=pltpu.VMEM), pl.BlockSpec(memory_space=pltpu.VMEM)],
+        out_shape=[pltpu.VMEM((rows, half), bf16), pltpu.VMEM((rows, half + 2 * LANES), bf16)],
         name="norm_split",
     )(core, xpos, resid.reshape(rows, width), norm_gain.reshape(1, width), dval, rew, near, lengths)
     got = lax.ppermute(packed, "c", SWAP)
+    got_in, own_in = on_chip(got), on_chip(own)
     send = pl.pallas_call(
         grad_kernel,
         grid_spec=pltpu.PrefetchScalarGridSpec(
             num_scalar_prefetch=1,
             grid=(nx,),
             in_specs=[
-                pl.BlockSpec((rows, chunk), lambda k, p: (0, k)),
-                pl.BlockSpec((rows, chunk), lambda k, p: (0, k)),
-                pl.BlockSpec((rows, cols), lambda k, p: (0, half // LANES)),
-                pl.BlockSpec((16, LANES), lambda k, p: (0, half // LANES + 1)),
+                pl.BlockSpec(memory_space=pltpu.VMEM),
+                pl.BlockSpec(memory_space=pltpu.VMEM),
                 whole(rows, cols),
                 whole(1, rolls),
-                whole(1, rolls),
+                pl.BlockSpec(memory_space=pltpu.VMEM),
                 whole(1, rolls),
             ],
             out_specs=pl.BlockSpec((ny, cols, nz * BLOCK), lambda k, p: ((p[0] + NX - k) % NX, 0, 0)),
-            scratch_shapes=[pltpu.VMEM((rows, cols), bf16), pltpu.VMEM((rows, cols), bf16)],
+            scratch_shapes=[pltpu.VMEM((cols, rows), bf16), pltpu.VMEM((cols, rows), bf16)],
         ),
         out_shape=jax.ShapeDtypeStruct((nx * ny, cols, nz * BLOCK), bf16),
         name="grad_partial",
-    )(xpos, own, got, got, got, dval, rew, near, lengths)
+    )(xpos, own_in, got_in, dval, rew, near, lengths)
     g_xy = lax.all_to_all(send, ("x", "y"), 0, 0, tiled=True)
     g_sum = jnp.sum(g_xy.astype(f32), axis=0).T.reshape(nz, BLOCK, cols)
     g_z = lax.ppermute(jnp.where(zpart == 0, g_sum[1], g_sum[0]), "zh", SWAP_Z)
@@ -173,7 +173,8 @@
     v_own = jnp.dot(own, w_full, preferred_element_type=f32)
     live = jnp.arange(slots, dtype=jnp.int32)[None, :] < lengths.reshape(rolls, 1)
     value = (v_own + v_got).reshape(rolls, slots, cols) * live.astype(f32)[:, :, None]
-    return value.astype(bf16), w_grad
+    value = value.astype(bf16)
+    return value, w_grad
 
 
 def solution(mesh):

time: 97.9 us -> 93.5 us (0.955)
  Pallas kernels: 9.41 us -> 6.62 us
  waiting for transfers between devices: 25.2 us -> 27 us
  starting transfers between devices: 56.6 us -> 54.9 us
  local copies, waits for them, and re-layouts: 2.96 us -> 1.37 us
    all_to_all x1, waiting for transfers between devices: 2.51 us -> 4.44 us  [per_device(): lax.all_to_all(jnp.broadcast_to(w_value[None], (ny, BLOCK, cols)), 'y', 0...]
    pallas_call x1, Pallas kernels: 4.76 us -> 2.9 us  [per_device(): pl.pallas_call(norm_kernel, grid=(rows // step,), in_specs=[pl.BlockSpec(...]
    unnamed x13 -> x5, local copies, waits for them, and re-layouts: 2.3 us -> 0.71 us
    all_to_all x1, starting transfers between devices: 7.36 us -> 6.02 us  [per_device(): g_xy = lax.all_to_all(send, ('x', 'y'), 0, 0, tiled=True)]
  transfers between devices with their start and end apart: 10 -> 10, of which waited for: 7 -> 7; matrix products, arithmetic and copies ran while one was open for 3% -> 3% of each run, Pallas kernels for 5% -> 4%
where the time goes in v4:
time: 93.5 us; the launch traced here: 92.8 us
  starting transfers between devices  54.9 us (59%)
  waiting for transfers between devices  27 us (29%)
  Pallas kernels  6.62 us (7%)
  local copies, waits for them, and re-layouts  1.37 us (1%)
  other arithmetic  1.24 us (1%)
    ppermute x1, starting transfers between devices, per_device(): w_far = lax.ppermute(w_y, 'zh', SWAP_Z)  14.2 us
    ppermute x3, starting transfers between devices, per_device(): w_parts.append(lax.ppermute(w_pair, 'x', X_SHIFTS[s]))  11.3 us
    ppermute x1, starting transfers between devices, per_device(): g_z = lax.ppermute(jnp.where(zpart == 0, g_sum[1], g_sum[0]), 'zh', SWAP_Z)  9.58 us
    ppermute x1, waiting for transfers between devices, per_device(): w_far = lax.ppermute(w_y, 'zh', SWAP_Z)  8.36 us
    all_to_all x1, starting transfers between devices, per_device(): lax.all_to_all(jnp.broadcast_to(w_value[None], (ny, BLOCK, cols)), 'y', 0...  7.55 us
    all_to_all x1, starting transfers between devices, per_device(): g_xy = lax.all_to_all(send, ('x', 'y'), 0, 0, tiled=True)  6.02 us
    ppermute x3, waiting for transfers between devices, per_device(): w_parts.append(lax.ppermute(w_pair, 'x', X_SHIFTS[s]))  4.92 us
    ppermute x1, waiting for transfers between devices, per_device(): g_z = lax.ppermute(jnp.where(zpart == 0, g_sum[1], g_sum[0]), 'zh', SWAP_Z)  4.88 us
  transfers between devices with their start and end apart: 10, of which 7 were waited for; matrix products, arithmetic and copies ran while one was open for 3% of the time, Pallas kernels for 4%

profile of v4, /device:TPU:72, one launch (start us, length us, event | category | flops | bytes accessed | tf_op | source)
XLA Modules:
  0.0 92.8 jit_solution(1905566773542414044)
XLA Ops:
  0.6 0.0 copy-start
  0.6 2.4 %collective-permute-start = (bf16[4]{0:T(256)(128)(2,1)}, bf16[4]{0:T(256)(128)(2,1)S(1)}, u32[]{:S(2)}, u32[]{:S(2)}) collective-permute-start(bf16[4]{0:T(256)(128)(2,1)} %param.10), channel_id=1, source_target_pairs={{0,12},{12,0},{24,36},{36,24},{48,60},{60,48},{72,84},{84,72},{1,1... | collective-permute-start | bytes 32 | tf_op jit(solution)/shard_map/ppermute | solution.py:113
  3.0 3.2 %collective-permute-done = bf16[4]{0:T(256)(128)(2,1)S(1)} collective-permute-done((bf16[4]{0:T(256)(128)(2,1)}, bf16[4]{0:T(256)(128)(2,1)S(1)}, u32[]{:S(2)}, u32[]{:S(2)}) %collective-permute-start) | collective-permute-done | bytes 40 | tf_op jit(solution)/shard_map/ppermute | solution.py:113
  6.2 2.9 %norm_split.1 = (bf16[128,4096]{1,0:T(8,128)(2,1)S(1)}, bf16[128,4352]{1,0:T(8,128)(2,1)S(1)}) custom-call(s32[1]{0:T(128)} %bitcast.core_ref, s32[1]{0:T(128)} %bitcast.1.xpos_ref, bf16[128,8192]{1,0:T(8,128)(2,1)} %bitcast.20, f32[1,8192]{1,0:T(1,128)} %bitcast.28, bf16[128,128]{1,0:T(8,128)(2,1)} %bitcast.25, bf16[1,4]{1,0:T(2,128)(2,1)} %bitcast.30, ...), custom_call_target="tpu_custom_call" | custom-call | tf_op jit(solution)/shard_map/norm_split/pallas_call | solution.py:128
  9.1 1.9 %collective-permute-start.5 = (bf16[128,4352]{1,0:T(8,128)(2,1)S(1)}, bf16[128,4352]{1,0:T(8,128)(2,1)S(1)}, u32[]{:S(2)}, u32[]{:S(2)}) collective-permute-start(bf16[128,4352]{1,0:T(8,128)(2,1)S(1)} %get-tuple-element.5), channel_id=1, source_target_pairs={{0,6},{6,0},{1,7},{7,1},{2,8},{8,2},{3,9},{9,3},{4,10},{10,4},{5,1... | collective-permute-start | bytes 3342344 | tf_op jit(solution)/shard_map/ppermute | solution.py:145
  11.1 0.0 copy-done
  11.1 0.7 broadcast_in_dim.2
  11.7 7.5 %all-to-all-start = ((bf16[8,64,128]{2,1,0:T(8,128)(2,1)}), bf16[8,64,128]{2,1,0:T(8,128)(2,1)S(1)}, u32[]{:S(2)}, u32[]{:S(2)}) async-start(bf16[8,64,128]{2,1,0:T(8,128)(2,1)} %broadcast_in_dim.2), calls=%async_computation | async-start | bytes 262144 | tf_op jit(solution)/shard_map/all_to_all | solution.py:114
  19.3 0.0 collective-permute-done.5.got_ref
  19.3 3.7 %grad_partial.1 = bf16[32,128,128]{2,1,0:T(8,128)(2,1)} custom-call(s32[1]{0:T(128)} %bitcast.1.xpos_ref, bf16[128,4096]{1,0:T(8,128)(2,1)S(1)} %get-tuple-element.4.own_ref, bf16[128,4352]{1,0:T(8,128)(2,1)S(1)} %collective-permute-done.5.got_ref, bf16[128,128]{1,0:T(8,128)(2,1)} %bitcast.26, bf16[1,4]{1,0:T(2,128)(2,1)} %bitcast.31, ...), custom_call_target="tpu_custom_call" | custom-call | tf_op jit(solution)/shard_map/grad_partial/pallas_call | solution.py:147
  23.0 4.4 %all-to-all-done = bf16[8,64,128]{2,1,0:T(8,128)(2,1)S(1)} async-done(((bf16[8,64,128]{2,1,0:T(8,128)(2,1)}), bf16[8,64,128]{2,1,0:T(8,128)(2,1)S(1)}, u32[]{:S(2)}, u32[]{:S(2)}) %all-to-all-start) | async-done | bytes 131104 | tf_op jit(solution)/shard_map/all_to_all | solution.py:114
  27.5 6.0 %all-to-all-start.1 = ((bf16[32,128,128]{2,1,0:T(8,128)(2,1)}), bf16[32,128,128]{2,1,0:T(8,128)(2,1)S(1)}, u32[]{:S(2)}, u32[]{:S(2)}) async-start(bf16[32,128,128]{2,1,0:T(8,128)(2,1)} %grad_partial.1), calls=%async_computation.1 | async-start | bytes 2097152 | tf_op jit(solution)/shard_map/all_to_all | solution.py:166
  33.5 14.2 %collective-permute-start.1 = (bf16[8,64,128]{2,1,0:T(8,128)(2,1)S(1)}, bf16[8,64,128]{2,1,0:T(8,128)(2,1)S(1)}, u32[]{:S(2)}, u32[]{:S(2)}) collective-permute-start(bf16[8,64,128]{2,1,0:T(8,128)(2,1)S(1)} %all-to-all-done), channel_id=1, source_target_pairs={{0,96},{96,0},{1,97},{97,1},{2,98},{98,2},{3,99},{99,3},{4,100},{1... | collective-permute-start | bytes 393224 | tf_op jit(solution)/shard_map/ppermute | solution.py:115
  47.7 8.4 %collective-permute-done.1 = bf16[8,64,128]{2,1,0:T(8,128)(2,1)S(1)} collective-permute-done((bf16[8,64,128]{2,1,0:T(8,128)(2,1)S(1)}, bf16[8,64,128]{2,1,0:T(8,128)(2,1)S(1)}, u32[]{:S(2)}, u32[]{:S(2)}) %collective-permute-start.1) | collective-permute-done | bytes 131104 | tf_op jit(solution)/shard_map/ppermute | solution.py:115
  56.1 3.4 %collective-permute-start.2 = (bf16[8,2,64,128]{3,2,1,0:T(8,128)(2,1)S(1)}, bf16[8,2,64,128]{3,2,1,0:T(8,128)(2,1)S(1)}, u32[]{:S(2)}, u32[]{:S(2)}) collective-permute-start(bf16[8,2,64,128]{3,2,1,0:T(8,128)(2,1)S(1)} %maximum_select_fusion), channel_id=1, source_target_pairs={{0,192},{192,384},{384,576},{576,0},{1,193},{193,385},{385,577},{5... | collective-permute-start | bytes 786440 | tf_op jit(solution)/shard_map/ppermute | solution.py:120
  59.5 4.6 %collective-permute-start.3 = (bf16[8,2,64,128]{3,2,1,0:T(8,128)(2,1)S(1)}, bf16[8,2,64,128]{3,2,1,0:T(8,128)(2,1)S(1)}, u32[]{:S(2)}, u32[]{:S(2)}) collective-permute-start(bf16[8,2,64,128]{3,2,1,0:T(8,128)(2,1)S(1)} %maximum_select_fusion), channel_id=1, source_target_pairs={{0,384},{192,576},{384,0},{576,192},{1,385},{193,577},{385,1},{577... | collective-permute-start | bytes 786440 | tf_op jit(solution)/shard_map/ppermute | solution.py:120
  64.2 3.3 %collective-permute-start.4 = (bf16[8,2,64,128]{3,2,1,0:T(8,128)(2,1)S(1)}, bf16[8,2,64,128]{3,2,1,0:T(8,128)(2,1)S(1)}, u32[]{:S(2)}, u32[]{:S(2)}) collective-permute-start(bf16[8,2,64,128]{3,2,1,0:T(8,128)(2,1)S(1)} %maximum_select_fusion), channel_id=1, source_target_pairs={{0,576},{192,0},{384,192},{576,384},{1,577},{193,1},{385,193},{577... | collective-permute-start | bytes 786440 | tf_op jit(solution)/shard_map/ppermute | solution.py:120
  67.5 0.0 collective-permute-done.2
  67.5 1.9 %collective-permute-done.3 = bf16[8,2,64,128]{3,2,1,0:T(8,128)(2,1)S(1)} collective-permute-done((bf16[8,2,64,128]{3,2,1,0:T(8,128)(2,1)S(1)}, bf16[8,2,64,128]{3,2,1,0:T(8,128)(2,1)S(1)}, u32[]{:S(2)}, u32[]{:S(2)}) %collective-permute-start.3) | collective-permute-done | bytes 262176 | tf_op jit(solution)/shard_map/ppermute | solution.py:120
  69.4 3.0 %collective-permute-done.4 = bf16[8,2,64,128]{3,2,1,0:T(8,128)(2,1)S(1)} collective-permute-done((bf16[8,2,64,128]{3,2,1,0:T(8,128)(2,1)S(1)}, bf16[8,2,64,128]{3,2,1,0:T(8,128)(2,1)S(1)}, u32[]{:S(2)}, u32[]{:S(2)}) %collective-permute-start.4) | collective-permute-done | bytes 262176 | tf_op jit(solution)/shard_map/ppermute | solution.py:120
  72.4 0.1 pad_maximum_fusion
  72.6 0.0 copy-start.1
  72.6 0.4 fusion
  73.0 1.9 %collective-permute-start.6 = (f32[128,128]{1,0:T(8,128)S(1)}, f32[128,128]{1,0:T(8,128)S(1)}, u32[]{:S(2)}, u32[]{:S(2)}) collective-permute-start(f32[128,128]{1,0:T(8,128)S(1)} %fusion), channel_id=1, source_target_pairs={{0,6},{6,0},{1,7},{7,1},{2,8},{8,2},{3,9},{9,3},{4,10},{10,4},{5,1... | collective-permute-start | bytes 196616 | tf_op jit(solution)/shard_map/ppermute | solution.py:172
  74.9 0.0 copy-done.1
  75.0 0.1 fusion.2
  75.0 1.1 %collective-permute-done.6 = f32[128,128]{1,0:T(8,128)S(1)} collective-permute-done((f32[128,128]{1,0:T(8,128)S(1)}, f32[128,128]{1,0:T(8,128)S(1)}, u32[]{:S(2)}, u32[]{:S(2)}) %collective-permute-start.6) | collective-permute-done | bytes 65568 | tf_op jit(solution)/shard_map/ppermute | solution.py:172
  76.2 0.4 convolution_add_fusion
  76.6 0.0 all-to-all-done.1
  76.6 0.2 convert_reduce_fusion
  76.8 0.1 slice_select_fusion
  76.9 9.6 %collective-permute-start.7 = (f32[64,128]{0,1:T(8,128)S(1)}, f32[64,128]{0,1:T(8,128)S(1)}, u32[]{:S(2)}, u32[]{:S(2)}) collective-permute-start(f32[64,128]{0,1:T(8,128)S(1)} %slice_select_fusion), channel_id=1, source_target_pairs={{0,96},{96,0},{1,97},{97,1},{2,98},{98,2},{3,99},{99,3},{4,100},{1... | collective-permute-start | bytes 98312 | tf_op jit(solution)/shard_map/ppermute | solution.py:168
  86.5 0.7 multiply_convert_fusion
  87.2 4.9 %collective-permute-done.7 = f32[64,128]{0,1:T(8,128)S(1)} collective-permute-done((f32[64,128]{0,1:T(8,128)S(1)}, f32[64,128]{0,1:T(8,128)S(1)}, u32[]{:S(2)}, u32[]{:S(2)}) %collective-permute-start.7) | collective-permute-done | bytes 32800 | tf_op jit(solution)/shard_map/ppermute | solution.py:168
  92.0 0.1 add_convert_fusion
  92.1 0.7 copy.8
  (1 shorter events, 0.0 us)
Async XLA Ops:
  0.6 10.4 %copy-start = (bf16[64,128]{1,0:T(8,128)(2,1)S(1)}, bf16[64,128]{1,0:T(8,128)(2,1)}, u32[]{:S(2)}) copy-start(bf16[64,128]{1,0:T(8,128)(2,1)} %param.8) | copy-start | bytes 49156
  0.6 5.6 %collective-permute-start = (bf16[4]{0:T(256)(128)(2,1)}, bf16[4]{0:T(256)(128)(2,1)S(1)}, u32[]{:S(2)}, u32[]{:S(2)}) collective-permute-start(bf16[4]{0:T(256)(128)(2,1)} %param.10), channel_id=1, source_target_pairs={{0,12},{12,0},{24,36},{36,24},{48,60},{60,48},{72,84},{84,72},{1,1... | collective-permute-start | bytes 32 | tf_op jit(solution)/shard_map/ppermute | solution.py:113
  9.1 10.2 %collective-permute-start.5 = (bf16[128,4352]{1,0:T(8,128)(2,1)S(1)}, bf16[128,4352]{1,0:T(8,128)(2,1)S(1)}, u32[]{:S(2)}, u32[]{:S(2)}) collective-permute-start(bf16[128,4352]{1,0:T(8,128)(2,1)S(1)} %get-tuple-element.5), channel_id=1, source_target_pairs={{0,6},{6,0},{1,7},{7,1},{2,8},{8,2},{3,9},{9,3},{4,10},{10,4},{5,1... | collective-permute-start | bytes 3342344 | tf_op jit(solution)/shard_map/ppermute | solution.py:145
  11.7 15.7 %all-to-all-start = ((bf16[8,64,128]{2,1,0:T(8,128)(2,1)}), bf16[8,64,128]{2,1,0:T(8,128)(2,1)S(1)}, u32[]{:S(2)}, u32[]{:S(2)}) async-start(bf16[8,64,128]{2,1,0:T(8,128)(2,1)} %broadcast_in_dim.2), calls=%async_computation | async-start | bytes 262144 | tf_op jit(solution)/shard_map/all_to_all | solution.py:114
  27.5 49.2 %all-to-all-start.1 = ((bf16[32,128,128]{2,1,0:T(8,128)(2,1)}), bf16[32,128,128]{2,1,0:T(8,128)(2,1)S(1)}, u32[]{:S(2)}, u32[]{:S(2)}) async-start(bf16[32,128,128]{2,1,0:T(8,128)(2,1)} %grad_partial.1), calls=%async_computation.1 | async-start | bytes 2097152 | tf_op jit(solution)/shard_map/all_to_all | solution.py:166
  33.5 22.6 %collective-permute-start.1 = (bf16[8,64,128]{2,1,0:T(8,128)(2,1)S(1)}, bf16[8,64,128]{2,1,0:T(8,128)(2,1)S(1)}, u32[]{:S(2)}, u32[]{:S(2)}) collective-permute-start(bf16[8,64,128]{2,1,0:T(8,128)(2,1)S(1)} %all-to-all-done), channel_id=1, source_target_pairs={{0,96},{96,0},{1,97},{97,1},{2,98},{98,2},{3,99},{99,3},{4,100},{1... | collective-permute-start | bytes 393224 | tf_op jit(solution)/shard_map/ppermute | solution.py:115
  56.1 11.4 %collective-permute-start.2 = (bf16[8,2,64,128]{3,2,1,0:T(8,128)(2,1)S(1)}, bf16[8,2,64,128]{3,2,1,0:T(8,128)(2,1)S(1)}, u32[]{:S(2)}, u32[]{:S(2)}) collective-permute-start(bf16[8,2,64,128]{3,2,1,0:T(8,128)(2,1)S(1)} %maximum_select_fusion), channel_id=1, source_target_pairs={{0,192},{192,384},{384,576},{576,0},{1,193},{193,385},{385,577},{5... | collective-permute-start | bytes 786440 | tf_op jit(solution)/shard_map/ppermute | solution.py:120
  59.5 9.9 %collective-permute-start.3 = (bf16[8,2,64,128]{3,2,1,0:T(8,128)(2,1)S(1)}, bf16[8,2,64,128]{3,2,1,0:T(8,128)(2,1)S(1)}, u32[]{:S(2)}, u32[]{:S(2)}) collective-permute-start(bf16[8,2,64,128]{3,2,1,0:T(8,128)(2,1)S(1)} %maximum_select_fusion), channel_id=1, source_target_pairs={{0,384},{192,576},{384,0},{576,192},{1,385},{193,577},{385,1},{577... | collective-permute-start | bytes 786440 | tf_op jit(solution)/shard_map/ppermute | solution.py:120
  64.2 8.3 %collective-permute-start.4 = (bf16[8,2,64,128]{3,2,1,0:T(8,128)(2,1)S(1)}, bf16[8,2,64,128]{3,2,1,0:T(8,128)(2,1)S(1)}, u32[]{:S(2)}, u32[]{:S(2)}) collective-permute-start(bf16[8,2,64,128]{3,2,1,0:T(8,128)(2,1)S(1)} %maximum_select_fusion), channel_id=1, source_target_pairs={{0,576},{192,0},{384,192},{576,384},{1,577},{193,1},{385,193},{577... | collective-permute-start | bytes 786440 | tf_op jit(solution)/shard_map/ppermute | solution.py:120
  72.6 2.4 %copy-start.1 = (s32[1,4]{1,0:T(1,128)S(1)}, s32[1,4]{1,0:T(1,128)}, u32[]{:S(2)}) copy-start(s32[1,4]{1,0:T(1,128)} %len_ref.3) | copy-start | bytes 52
  73.0 3.1 %collective-permute-start.6 = (f32[128,128]{1,0:T(8,128)S(1)}, f32[128,128]{1,0:T(8,128)S(1)}, u32[]{:S(2)}, u32[]{:S(2)}) collective-permute-start(f32[128,128]{1,0:T(8,128)S(1)} %fusion), channel_id=1, source_target_pairs={{0,6},{6,0},{1,7},{7,1},{2,8},{8,2},{3,9},{9,3},{4,10},{10,4},{5,1... | collective-permute-start | bytes 196616 | tf_op jit(solution)/shard_map/ppermute | solution.py:172
  76.9 15.2 %collective-permute-start.7 = (f32[64,128]{0,1:T(8,128)S(1)}, f32[64,128]{0,1:T(8,128)S(1)}, u32[]{:S(2)}, u32[]{:S(2)}) collective-permute-start(f32[64,128]{0,1:T(8,128)S(1)} %slice_select_fusion), channel_id=1, source_target_pairs={{0,96},{96,0},{1,97},{97,1},{2,98},{98,2},{3,99},{99,3},{4,100},{1... | collective-permute-start | bytes 98312 | tf_op jit(solution)/shard_map/ppermute | solution.py:168

commit v5 on v4

--- a/solution.py
+++ b/solution.py
@@ -11,6 +11,7 @@
 Y_PAIR = tuple((j, j ^ 1) for j in range(8))
 LANES = 128
 BLOCK = 64
+VMEM_GRANT = 10 * 2**20
 NX = 4
 X_SHIFTS = tuple(tuple((j, (j + s) % NX) for j in range(NX)) for s in range(NX))
 SWAP_Z = ((0, 1), (1, 0))
@@ -98,6 +99,20 @@
         out_ref[j] = acc[:, j * LANES : (j + 1) * LANES].astype(bf16)
 
 
+def value_kernel(z_ref, got_ref, own_ref, *refs):
+    *parts, v_other_ref, v_own_ref, w_ref = refs
+    first = z_ref[0] == 0
+    for s, (near, far) in enumerate(zip(parts[:NX], parts[NX:])):
+        for y in range(near.shape[0]):
+            at = (s * near.shape[0] + y) * 2 * BLOCK
+            a, b = near[y].astype(f32), far[y].astype(f32)
+            w_ref[at : at + BLOCK] = jnp.where(first, a, b).astype(bf16)
+            w_ref[at + BLOCK : at + 2 * BLOCK] = jnp.where(first, b, a).astype(bf16)
+    half = w_ref.shape[0]
+    v_other_ref[...] = jnp.dot(got_ref[:, :half], w_ref[...], preferred_element_type=f32)
+    v_own_ref[...] = jnp.dot(own_ref[...], w_ref[...], preferred_element_type=f32)
+
+
 def on_chip(array):
     return pltpu.with_memory_space_constraint(array, pltpu.VMEM)
 
@@ -114,14 +129,13 @@
     w_y = lax.all_to_all(jnp.broadcast_to(w_value[None], (ny, BLOCK, cols)), "y", 0, 0, tiled=True)
     w_far = lax.ppermute(w_y, "zh", SWAP_Z)
     zpart = lax.axis_index("zh")
-    w_pair = jnp.where(zpart == 0, jnp.stack([w_y, w_far], axis=1), jnp.stack([w_far, w_y], axis=1))
-    w_parts = [w_pair]
+    own_w, far_w = [w_y], [w_far]
     for s in range(1, nx):
-        w_parts.append(lax.ppermute(w_pair, "x", X_SHIFTS[s]))
-    w_full = jnp.concatenate(w_parts).reshape(half, cols)
-
+        own_w.append(lax.ppermute(w_y, "x", X_SHIFTS[s]))
+        far_w.append(lax.ppermute(w_far, "x", X_SHIFTS[s]))
     core = lax.axis_index("c").astype(jnp.int32).reshape(1)
     xpos = lax.axis_index("x").astype(jnp.int32).reshape(1)
+    zpos = zpart.astype(jnp.int32).reshape(1)
     dval = d_value.reshape(rows, cols)
     rew, near = rewards.reshape(1, rolls), on_chip(near.reshape(1, rolls))
     step = 64
@@ -161,6 +175,7 @@
             scratch_shapes=[pltpu.VMEM((cols, rows), bf16), pltpu.VMEM((cols, rows), bf16)],
         ),
         out_shape=jax.ShapeDtypeStruct((nx * ny, cols, nz * BLOCK), bf16),
+        compiler_params=pltpu.CompilerParams(vmem_limit_bytes=VMEM_GRANT),
         name="grad_partial",
     )(xpos, own_in, got_in, dval, rew, near, lengths)
     g_xy = lax.all_to_all(send, ("x", "y"), 0, 0, tiled=True)
@@ -168,9 +183,17 @@
     g_z = lax.ppermute(jnp.where(zpart == 0, g_sum[1], g_sum[0]), "zh", SWAP_Z)
     w_grad = (jnp.where(zpart == 0, g_sum[0], g_sum[1]) + g_z).astype(bf16)
 
-    v_other = jnp.dot(got[:, :half], w_full, preferred_element_type=f32)
+    in_vmem = pl.BlockSpec(memory_space=pltpu.VMEM)
+    v_other, v_own = pl.pallas_call(
+        value_kernel,
+        in_specs=[pl.BlockSpec(memory_space=pltpu.SMEM)] + [in_vmem] * (2 + 2 * nx),
+        out_specs=[in_vmem, in_vmem],
+        out_shape=[pltpu.VMEM((rows, cols), f32), pltpu.VMEM((rows, cols), f32)],
+        scratch_shapes=[pltpu.VMEM((half, cols), bf16)],
+        compiler_params=pltpu.CompilerParams(vmem_limit_bytes=VMEM_GRANT),
+        name="value_parts",
+    )(zpos, got_in, own_in, *[on_chip(w) for w in own_w + far_w])
     v_got = lax.ppermute(v_other, "c", SWAP)
-    v_own = jnp.dot(own, w_full, preferred_element_type=f32)
     live = jnp.arange(slots, dtype=jnp.int32)[None, :] < lengths.reshape(rolls, 1)
     value = (v_own + v_got).reshape(rolls, slots, cols) * live.astype(f32)[:, :, None]
     value = value.astype(bf16)

time: 93.5 us -> 93.2 us (level)
  the two profiles are of different devices: /device:TPU:72 before, /device:TPU:2 now
where the time goes in v5:
time: 93.2 us; the launch traced here: 92.5 us
  starting transfers between devices  58.7 us (63%)
  waiting for transfers between devices  22.5 us (24%)
  Pallas kernels  6.67 us (7%)
  other arithmetic  2.32 us (2%)
  local copies, waits for them, and re-layouts  1.4 us (2%)
    ppermute x3, starting transfers between devices, per_device(): own_w.append(lax.ppermute(w_y, 'x', X_SHIFTS[s]))  10.5 us
    all_to_all x1, starting transfers between devices, per_device(): g_xy = lax.all_to_all(send, ('x', 'y'), 0, 0, tiled=True)  10.3 us
    ppermute x1, starting transfers between devices, per_device(): w_far = lax.ppermute(w_y, 'zh', SWAP_Z)  9.91 us
    ppermute x3, starting transfers between devices, per_device(): far_w.append(lax.ppermute(w_far, 'x', X_SHIFTS[s]))  9.23 us
    ppermute x1, waiting for transfers between devices, per_device(): g_z = lax.ppermute(jnp.where(zpart == 0, g_sum[1], g_sum[0]), 'zh', SWAP_Z)  7.58 us
    all_to_all x1, starting transfers between devices, per_device(): lax.all_to_all(jnp.broadcast_to(w_value[None], (ny, BLOCK, cols)), 'y', 0...  7.1 us
    all_to_all x1, waiting for transfers between devices, per_device(): lax.all_to_all(jnp.broadcast_to(w_value[None], (ny, BLOCK, cols)), 'y', 0...  6.77 us
    ppermute x3, waiting for transfers between devices, per_device(): far_w.append(lax.ppermute(w_far, 'x', X_SHIFTS[s]))  4.9 us
  transfers between devices with their start and end apart: 13, of which 6 were waited for; matrix products, arithmetic and copies ran while one was open for 2% of the time, Pallas kernels for 4%

profile of v5, /device:TPU:2, one launch (start us, length us, event | category | flops | bytes accessed | tf_op | source)
XLA Modules:
  0.0 92.5 jit_solution(10763711766465311346)
XLA Ops:
  0.6 0.0 copy-start.2
  0.6 0.0 copy-start
  0.7 0.0 copy-start.1
  0.7 0.0 copy-start.3
  0.7 3.6 %collective-permute-start = (bf16[4]{0:T(256)(128)(2,1)}, bf16[4]{0:T(256)(128)(2,1)S(1)}, u32[]{:S(2)}, u32[]{:S(2)}) collective-permute-start(bf16[4]{0:T(256)(128)(2,1)} %param.10), channel_id=1, source_target_pairs={{0,12},{12,0},{24,36},{36,24},{48,60},{60,48},{72,84},{84,72},{1,1... | collective-permute-start | bytes 32 | tf_op jit(solution)/shard_map/ppermute | solution.py:128
  4.3 2.1 %collective-permute-done = bf16[4]{0:T(256)(128)(2,1)S(1)} collective-permute-done((bf16[4]{0:T(256)(128)(2,1)}, bf16[4]{0:T(256)(128)(2,1)S(1)}, u32[]{:S(2)}, u32[]{:S(2)}) %collective-permute-start) | collective-permute-done | bytes 40 | tf_op jit(solution)/shard_map/ppermute | solution.py:128
  6.4 2.9 %norm_split.1 = (bf16[128,4096]{1,0:T(8,128)(2,1)S(1)}, bf16[128,4352]{1,0:T(8,128)(2,1)S(1)}) custom-call(s32[1]{0:T(128)} %bitcast.1.core_ref, s32[1]{0:T(128)} %bitcast.2.xpos_ref, bf16[128,8192]{1,0:T(8,128)(2,1)} %bitcast.18, f32[1,8192]{1,0:T(1,128)} %bitcast.22, bf16[128,128]{1,0:T(8,128)(2,1)} %bitcast.11, bf16[1,4]{1,0:T(2,128)(2,1)} %bitcast.14, ...), custom_call_target="tpu_custom_call" | custom-call | tf_op jit(solution)/shard_map/norm_split/pallas_call | solution.py:142
  9.3 1.9 %collective-permute-start.1 = (bf16[128,4352]{1,0:T(8,128)(2,1)S(1)}, bf16[128,4352]{1,0:T(8,128)(2,1)S(1)}, u32[]{:S(2)}, u32[]{:S(2)}) collective-permute-start(bf16[128,4352]{1,0:T(8,128)(2,1)S(1)} %get-tuple-element.6), channel_id=1, source_target_pairs={{0,6},{6,0},{1,7},{7,1},{2,8},{8,2},{3,9},{9,3},{4,10},{10,4},{5,1... | collective-permute-start | bytes 3342344 | tf_op jit(solution)/shard_map/ppermute | solution.py:159
  11.2 0.0 copy-done.3
  11.2 0.7 broadcast_in_dim.2
  11.9 7.1 %all-to-all-start = ((bf16[8,64,128]{2,1,0:T(8,128)(2,1)}), bf16[8,64,128]{2,1,0:T(8,128)(2,1)S(1)}, u32[]{:S(2)}, u32[]{:S(2)}) async-start(bf16[8,64,128]{2,1,0:T(8,128)(2,1)} %broadcast_in_dim.2), calls=%async_computation | async-start | bytes 262144 | tf_op jit(solution)/shard_map/all_to_all | solution.py:129
  19.0 0.0 collective-permute-done.1.got_ref
  19.0 0.0 copy-done.2
  19.0 0.0 copy-done
  19.1 0.0 copy-done.1
  19.1 2.9 %grad_partial.1 = bf16[32,128,128]{2,1,0:T(8,128)(2,1)} custom-call(s32[1]{0:T(128)} %bitcast.2.xpos_ref, bf16[128,4096]{1,0:T(8,128)(2,1)S(1)} %get-tuple-element.7.own_ref, bf16[128,4352]{1,0:T(8,128)(2,1)S(1)} %collective-permute-done.1.got_ref, bf16[128,128]{1,0:T(8,128)(2,1)S(1)} %bitcast.12, bf16[1,4]{1,0:T(2,128)(2,1)S(1)} %bitcast.15, ...), custom_call_target="tpu_custom_call" | custom-call | tf_op jit(solution)/shard_map/grad_partial/pallas_call | solution.py:161
  22.0 6.8 %all-to-all-done.refs_0_ = bf16[8,64,128]{2,1,0:T(8,128)(2,1)S(1)} async-done(((bf16[8,64,128]{2,1,0:T(8,128)(2,1)}), bf16[8,64,128]{2,1,0:T(8,128)(2,1)S(1)}, u32[]{:S(2)}, u32[]{:S(2)}) %all-to-all-start) | async-done | bytes 131104 | tf_op jit(solution)/shard_map/all_to_all | solution.py:129
  28.8 10.3 %all-to-all-start.1 = ((bf16[32,128,128]{2,1,0:T(8,128)(2,1)}), bf16[32,128,128]{2,1,0:T(8,128)(2,1)}, u32[]{:S(2)}, u32[]{:S(2)}) async-start(bf16[32,128,128]{2,1,0:T(8,128)(2,1)} %grad_partial.1), calls=%async_computation.1 | async-start | bytes 2097152 | tf_op jit(solution)/shard_map/all_to_all | solution.py:181
  39.0 9.9 %collective-permute-start.5 = (bf16[8,64,128]{2,1,0:T(8,128)(2,1)S(1)}, bf16[8,64,128]{2,1,0:T(8,128)(2,1)S(1)}, u32[]{:S(2)}, u32[]{:S(2)}) collective-permute-start(bf16[8,64,128]{2,1,0:T(8,128)(2,1)S(1)} %all-to-all-done.refs_0_), channel_id=1, source_target_pairs={{0,96},{96,0},{1,97},{97,1},{2,98},{98,2},{3,99},{99,3},{4,100},{1... | collective-permute-start | bytes 393224 | tf_op jit(solution)/shard_map/ppermute | solution.py:130
  49.0 3.4 %collective-permute-start.2 = (bf16[8,64,128]{2,1,0:T(8,128)(2,1)S(1)}, bf16[8,64,128]{2,1,0:T(8,128)(2,1)S(1)}, u32[]{:S(2)}, u32[]{:S(2)}) collective-permute-start(bf16[8,64,128]{2,1,0:T(8,128)(2,1)S(1)} %all-to-all-done.refs_0_), channel_id=1, source_target_pairs={{0,192},{192,384},{384,576},{576,0},{1,193},{193,385},{385,577},{5... | collective-permute-start | bytes 393224 | tf_op jit(solution)/shard_map/ppermute | solution.py:134
  52.3 2.8 %collective-permute-start.3 = (bf16[8,64,128]{2,1,0:T(8,128)(2,1)S(1)}, bf16[8,64,128]{2,1,0:T(8,128)(2,1)S(1)}, u32[]{:S(2)}, u32[]{:S(2)}) collective-permute-start(bf16[8,64,128]{2,1,0:T(8,128)(2,1)S(1)} %all-to-all-done.refs_0_), channel_id=1, source_target_pairs={{0,384},{192,576},{384,0},{576,192},{1,385},{193,577},{385,1},{577... | collective-permute-start | bytes 393224 | tf_op jit(solution)/shard_map/ppermute | solution.py:134
  55.2 4.3 %collective-permute-start.4 = (bf16[8,64,128]{2,1,0:T(8,128)(2,1)S(1)}, bf16[8,64,128]{2,1,0:T(8,128)(2,1)S(1)}, u32[]{:S(2)}, u32[]{:S(2)}) collective-permute-start(bf16[8,64,128]{2,1,0:T(8,128)(2,1)S(1)} %all-to-all-done.refs_0_), channel_id=1, source_target_pairs={{0,576},{192,0},{384,192},{576,384},{1,577},{193,1},{385,193},{577... | collective-permute-start | bytes 393224 | tf_op jit(solution)/shard_map/ppermute | solution.py:134
  59.5 0.0 collective-permute-done.5.refs_4_
  59.5 1.9 %collective-permute-start.6 = (bf16[8,64,128]{2,1,0:T(8,128)(2,1)S(1)}, bf16[8,64,128]{2,1,0:T(8,128)(2,1)S(1)}, u32[]{:S(2)}, u32[]{:S(2)}) collective-permute-start(bf16[8,64,128]{2,1,0:T(8,128)(2,1)S(1)} %collective-permute-done.5.refs_4_), channel_id=1, source_target_pairs={{0,192},{192,384},{384,576},{576,0},{1,193},{193,385},{385,577},{5... | collective-permute-start | bytes 393224 | tf_op jit(solution)/shard_map/ppermute | solution.py:135
  61.4 5.4 %collective-permute-start.7 = (bf16[8,64,128]{2,1,0:T(8,128)(2,1)S(1)}, bf16[8,64,128]{2,1,0:T(8,128)(2,1)S(1)}, u32[]{:S(2)}, u32[]{:S(2)}) collective-permute-start(bf16[8,64,128]{2,1,0:T(8,128)(2,1)S(1)} %collective-permute-done.5.refs_4_), channel_id=1, source_target_pairs={{0,384},{192,576},{384,0},{576,192},{1,385},{193,577},{385,1},{577... | collective-permute-start | bytes 393224 | tf_op jit(solution)/shard_map/ppermute | solution.py:135
  66.8 0.0 collective-permute-done.2.refs_1_
  66.8 1.9 %collective-permute-start.8 = (bf16[8,64,128]{2,1,0:T(8,128)(2,1)S(1)}, bf16[8,64,128]{2,1,0:T(8,128)(2,1)S(1)}, u32[]{:S(2)}, u32[]{:S(2)}) collective-permute-start(bf16[8,64,128]{2,1,0:T(8,128)(2,1)S(1)} %collective-permute-done.5.refs_4_), channel_id=1, source_target_pairs={{0,576},{192,0},{384,192},{576,384},{1,577},{193,1},{385,193},{577... | collective-permute-start | bytes 393224 | tf_op jit(solution)/shard_map/ppermute | solution.py:135
  68.7 0.0 collective-permute-done.3.refs_2_
  68.7 0.0 collective-permute-done.4.refs_3_
  68.8 0.0 collective-permute-done.6.refs_5_
  68.8 2.6 %collective-permute-done.7.refs_6_ = bf16[8,64,128]{2,1,0:T(8,128)(2,1)S(1)} collective-permute-done((bf16[8,64,128]{2,1,0:T(8,128)(2,1)S(1)}, bf16[8,64,128]{2,1,0:T(8,128)(2,1)S(1)}, u32[]{:S(2)}, u32[]{:S(2)}) %collective-permute-start.7) | collective-permute-done | bytes 131104 | tf_op jit(solution)/shard_map/ppermute | solution.py:135
  71.4 2.3 %collective-permute-done.8.refs_7_ = bf16[8,64,128]{2,1,0:T(8,128)(2,1)S(1)} collective-permute-done((bf16[8,64,128]{2,1,0:T(8,128)(2,1)S(1)}, bf16[8,64,128]{2,1,0:T(8,128)(2,1)S(1)}, u32[]{:S(2)}, u32[]{:S(2)}) %collective-permute-start.8) | collective-permute-done | bytes 131104 | tf_op jit(solution)/shard_map/ppermute | solution.py:135
  73.7 0.8 value_parts.1
  74.5 1.9 %collective-permute-start.9 = (f32[128,128]{1,0:T(8,128)S(1)}, f32[128,128]{1,0:T(8,128)S(1)}, u32[]{:S(2)}, u32[]{:S(2)}) collective-permute-start(f32[128,128]{1,0:T(8,128)S(1)} %get-tuple-element.9), channel_id=1, source_target_pairs={{0,6},{6,0},{1,7},{7,1},{2,8},{8,2},{3,9},{9,3},{4,10},{10,4},{5,1... | collective-permute-start | bytes 196616 | tf_op jit(solution)/shard_map/ppermute | solution.py:196
  76.4 0.1 fusion
  76.5 1.1 %collective-permute-done.9 = f32[128,128]{1,0:T(8,128)S(1)} collective-permute-done((f32[128,128]{1,0:T(8,128)S(1)}, f32[128,128]{1,0:T(8,128)S(1)}, u32[]{:S(2)}, u32[]{:S(2)}) %collective-permute-start.9) | collective-permute-done | bytes 65568 | tf_op jit(solution)/shard_map/ppermute | solution.py:196
  77.7 0.0 all-to-all-done.1
  77.7 1.4 %convert_reduce_fusion = f32[128,128]{1,0:T(8,128)S(1)} fusion(bf16[32,128,128]{2,1,0:T(8,128)(2,1)} %all-to-all-done.1), kind=kLoop, calls=%fused_computation | loop fusion | flops 1032192 | bytes 1114112 | tf_op jit(solution)/shard_map/reduce_sum | solution.py:182
  79.1 0.1 slice_select_fusion
  79.2 4.3 %collective-permute-start.10 = (f32[64,128]{0,1:T(8,128)S(1)}, f32[64,128]{0,1:T(8,128)S(1)}, u32[]{:S(2)}, u32[]{:S(2)}) collective-permute-start(f32[64,128]{0,1:T(8,128)S(1)} %slice_select_fusion), channel_id=1, source_target_pairs={{0,96},{96,0},{1,97},{97,1},{2,98},{98,2},{3,99},{99,3},{4,100},{1... | collective-permute-start | bytes 98312 | tf_op jit(solution)/shard_map/ppermute | solution.py:183
  83.4 0.7 multiply_convert_fusion
  84.1 7.6 %collective-permute-done.10 = f32[64,128]{0,1:T(8,128)S(1)} collective-permute-done((f32[64,128]{0,1:T(8,128)S(1)}, f32[64,128]{0,1:T(8,128)S(1)}, u32[]{:S(2)}, u32[]{:S(2)}) %collective-permute-start.10) | collective-permute-done | bytes 32800 | tf_op jit(solution)/shard_map/ppermute | solution.py:183
  91.7 0.1 add_convert_fusion
  91.8 0.7 copy.8
  (1 shorter events, 0.0 us)
Async XLA Ops:
  0.6 18.4 %copy-start.2 = (bf16[4]{0:T(256)(128)(2,1)S(1)}, bf16[4]{0:T(256)(128)(2,1)}, u32[]{:S(2)}) copy-start(bf16[4]{0:T(256)(128)(2,1)} %param.10) | copy-start | bytes 28
  0.6 18.4 %copy-start = (bf16[4,32,128]{2,1,0:T(8,128)(2,1)S(1)}, bf16[4,32,128]{2,1,0:T(8,128)(2,1)}, u32[]{:S(2)}) copy-start(bf16[4,32,128]{2,1,0:T(8,128)(2,1)} %param.9) | copy-start | bytes 98308
  0.7 18.4 %copy-start.1 = (s32[1,4]{1,0:T(1,128)S(1)}, s32[1,4]{1,0:T(1,128)}, u32[]{:S(2)}) copy-start(s32[1,4]{1,0:T(1,128)} %len_ref.3) | copy-start | bytes 52
  0.7 10.6 %copy-start.3 = (bf16[64,128]{1,0:T(8,128)(2,1)S(1)}, bf16[64,128]{1,0:T(8,128)(2,1)}, u32[]{:S(2)}) copy-start(bf16[64,128]{1,0:T(8,128)(2,1)} %param.8) | copy-start | bytes 49156
  0.7 5.7 %collective-permute-start = (bf16[4]{0:T(256)(128)(2,1)}, bf16[4]{0:T(256)(128)(2,1)S(1)}, u32[]{:S(2)}, u32[]{:S(2)}) collective-permute-start(bf16[4]{0:T(256)(128)(2,1)} %param.10), channel_id=1, source_target_pairs={{0,12},{12,0},{24,36},{36,24},{48,60},{60,48},{72,84},{84,72},{1,1... | collective-permute-start | bytes 32 | tf_op jit(solution)/shard_map/ppermute | solution.py:128
  9.3 9.7 %collective-permute-start.1 = (bf16[128,4352]{1,0:T(8,128)(2,1)S(1)}, bf16[128,4352]{1,0:T(8,128)(2,1)S(1)}, u32[]{:S(2)}, u32[]{:S(2)}) collective-permute-start(bf16[128,4352]{1,0:T(8,128)(2,1)S(1)} %get-tuple-element.6), channel_id=1, source_target_pairs={{0,6},{6,0},{1,7},{7,1},{2,8},{8,2},{3,9},{9,3},{4,10},{10,4},{5,1... | collective-permute-start | bytes 3342344 | tf_op jit(solution)/shard_map/ppermute | solution.py:159
  11.9 16.8 %all-to-all-start = ((bf16[8,64,128]{2,1,0:T(8,128)(2,1)}), bf16[8,64,128]{2,1,0:T(8,128)(2,1)S(1)}, u32[]{:S(2)}, u32[]{:S(2)}) async-start(bf16[8,64,128]{2,1,0:T(8,128)(2,1)} %broadcast_in_dim.2), calls=%async_computation | async-start | bytes 262144 | tf_op jit(solution)/shard_map/all_to_all | solution.py:129
  28.8 48.9 %all-to-all-start.1 = ((bf16[32,128,128]{2,1,0:T(8,128)(2,1)}), bf16[32,128,128]{2,1,0:T(8,128)(2,1)}, u32[]{:S(2)}, u32[]{:S(2)}) async-start(bf16[32,128,128]{2,1,0:T(8,128)(2,1)} %grad_partial.1), calls=%async_computation.1 | async-start | bytes 2097152 | tf_op jit(solution)/shard_map/all_to_all | solution.py:181
  39.0 20.4 %collective-permute-start.5 = (bf16[8,64,128]{2,1,0:T(8,128)(2,1)S(1)}, bf16[8,64,128]{2,1,0:T(8,128)(2,1)S(1)}, u32[]{:S(2)}, u32[]{:S(2)}) collective-permute-start(bf16[8,64,128]{2,1,0:T(8,128)(2,1)S(1)} %all-to-all-done.refs_0_), channel_id=1, source_target_pairs={{0,96},{96,0},{1,97},{97,1},{2,98},{98,2},{3,99},{99,3},{4,100},{1... | collective-permute-start | bytes 393224 | tf_op jit(solution)/shard_map/ppermute | solution.py:130
  49.0 17.8 %collective-permute-start.2 = (bf16[8,64,128]{2,1,0:T(8,128)(2,1)S(1)}, bf16[8,64,128]{2,1,0:T(8,128)(2,1)S(1)}, u32[]{:S(2)}, u32[]{:S(2)}) collective-permute-start(bf16[8,64,128]{2,1,0:T(8,128)(2,1)S(1)} %all-to-all-done.refs_0_), channel_id=1, source_target_pairs={{0,192},{192,384},{384,576},{576,0},{1,193},{193,385},{385,577},{5... | collective-permute-start | bytes 393224 | tf_op jit(solution)/shard_map/ppermute | solution.py:134
  52.3 16.4 %collective-permute-start.3 = (bf16[8,64,128]{2,1,0:T(8,128)(2,1)S(1)}, bf16[8,64,128]{2,1,0:T(8,128)(2,1)S(1)}, u32[]{:S(2)}, u32[]{:S(2)}) collective-permute-start(bf16[8,64,128]{2,1,0:T(8,128)(2,1)S(1)} %all-to-all-done.refs_0_), channel_id=1, source_target_pairs={{0,384},{192,576},{384,0},{576,192},{1,385},{193,577},{385,1},{577... | collective-permute-start | bytes 393224 | tf_op jit(solution)/shard_map/ppermute | solution.py:134
  55.2 13.6 %collective-permute-start.4 = (bf16[8,64,128]{2,1,0:T(8,128)(2,1)S(1)}, bf16[8,64,128]{2,1,0:T(8,128)(2,1)S(1)}, u32[]{:S(2)}, u32[]{:S(2)}) collective-permute-start(bf16[8,64,128]{2,1,0:T(8,128)(2,1)S(1)} %all-to-all-done.refs_0_), channel_id=1, source_target_pairs={{0,576},{192,0},{384,192},{576,384},{1,577},{193,1},{385,193},{577... | collective-permute-start | bytes 393224 | tf_op jit(solution)/shard_map/ppermute | solution.py:134
  59.5 9.3 %collective-permute-start.6 = (bf16[8,64,128]{2,1,0:T(8,128)(2,1)S(1)}, bf16[8,64,128]{2,1,0:T(8,128)(2,1)S(1)}, u32[]{:S(2)}, u32[]{:S(2)}) collective-permute-start(bf16[8,64,128]{2,1,0:T(8,128)(2,1)S(1)} %collective-permute-done.5.refs_4_), channel_id=1, source_target_pairs={{0,192},{192,384},{384,576},{576,0},{1,193},{193,385},{385,577},{5... | collective-permute-start | bytes 393224 | tf_op jit(solution)/shard_map/ppermute | solution.py:135
  61.4 10.0 %collective-permute-start.7 = (bf16[8,64,128]{2,1,0:T(8,128)(2,1)S(1)}, bf16[8,64,128]{2,1,0:T(8,128)(2,1)S(1)}, u32[]{:S(2)}, u32[]{:S(2)}) collective-permute-start(bf16[8,64,128]{2,1,0:T(8,128)(2,1)S(1)} %collective-permute-done.5.refs_4_), channel_id=1, source_target_pairs={{0,384},{192,576},{384,0},{576,192},{1,385},{193,577},{385,1},{577... | collective-permute-start | bytes 393224 | tf_op jit(solution)/shard_map/ppermute | solution.py:135
  66.8 6.9 %collective-permute-start.8 = (bf16[8,64,128]{2,1,0:T(8,128)(2,1)S(1)}, bf16[8,64,128]{2,1,0:T(8,128)(2,1)S(1)}, u32[]{:S(2)}, u32[]{:S(2)}) collective-permute-start(bf16[8,64,128]{2,1,0:T(8,128)(2,1)S(1)} %collective-permute-done.5.refs_4_), channel_id=1, source_target_pairs={{0,576},{192,0},{384,192},{576,384},{1,577},{193,1},{385,193},{577... | collective-permute-start | bytes 393224 | tf_op jit(solution)/shard_map/ppermute | solution.py:135
  74.5 3.1 %collective-permute-start.9 = (f32[128,128]{1,0:T(8,128)S(1)}, f32[128,128]{1,0:T(8,128)S(1)}, u32[]{:S(2)}, u32[]{:S(2)}) collective-permute-start(f32[128,128]{1,0:T(8,128)S(1)} %get-tuple-element.9), channel_id=1, source_target_pairs={{0,6},{6,0},{1,7},{7,1},{2,8},{8,2},{3,9},{9,3},{4,10},{10,4},{5,1... | collective-permute-start | bytes 196616 | tf_op jit(solution)/shard_map/ppermute | solution.py:196
  79.2 12.6 %collective-permute-start.10 = (f32[64,128]{0,1:T(8,128)S(1)}, f32[64,128]{0,1:T(8,128)S(1)}, u32[]{:S(2)}, u32[]{:S(2)}) collective-permute-start(f32[64,128]{0,1:T(8,128)S(1)} %slice_select_fusion), channel_id=1, source_target_pairs={{0,96},{96,0},{1,97},{97,1},{2,98},{98,2},{3,99},{99,3},{4,100},{1... | collective-permute-start | bytes 98312 | tf_op jit(solution)/shard_map/ppermute | solution.py:183

commit v6 on v5

--- a/solution.py
+++ b/solution.py
@@ -97,6 +97,16 @@
     acc = acc + jnp.dot(ds_other[...], got_ref[:, here], preferred_element_type=f32)
     for j in range(out_ref.shape[0]):
         out_ref[j] = acc[:, j * LANES : (j + 1) * LANES].astype(bf16)
+
+
+def sum_kernel(z_ref, got_ref, keep_ref, send_ref):
+    total = got_ref[0].astype(f32)
+    for s in range(1, got_ref.shape[0]):
+        total = total + got_ref[s].astype(f32)
+    turned = total.T
+    first = z_ref[0] == 0
+    keep_ref[...] = jnp.where(first, turned[:BLOCK], turned[BLOCK:])
+    send_ref[...] = jnp.where(first, turned[BLOCK:], turned[:BLOCK])
 
 
 def value_kernel(z_ref, got_ref, own_ref, *refs):
@@ -174,16 +184,23 @@
             out_specs=pl.BlockSpec((ny, cols, nz * BLOCK), lambda k, p: ((p[0] + NX - k) % NX, 0, 0)),
             scratch_shapes=[pltpu.VMEM((cols, rows), bf16), pltpu.VMEM((cols, rows), bf16)],
         ),
-        out_shape=jax.ShapeDtypeStruct((nx * ny, cols, nz * BLOCK), bf16),
+        out_shape=pltpu.HBM((nx * ny, cols, nz * BLOCK), bf16),
         compiler_params=pltpu.CompilerParams(vmem_limit_bytes=VMEM_GRANT),
         name="grad_partial",
     )(xpos, own_in, got_in, dval, rew, near, lengths)
     g_xy = lax.all_to_all(send, ("x", "y"), 0, 0, tiled=True)
-    g_sum = jnp.sum(g_xy.astype(f32), axis=0).T.reshape(nz, BLOCK, cols)
-    g_z = lax.ppermute(jnp.where(zpart == 0, g_sum[1], g_sum[0]), "zh", SWAP_Z)
-    w_grad = (jnp.where(zpart == 0, g_sum[0], g_sum[1]) + g_z).astype(bf16)
-
     in_vmem = pl.BlockSpec(memory_space=pltpu.VMEM)
+    g_keep, g_send = pl.pallas_call(
+        sum_kernel,
+        in_specs=[pl.BlockSpec(memory_space=pltpu.SMEM), in_vmem],
+        out_specs=[in_vmem, in_vmem],
+        out_shape=[pltpu.VMEM((BLOCK, cols), f32), pltpu.VMEM((BLOCK, cols), f32)],
+        compiler_params=pltpu.CompilerParams(vmem_limit_bytes=VMEM_GRANT),
+        name="grad_sum",
+    )(zpos, on_chip(g_xy))
+    g_z = lax.ppermute(g_send, "zh", SWAP_Z)
+    w_grad = (g_keep + g_z).astype(bf16)
+
     v_other, v_own = pl.pallas_call(
         value_kernel,
         in_specs=[pl.BlockSpec(memory_space=pltpu.SMEM)] + [in_vmem] * (2 + 2 * nx),

time: 93.2 us -> 95 us (1.019)
  Pallas kernels: 6.67 us -> 9.15 us
  waiting for transfers between devices: 22.5 us -> 20.2 us
  starting transfers between devices: 58.7 us -> 60.5 us
    ppermute x1, waiting for transfers between devices: 7.58 us -> 5.16 us  [per_device(): g_z = lax.ppermute(g_send, 'zh', SWAP_Z)]
    ppermute x1, starting transfers between devices: 4.28 us -> 6.25 us  [per_device(): g_z = lax.ppermute(g_send, 'zh', SWAP_Z)]
    reduce_sum x1 -> x0, other arithmetic: 1.38 us -> none  [per_device(): g_sum = jnp.sum(g_xy.astype(f32), axis=0).T.reshape(nz, BLOCK, cols)]
    pallas_call x1, Pallas kernels: 0.84 us -> 2.01 us  [per_device(): pl.pallas_call(value_kernel, in_specs=[pl.BlockSpec(memory_space=pltpu.SM...]
    pallas_call x1, Pallas kernels: 2.9 us -> 4.02 us  [per_device(): pl.pallas_call(norm_kernel, grid=(rows // step,), in_specs=[pl.BlockSpec(...]
  transfers between devices with their start and end apart: 13 -> 13, of which waited for: 6 -> 6; matrix products, arithmetic and copies ran while one was open for 2% -> 2% of each run, Pallas kernels for 4% -> 5%
where the time goes in v6:
time: 95 us; the launch traced here: 94.3 us
  starting transfers between devices  60.5 us (64%)
  waiting for transfers between devices  20.2 us (21%)
  Pallas kernels  9.15 us (10%)
  local copies, waits for them, and re-layouts  2.23 us (2%)
  other arithmetic  1.39 us (1%)
    ppermute x1, starting transfers between devices, per_device(): w_far = lax.ppermute(w_y, 'zh', SWAP_Z)  10.5 us
    ppermute x3, starting transfers between devices, per_device(): own_w.append(lax.ppermute(w_y, 'x', X_SHIFTS[s]))  10.5 us
    all_to_all x1, starting transfers between devices, per_device(): g_xy = lax.all_to_all(send, ('x', 'y'), 0, 0, tiled=True)  9.61 us
    ppermute x3, starting transfers between devices, per_device(): far_w.append(lax.ppermute(w_far, 'x', X_SHIFTS[s]))  9.22 us
    all_to_all x1, starting transfers between devices, per_device(): lax.all_to_all(jnp.broadcast_to(w_value[None], (ny, BLOCK, cols)), 'y', 0...  7.1 us
    all_to_all x1, waiting for transfers between devices, per_device(): lax.all_to_all(jnp.broadcast_to(w_value[None], (ny, BLOCK, cols)), 'y', 0...  6.78 us
    ppermute x1, starting transfers between devices, per_device(): g_z = lax.ppermute(g_send, 'zh', SWAP_Z)  6.25 us
    ppermute x1, waiting for transfers between devices, per_device(): g_z = lax.ppermute(g_send, 'zh', SWAP_Z)  5.16 us
  transfers between devices with their start and end apart: 13, of which 6 were waited for; matrix products, arithmetic and copies ran while one was open for 2% of the time, Pallas kernels for 5%

profile of v6, /device:TPU:2, one launch (start us, length us, event | category | flops | bytes accessed | tf_op | source)
XLA Modules:
  0.0 94.3 jit_solution(4225437804623523299)
XLA Ops:
  0.6 0.0 copy-start.5
  0.6 3.5 %collective-permute-start = (bf16[4]{0:T(256)(128)(2,1)}, bf16[4]{0:T(256)(128)(2,1)S(1)}, u32[]{:S(2)}, u32[]{:S(2)}) collective-permute-start(bf16[4]{0:T(256)(128)(2,1)} %param.10), channel_id=1, source_target_pairs={{0,12},{12,0},{24,36},{36,24},{48,60},{60,48},{72,84},{84,72},{1,1... | collective-permute-start | bytes 32 | tf_op jit(solution)/shard_map/ppermute | solution.py:138
  4.1 2.1 %collective-permute-done = bf16[4]{0:T(256)(128)(2,1)S(1)} collective-permute-done((bf16[4]{0:T(256)(128)(2,1)}, bf16[4]{0:T(256)(128)(2,1)S(1)}, u32[]{:S(2)}, u32[]{:S(2)}) %collective-permute-start) | collective-permute-done | bytes 40 | tf_op jit(solution)/shard_map/ppermute | solution.py:138
  6.2 0.0 copy-start
  6.2 0.0 copy-start.3
  6.2 0.0 copy-start.4
  6.2 4.0 %norm_split.1 = (bf16[128,4096]{1,0:T(8,128)(2,1)S(1)}, bf16[128,4352]{1,0:T(8,128)(2,1)}) custom-call(s32[1]{0:T(128)} %bitcast.1.core_ref, s32[1]{0:T(128)} %bitcast.2.xpos_ref, bf16[128,8192]{1,0:T(8,128)(2,1)} %bitcast.17, f32[1,8192]{1,0:T(1,128)} %bitcast.19, bf16[128,128]{1,0:T(8,128)(2,1)} %bitcast.10, bf16[1,4]{1,0:T(2,128)(2,1)} %bitcast.13, ...), custom_call_target="tpu_custom_call" | custom-call | tf_op jit(solution)/shard_map/norm_split/pallas_call | solution.py:152
  10.3 1.9 %collective-permute-start.1 = (bf16[128,4352]{1,0:T(8,128)(2,1)}, bf16[128,4352]{1,0:T(8,128)(2,1)S(1)}, u32[]{:S(2)}, u32[]{:S(2)}) collective-permute-start(bf16[128,4352]{1,0:T(8,128)(2,1)} %get-tuple-element.8), channel_id=1, source_target_pairs={{0,6},{6,0},{1,7},{7,1},{2,8},{8,2},{3,9},{9,3},{4,10},{10,4},{5,1... | collective-permute-start | bytes 3342344 | tf_op jit(solution)/shard_map/ppermute | solution.py:169
  12.2 0.0 copy-done.5
  12.2 0.7 broadcast_in_dim.2
  12.9 7.1 %all-to-all-start = ((bf16[8,64,128]{2,1,0:T(8,128)(2,1)}), bf16[8,64,128]{2,1,0:T(8,128)(2,1)S(1)}, u32[]{:S(2)}, u32[]{:S(2)}) async-start(bf16[8,64,128]{2,1,0:T(8,128)(2,1)} %broadcast_in_dim.2), calls=%async_computation | async-start | bytes 262144 | tf_op jit(solution)/shard_map/all_to_all | solution.py:139
  20.0 0.0 collective-permute-done.1.got_ref
  20.0 0.0 copy-done
  20.0 0.0 copy-done.3
  20.0 0.0 copy-done.4
  20.0 2.9 %grad_partial.1 = bf16[32,128,128]{2,1,0:T(8,128)(2,1)} custom-call(s32[1]{0:T(128)} %bitcast.2.xpos_ref, bf16[128,4096]{1,0:T(8,128)(2,1)S(1)} %get-tuple-element.9.own_ref, bf16[128,4352]{1,0:T(8,128)(2,1)S(1)} %collective-permute-done.1.got_ref, bf16[128,128]{1,0:T(8,128)(2,1)S(1)} %bitcast.11, bf16[1,4]{1,0:T(2,128)(2,1)S(1)} %bitcast.14, ...), custom_call_target="tpu_custom_call" | custom-call | tf_op jit(solution)/shard_map/grad_partial/pallas_call | solution.py:171
  22.9 6.8 %all-to-all-done.refs_0_ = bf16[8,64,128]{2,1,0:T(8,128)(2,1)S(1)} async-done(((bf16[8,64,128]{2,1,0:T(8,128)(2,1)}), bf16[8,64,128]{2,1,0:T(8,128)(2,1)S(1)}, u32[]{:S(2)}, u32[]{:S(2)}) %all-to-all-start) | async-done | bytes 131104 | tf_op jit(solution)/shard_map/all_to_all | solution.py:139
  29.7 9.6 %all-to-all-start.1 = ((bf16[32,128,128]{2,1,0:T(8,128)(2,1)}), bf16[32,128,128]{2,1,0:T(8,128)(2,1)S(1)}, u32[]{:S(2)}, u32[]{:S(2)}) async-start(bf16[32,128,128]{2,1,0:T(8,128)(2,1)} %grad_partial.1), calls=%async_computation.1 | async-start | bytes 2097152 | tf_op jit(solution)/shard_map/all_to_all | solution.py:191
  39.3 10.5 %collective-permute-start.5 = (bf16[8,64,128]{2,1,0:T(8,128)(2,1)S(1)}, bf16[8,64,128]{2,1,0:T(8,128)(2,1)S(1)}, u32[]{:S(2)}, u32[]{:S(2)}) collective-permute-start(bf16[8,64,128]{2,1,0:T(8,128)(2,1)S(1)} %all-to-all-done.refs_0_), channel_id=1, source_target_pairs={{0,96},{96,0},{1,97},{97,1},{2,98},{98,2},{3,99},{99,3},{4,100},{1... | collective-permute-start | bytes 393224 | tf_op jit(solution)/shard_map/ppermute | solution.py:140
  49.8 3.4 %collective-permute-start.2 = (bf16[8,64,128]{2,1,0:T(8,128)(2,1)S(1)}, bf16[8,64,128]{2,1,0:T(8,128)(2,1)S(1)}, u32[]{:S(2)}, u32[]{:S(2)}) collective-permute-start(bf16[8,64,128]{2,1,0:T(8,128)(2,1)S(1)} %all-to-all-done.refs_0_), channel_id=1, source_target_pairs={{0,192},{192,384},{384,576},{576,0},{1,193},{193,385},{385,577},{5... | collective-permute-start | bytes 393224 | tf_op jit(solution)/shard_map/ppermute | solution.py:144
  53.2 2.7 %collective-permute-start.3 = (bf16[8,64,128]{2,1,0:T(8,128)(2,1)S(1)}, bf16[8,64,128]{2,1,0:T(8,128)(2,1)}, u32[]{:S(2)}, u32[]{:S(2)}) collective-permute-start(bf16[8,64,128]{2,1,0:T(8,128)(2,1)S(1)} %all-to-all-done.refs_0_), channel_id=1, source_target_pairs={{0,384},{192,576},{384,0},{576,192},{1,385},{193,577},{385,1},{577... | collective-permute-start | bytes 393224 | tf_op jit(solution)/shard_map/ppermute | solution.py:144
  56.0 4.3 %collective-permute-start.4 = (bf16[8,64,128]{2,1,0:T(8,128)(2,1)S(1)}, bf16[8,64,128]{2,1,0:T(8,128)(2,1)}, u32[]{:S(2)}, u32[]{:S(2)}) collective-permute-start(bf16[8,64,128]{2,1,0:T(8,128)(2,1)S(1)} %all-to-all-done.refs_0_), channel_id=1, source_target_pairs={{0,576},{192,0},{384,192},{576,384},{1,577},{193,1},{385,193},{577... | collective-permute-start | bytes 393224 | tf_op jit(solution)/shard_map/ppermute | solution.py:144
  60.3 0.0 collective-permute-done.5.refs_4_
  60.3 1.9 %collective-permute-start.6 = (bf16[8,64,128]{2,1,0:T(8,128)(2,1)S(1)}, bf16[8,64,128]{2,1,0:T(8,128)(2,1)}, u32[]{:S(2)}, u32[]{:S(2)}) collective-permute-start(bf16[8,64,128]{2,1,0:T(8,128)(2,1)S(1)} %collective-permute-done.5.refs_4_), channel_id=1, source_target_pairs={{0,192},{192,384},{384,576},{576,0},{1,193},{193,385},{385,577},{5... | collective-permute-start | bytes 393224 | tf_op jit(solution)/shard_map/ppermute | solution.py:145
  62.3 5.4 %collective-permute-start.7 = (bf16[8,64,128]{2,1,0:T(8,128)(2,1)S(1)}, bf16[8,64,128]{2,1,0:T(8,128)(2,1)}, u32[]{:S(2)}, u32[]{:S(2)}) collective-permute-start(bf16[8,64,128]{2,1,0:T(8,128)(2,1)S(1)} %collective-permute-done.5.refs_4_), channel_id=1, source_target_pairs={{0,384},{192,576},{384,0},{576,192},{1,385},{193,577},{385,1},{577... | collective-permute-start | bytes 393224 | tf_op jit(solution)/shard_map/ppermute | solution.py:145
  67.7 0.0 collective-permute-done.2.refs_1_
  67.7 0.0 copy-start.1
  67.7 0.6 copy-done.1
  68.3 1.9 %collective-permute-start.8 = (bf16[8,64,128]{2,1,0:T(8,128)(2,1)S(1)}, bf16[8,64,128]{2,1,0:T(8,128)(2,1)}, u32[]{:S(2)}, u32[]{:S(2)}) collective-permute-start(bf16[8,64,128]{2,1,0:T(8,128)(2,1)S(1)} %collective-permute-done.5.refs_4_), channel_id=1, source_target_pairs={{0,576},{192,0},{384,192},{576,384},{1,577},{193,1},{385,193},{577... | collective-permute-start | bytes 393224 | tf_op jit(solution)/shard_map/ppermute | solution.py:145
  70.3 0.0 collective-permute-done.3.refs_2_
  70.3 0.0 collective-permute-done.4.refs_3_
  70.3 0.0 collective-permute-done.6.refs_5_
  70.3 1.5 %collective-permute-done.7.refs_6_ = bf16[8,64,128]{2,1,0:T(8,128)(2,1)} collective-permute-done((bf16[8,64,128]{2,1,0:T(8,128)(2,1)S(1)}, bf16[8,64,128]{2,1,0:T(8,128)(2,1)}, u32[]{:S(2)}, u32[]{:S(2)}) %collective-permute-start.7) | collective-permute-done | bytes 131104 | tf_op jit(solution)/shard_map/ppermute | solution.py:145
  71.8 3.5 %collective-permute-done.8.refs_7_ = bf16[8,64,128]{2,1,0:T(8,128)(2,1)} collective-permute-done((bf16[8,64,128]{2,1,0:T(8,128)(2,1)S(1)}, bf16[8,64,128]{2,1,0:T(8,128)(2,1)}, u32[]{:S(2)}, u32[]{:S(2)}) %collective-permute-start.8) | collective-permute-done | bytes 131104 | tf_op jit(solution)/shard_map/ppermute | solution.py:145
  75.3 0.0 copy-start.2
  75.3 0.9 copy-done.2
  76.2 2.0 %value_parts.1 = (f32[128,128]{1,0:T(8,128)S(1)}, f32[128,128]{1,0:T(8,128)S(1)}) custom-call(s32[1]{0:T(128)} %bitcast.z_ref, bf16[128,4352]{1,0:T(8,128)(2,1)S(1)} %collective-permute-done.1.got_ref, bf16[128,4096]{1,0:T(8,128)(2,1)S(1)} %get-tuple-element.9.own_ref, bf16[8,64,128]{2,1,0:T(8,128)(2,1)S(1)} %all-to-all-done.refs_0_, ...), custom_call_target="tpu_custom_call" | custom-call | tf_op jit(solution)/shard_map/value_parts/pallas_call | solution.py:204
  78.2 1.9 %collective-permute-start.9 = (f32[128,128]{1,0:T(8,128)S(1)}, f32[128,128]{1,0:T(8,128)S(1)}, u32[]{:S(2)}, u32[]{:S(2)}) collective-permute-start(f32[128,128]{1,0:T(8,128)S(1)} %get-tuple-element.11), channel_id=1, source_target_pairs={{0,6},{6,0},{1,7},{7,1},{2,8},{8,2},{3,9},{9,3},{4,10},{10,4},{5,1... | collective-permute-start | bytes 196616 | tf_op jit(solution)/shard_map/ppermute | solution.py:213
  80.1 0.1 fusion
  80.2 1.1 %collective-permute-done.9 = f32[128,128]{1,0:T(8,128)S(1)} collective-permute-done((f32[128,128]{1,0:T(8,128)S(1)}, f32[128,128]{1,0:T(8,128)S(1)}, u32[]{:S(2)}, u32[]{:S(2)}) %collective-permute-start.9) | collective-permute-done | bytes 65568 | tf_op jit(solution)/shard_map/ppermute | solution.py:213
  81.4 0.0 all-to-all-done.1.got_ref
  81.4 0.2 grad_sum.1
  81.6 6.3 %collective-permute-start.10 = (f32[64,128]{1,0:T(8,128)S(1)}, f32[64,128]{1,0:T(8,128)S(1)}, u32[]{:S(2)}, u32[]{:S(2)}) collective-permute-start(f32[64,128]{1,0:T(8,128)S(1)} %get-tuple-element.13), channel_id=1, source_target_pairs={{0,96},{96,0},{1,97},{97,1},{2,98},{98,2},{3,99},{99,3},{4,100},{1... | collective-permute-start | bytes 98312 | tf_op jit(solution)/shard_map/ppermute | solution.py:201
  87.9 0.7 multiply_convert_fusion
  88.6 5.2 %collective-permute-done.10 = f32[64,128]{1,0:T(8,128)S(1)} collective-permute-done((f32[64,128]{1,0:T(8,128)S(1)}, f32[64,128]{1,0:T(8,128)S(1)}, u32[]{:S(2)}, u32[]{:S(2)}) %collective-permute-start.10) | collective-permute-done | bytes 32800 | tf_op jit(solution)/shard_map/ppermute | solution.py:201
  93.7 0.6 add_convert_fusion
  (1 shorter events, 0.0 us)
Async XLA Ops:
  0.6 11.5 %copy-start.5 = (bf16[64,128]{1,0:T(8,128)(2,1)S(1)}, bf16[64,128]{1,0:T(8,128)(2,1)}, u32[]{:S(2)}) copy-start(bf16[64,128]{1,0:T(8,128)(2,1)} %param.8) | copy-start | bytes 49156
  0.6 5.6 %collective-permute-start = (bf16[4]{0:T(256)(128)(2,1)}, bf16[4]{0:T(256)(128)(2,1)S(1)}, u32[]{:S(2)}, u32[]{:S(2)}) collective-permute-start(bf16[4]{0:T(256)(128)(2,1)} %param.10), channel_id=1, source_target_pairs={{0,12},{12,0},{24,36},{36,24},{48,60},{60,48},{72,84},{84,72},{1,1... | collective-permute-start | bytes 32 | tf_op jit(solution)/shard_map/ppermute | solution.py:138
  6.2 13.7 %copy-start = (bf16[4,32,128]{2,1,0:T(8,128)(2,1)S(1)}, bf16[4,32,128]{2,1,0:T(8,128)(2,1)}, u32[]{:S(2)}) copy-start(bf16[4,32,128]{2,1,0:T(8,128)(2,1)} %param.9) | copy-start | bytes 98308
  6.2 13.7 %copy-start.3 = (s32[1,4]{1,0:T(1,128)S(1)}, s32[1,4]{1,0:T(1,128)}, u32[]{:S(2)}) copy-start(s32[1,4]{1,0:T(1,128)} %len_ref.3) | copy-start | bytes 52
  6.2 13.7 %copy-start.4 = (bf16[4]{0:T(256)(128)(2,1)S(1)}, bf16[4]{0:T(256)(128)(2,1)}, u32[]{:S(2)}) copy-start(bf16[4]{0:T(256)(128)(2,1)} %param.10) | copy-start | bytes 28
  10.3 9.7 %collective-permute-start.1 = (bf16[128,4352]{1,0:T(8,128)(2,1)}, bf16[128,4352]{1,0:T(8,128)(2,1)S(1)}, u32[]{:S(2)}, u32[]{:S(2)}) collective-permute-start(bf16[128,4352]{1,0:T(8,128)(2,1)} %get-tuple-element.8), channel_id=1, source_target_pairs={{0,6},{6,0},{1,7},{7,1},{2,8},{8,2},{3,9},{9,3},{4,10},{10,4},{5,1... | collective-permute-start | bytes 3342344 | tf_op jit(solution)/shard_map/ppermute | solution.py:169
  12.9 16.8 %all-to-all-start = ((bf16[8,64,128]{2,1,0:T(8,128)(2,1)}), bf16[8,64,128]{2,1,0:T(8,128)(2,1)S(1)}, u32[]{:S(2)}, u32[]{:S(2)}) async-start(bf16[8,64,128]{2,1,0:T(8,128)(2,1)} %broadcast_in_dim.2), calls=%async_computation | async-start | bytes 262144 | tf_op jit(solution)/shard_map/all_to_all | solution.py:139
  29.7 51.7 %all-to-all-start.1 = ((bf16[32,128,128]{2,1,0:T(8,128)(2,1)}), bf16[32,128,128]{2,1,0:T(8,128)(2,1)S(1)}, u32[]{:S(2)}, u32[]{:S(2)}) async-start(bf16[32,128,128]{2,1,0:T(8,128)(2,1)} %grad_partial.1), calls=%async_computation.1 | async-start | bytes 2097152 | tf_op jit(solution)/shard_map/all_to_all | solution.py:191
  39.3 21.0 %collective-permute-start.5 = (bf16[8,64,128]{2,1,0:T(8,128)(2,1)S(1)}, bf16[8,64,128]{2,1,0:T(8,128)(2,1)S(1)}, u32[]{:S(2)}, u32[]{:S(2)}) collective-permute-start(bf16[8,64,128]{2,1,0:T(8,128)(2,1)S(1)} %all-to-all-done.refs_0_), channel_id=1, source_target_pairs={{0,96},{96,0},{1,97},{97,1},{2,98},{98,2},{3,99},{99,3},{4,100},{1... | collective-permute-start | bytes 393224 | tf_op jit(solution)/shard_map/ppermute | solution.py:140
  49.8 17.8 %collective-permute-start.2 = (bf16[8,64,128]{2,1,0:T(8,128)(2,1)S(1)}, bf16[8,64,128]{2,1,0:T(8,128)(2,1)S(1)}, u32[]{:S(2)}, u32[]{:S(2)}) collective-permute-start(bf16[8,64,128]{2,1,0:T(8,128)(2,1)S(1)} %all-to-all-done.refs_0_), channel_id=1, source_target_pairs={{0,192},{192,384},{384,576},{576,0},{1,193},{193,385},{385,577},{5... | collective-permute-start | bytes 393224 | tf_op jit(solution)/shard_map/ppermute | solution.py:144
  53.2 17.0 %collective-permute-start.3 = (bf16[8,64,128]{2,1,0:T(8,128)(2,1)S(1)}, bf16[8,64,128]{2,1,0:T(8,128)(2,1)}, u32[]{:S(2)}, u32[]{:S(2)}) collective-permute-start(bf16[8,64,128]{2,1,0:T(8,128)(2,1)S(1)} %all-to-all-done.refs_0_), channel_id=1, source_target_pairs={{0,384},{192,576},{384,0},{576,192},{1,385},{193,577},{385,1},{577... | collective-permute-start | bytes 393224 | tf_op jit(solution)/shard_map/ppermute | solution.py:144
  56.0 14.3 %collective-permute-start.4 = (bf16[8,64,128]{2,1,0:T(8,128)(2,1)S(1)}, bf16[8,64,128]{2,1,0:T(8,128)(2,1)}, u32[]{:S(2)}, u32[]{:S(2)}) collective-permute-start(bf16[8,64,128]{2,1,0:T(8,128)(2,1)S(1)} %all-to-all-done.refs_0_), channel_id=1, source_target_pairs={{0,576},{192,0},{384,192},{576,384},{1,577},{193,1},{385,193},{577... | collective-permute-start | bytes 393224 | tf_op jit(solution)/shard_map/ppermute | solution.py:144
  60.3 9.9 %collective-permute-start.6 = (bf16[8,64,128]{2,1,0:T(8,128)(2,1)S(1)}, bf16[8,64,128]{2,1,0:T(8,128)(2,1)}, u32[]{:S(2)}, u32[]{:S(2)}) collective-permute-start(bf16[8,64,128]{2,1,0:T(8,128)(2,1)S(1)} %collective-permute-done.5.refs_4_), channel_id=1, source_target_pairs={{0,192},{192,384},{384,576},{576,0},{1,193},{193,385},{385,577},{5... | collective-permute-start | bytes 393224 | tf_op jit(solution)/shard_map/ppermute | solution.py:145
  62.3 9.5 %collective-permute-start.7 = (bf16[8,64,128]{2,1,0:T(8,128)(2,1)S(1)}, bf16[8,64,128]{2,1,0:T(8,128)(2,1)}, u32[]{:S(2)}, u32[]{:S(2)}) collective-permute-start(bf16[8,64,128]{2,1,0:T(8,128)(2,1)S(1)} %collective-permute-done.5.refs_4_), channel_id=1, source_target_pairs={{0,384},{192,576},{384,0},{576,192},{1,385},{193,577},{385,1},{577... | collective-permute-start | bytes 393224 | tf_op jit(solution)/shard_map/ppermute | solution.py:145
  67.7 0.7 copy-start.1
  68.3 7.0 %collective-permute-start.8 = (bf16[8,64,128]{2,1,0:T(8,128)(2,1)S(1)}, bf16[8,64,128]{2,1,0:T(8,128)(2,1)}, u32[]{:S(2)}, u32[]{:S(2)}) collective-permute-start(bf16[8,64,128]{2,1,0:T(8,128)(2,1)S(1)} %collective-permute-done.5.refs_4_), channel_id=1, source_target_pairs={{0,576},{192,0},{384,192},{576,384},{1,577},{193,1},{385,193},{577... | collective-permute-start | bytes 393224 | tf_op jit(solution)/shard_map/ppermute | solution.py:145
  75.3 0.9 copy-start.2
  78.2 3.1 %collective-permute-start.9 = (f32[128,128]{1,0:T(8,128)S(1)}, f32[128,128]{1,0:T(8,128)S(1)}, u32[]{:S(2)}, u32[]{:S(2)}) collective-permute-start(f32[128,128]{1,0:T(8,128)S(1)} %get-tuple-element.11), channel_id=1, source_target_pairs={{0,6},{6,0},{1,7},{7,1},{2,8},{8,2},{3,9},{9,3},{4,10},{10,4},{5,1... | collective-permute-start | bytes 196616 | tf_op jit(solution)/shard_map/ppermute | solution.py:213
  81.6 12.1 %collective-permute-start.10 = (f32[64,128]{1,0:T(8,128)S(1)}, f32[64,128]{1,0:T(8,128)S(1)}, u32[]{:S(2)}, u32[]{:S(2)}) collective-permute-start(f32[64,128]{1,0:T(8,128)S(1)} %get-tuple-element.13), channel_id=1, source_target_pairs={{0,96},{96,0},{1,97},{97,1},{2,98},{98,2},{3,99},{99,3},{4,100},{1... | collective-permute-start | bytes 98312 | tf_op jit(solution)/shard_map/ppermute | solution.py:201
